TPU v7x, 32 devices: a whole 2x2x4 slice. The times are simulated.
32 devices in a mesh: shard: 8 (over z, x), seq: 4 (over y, core).
Axes of the slice: x: 2, y: 2, z: 4, core: 2. Of those that a mesh axis runs over, the one named last changes fastest.
Arguments:
- tokens: bfloat16 [8, 8, 512, 768], P(None, 'shard', 'seq'), may hold values from -6 to 6
- lengths: int32 [8], replicated, may hold values from 512 to 4096, as said below
- deal_order: int32 [8], replicated, may hold values from 0 to 7, as said below
- w_query: bfloat16 [768, 768], P('shard'), may hold values from -0.3125 to 0.3125
- w_key: bfloat16 [768, 768], P('shard'), may hold values from -0.3125 to 0.3125
- w_value: bfloat16 [768, 768], P('shard'), may hold values from -0.21875 to 0.21875
- w_output: bfloat16 [768, 768], P('shard'), may hold values from -0.625 to 0.625
- b_query: bfloat16 [768], P('shard'), may hold values from -4 to 4
- b_value: bfloat16 [768], P('shard'), may hold values from -4 to 4
- b_output: bfloat16 [768], P('shard'), may hold values from -4 to 4
- ln1_gain: bfloat16 [768], P('shard'), may hold values from 0.5 to 1.5
- ln1_shift: bfloat16 [768], P('shard'), may hold values from -4 to 4
- w_inner: bfloat16 [768, 3072], P('shard'), may hold values from -0.21875 to 0.21875
- b_inner: bfloat16 [3072], P('shard'), may hold values from -4 to 4
- w_outer: bfloat16 [3072, 768], P('shard'), may hold values from -0.15625 to 0.15625
- b_outer: bfloat16 [768], P('shard'), may hold values from -4 to 4
- ln2_gain: bfloat16 [768], P('shard'), may hold values from 0.5 to 1.5
- ln2_shift: bfloat16 [768], P('shard'), may hold values from -4 to 4
- cotangent: bfloat16 [8, 8, 512, 768], P('shard', None, 'seq'), may hold values from -6 to 6
Outputs:
- activations: bfloat16 [8, 8, 512, 768], P('shard', None, 'seq')
- d_tokens: bfloat16 [8, 8, 512, 768], P(None, 'shard', 'seq')
- d_w_query: float32 [768, 768], P('shard')
- d_w_key: float32 [768, 768], P('shard')
- d_w_value: float32 [768, 768], P('shard')
- d_w_output: float32 [768, 768], P('shard')
- d_b_query: float32 [768], P('shard')
- d_b_value: float32 [768], P('shard')
- d_b_output: float32 [768], P('shard')
- d_ln1_gain: float32 [768], P('shard')
- d_ln1_shift: float32 [768], P('shard')
- d_w_inner: float32 [768, 3072], P('shard')
- d_b_inner: float32 [3072], P('shard')
- d_w_outer: float32 [3072, 768], P('shard')
- d_b_outer: float32 [768], P('shard')
- d_ln2_gain: float32 [768], P('shard')
- d_ln2_shift: float32 [768], P('shard')
Inputs may be any that keep to these rules, and one draw needn't show every extreme that they name: Sequence q has lengths[q] real tokens, the rest of its 4096 slots are padding; some sequence has exactly 4096. `deal_order`: each number 0 to 7 once.
All inputs are finite; a program needn't handle non-finite values.
Results may differ from a plain program's by a relative error of at most 0.018.
Values may be sent and summed in bfloat16 or wider, within the bound.
No kernel may reach another device: no remote copies, remote signals or barrier semaphores. Data moves between devices by JAX's collectives and lax.ppermute only.
A program may use at most 256 MiB of HBM per device.

v0:
```python
import math

import jax
import jax.numpy as jnp
from jax import lax
from jax.sharding import PartitionSpec as P

HEADS = 12
HD = 64


far_below = -1000000000.0


def shortened(array):
    return jax.tree.map(lambda a: a.astype(jnp.bfloat16) if a.dtype == jnp.float32 else a, array)


def layer_norm(residual, ln_gain, ln_shift):
    centred = residual - jnp.mean(residual, axis=-1, keepdims=True)
    variance = jnp.mean(centred * centred, axis=-1, keepdims=True)
    return centred * lax.rsqrt(variance + 1e-12) * ln_gain + ln_shift


def gelu_exact(inner_pre):
    return jax.nn.gelu(inner_pre, approximate=False)


def dense_dot(left_side, right_side):
    return jnp.dot(left_side, right_side, preferred_element_type=jnp.float32)


def masked_scores(q_block, key_rows, counted, score_scale):
    scores = (
        jnp.einsum("qhd,khd->hqk", q_block, key_rows, preferred_element_type=jnp.float32)
        * score_scale
    )
    return jnp.where(counted[None, None, :], scores, far_below)


def attend_forward(packed):
    query_rows, key_rows, value_rows, counted = packed
    slot_len, local_heads, head_dim = query_rows.shape
    block_rows = min(512, slot_len)
    score_scale = 1.0 / math.sqrt(head_dim)
    q_blocks = query_rows.reshape(slot_len // block_rows, block_rows, local_heads, head_dim)

    def one_block(q_block):
        scores = masked_scores(q_block, key_rows, counted, score_scale)
        top_score = jnp.max(scores, axis=-1, keepdims=True)
        raised = jnp.exp(scores - top_score)
        row_total = jnp.sum(raised, axis=-1, keepdims=True)
        soft_probs = (raised / row_total).astype(jnp.bfloat16)
        mixed_block = jnp.einsum(
            "hqk,khd->qhd", soft_probs, value_rows, preferred_element_type=jnp.float32
        )
        return (mixed_block.astype(jnp.bfloat16), (top_score + jnp.log(row_total))[..., 0])

    mixed_blocks, log_total = lax.map(one_block, q_blocks)
    return (mixed_blocks.reshape(slot_len, local_heads, head_dim), log_total)


def attend_backward(packed):
    query_rows, key_rows, value_rows, counted, log_total, d_mixed = packed
    slot_len, local_heads, head_dim = query_rows.shape
    block_rows = min(512, slot_len)
    block_count = slot_len // block_rows
    score_scale = 1.0 / math.sqrt(head_dim)
    q_blocks = query_rows.reshape(block_count, block_rows, local_heads, head_dim)
    g_blocks = d_mixed.reshape(block_count, block_rows, local_heads, head_dim)

    def one_block(running, block_in):
        d_keys, d_values = running
        q_block, g_block, lse_block = block_in
        scores = masked_scores(q_block, key_rows, counted, score_scale)
        soft_probs = jnp.exp(scores - lse_block[..., None])
        d_values = d_values + jnp.einsum(
            "hqk,qhd->khd",
            soft_probs.astype(jnp.bfloat16),
            g_block,
            preferred_element_type=jnp.float32,
        )
        d_probs = jnp.einsum(
            "qhd,khd->hqk", g_block, value_rows, preferred_element_type=jnp.float32
        )
        row_sum = jnp.sum(soft_probs * d_probs, axis=-1, keepdims=True)
        d_scores = (soft_probs * (d_probs - row_sum)).astype(jnp.bfloat16)
        d_query = (
            jnp.einsum("hqk,khd->qhd", d_scores, key_rows, preferred_element_type=jnp.float32)
            * score_scale
        )
        d_keys = (
            d_keys
            + jnp.einsum("hqk,qhd->khd", d_scores, q_block, preferred_element_type=jnp.float32)
            * score_scale
        )
        return ((d_keys, d_values), d_query.astype(jnp.bfloat16))

    empty_grad = jnp.zeros((slot_len, local_heads, head_dim), jnp.float32)
    (d_keys, d_values), d_query = lax.scan(
        one_block, (empty_grad, empty_grad), (q_blocks, g_blocks, log_total)
    )
    return (
        d_query.reshape(slot_len, local_heads, head_dim),
        d_keys.astype(jnp.bfloat16),
        d_values.astype(jnp.bfloat16),
    )


def body(
    tokens,
    lengths,
    deal_order,
    w_query,
    w_key,
    w_value,
    w_output,
    b_query,
    b_value,
    b_output,
    ln1_gain,
    ln1_shift,
    w_inner,
    b_inner,
    w_outer,
    b_outer,
    ln2_gain,
    ln2_shift,
    cotangent,
):
    shards = lax.axis_size("shard")
    splits = lax.axis_size("seq")
    devices = shards * splits
    seq_count = tokens.shape[0]
    stretch_len = tokens.shape[2]
    model_width = tokens.shape[3]
    group_seqs = seq_count // shards
    slot_len = shards * splits * stretch_len
    local_width = model_width // splits
    local_heads = HEADS // splits
    params = (
        w_query,
        w_key,
        w_value,
        w_output,
        b_query,
        b_value,
        b_output,
        ln1_gain,
        ln1_shift,
        w_inner,
        b_inner,
        w_outer,
        b_outer,
        ln2_gain,
        ln2_shift,
    )
    gathered = (
        lax.all_gather(params[0], "shard", axis=0, tiled=True),
        lax.all_gather(params[1], "shard", axis=0, tiled=True),
        lax.all_gather(params[2], "shard", axis=0, tiled=True),
        lax.all_gather(params[3], "shard", axis=0, tiled=True),
        lax.all_gather(params[4], "shard", axis=0, tiled=True),
        lax.all_gather(params[5], "shard", axis=0, tiled=True),
        lax.all_gather(params[6], "shard", axis=0, tiled=True),
        lax.all_gather(params[7], "shard", axis=0, tiled=True),
        lax.all_gather(params[8], "shard", axis=0, tiled=True),
        lax.all_gather(params[9], "shard", axis=0, tiled=True),
        lax.all_gather(params[10], "shard", axis=0, tiled=True),
        lax.all_gather(params[11], "shard", axis=0, tiled=True),
        lax.all_gather(params[12], "shard", axis=0, tiled=True),
        lax.all_gather(params[13], "shard", axis=0, tiled=True),
        lax.all_gather(params[14], "shard", axis=0, tiled=True),
    )
    (
        query_weight,
        key_weight,
        value_weight,
        output_weight,
        query_bias,
        value_bias,
        output_bias,
        norm1_gain,
        norm1_shift,
        inner_weight,
        inner_bias,
        outer_weight,
        outer_bias,
        norm2_gain,
        norm2_shift,
    ) = gathered
    ordered = jnp.take(tokens, deal_order, axis=0)
    dealt_blocks = lax.all_to_all(ordered, "shard", split_axis=0, concat_axis=1, tiled=True)
    token_rows = dealt_blocks.reshape(-1, model_width)
    owned_slots = lax.dynamic_slice_in_dim(
        deal_order, lax.axis_index("shard") * group_seqs, group_seqs
    )
    matches = owned_slots[:, None] == jnp.arange(seq_count, dtype=jnp.int32)[None, :]
    slot_lengths = jnp.sum(jnp.where(matches, lengths[None, :], 0), axis=1)
    counted = jnp.arange(slot_len, dtype=jnp.int32)[None, :] < slot_lengths[:, None]

    def to_heads(source):
        return source.reshape(group_seqs, shards, stretch_len, splits, local_width)

    def to_tokens(source):
        return source.reshape(group_seqs, shards, splits * stretch_len, 1, local_width)

    def as_slots(source):
        return source.reshape(group_seqs, slot_len, local_heads, HD)

    query_rows = (dense_dot(token_rows, query_weight) + query_bias).astype(jnp.bfloat16)
    key_rows = dense_dot(token_rows, key_weight).astype(jnp.bfloat16)
    value_rows = (dense_dot(token_rows, value_weight) + value_bias).astype(jnp.bfloat16)
    heads_q, heads_k, heads_v = (
        lax.all_to_all(to_heads(query_rows), "seq", split_axis=3, concat_axis=2, tiled=True),
        lax.all_to_all(to_heads(key_rows), "seq", split_axis=3, concat_axis=2, tiled=True),
        lax.all_to_all(to_heads(value_rows), "seq", split_axis=3, concat_axis=2, tiled=True),
    )
    heads_q = as_slots(heads_q)
    heads_k = as_slots(heads_k)
    heads_v = as_slots(heads_v)
    mixed_heads, log_total = lax.map(attend_forward, (heads_q, heads_k, heads_v, counted))
    mixed_back = lax.all_to_all(
        to_tokens(mixed_heads), "seq", split_axis=2, concat_axis=3, tiled=True
    )
    mixed_rows = mixed_back.reshape(-1, model_width)
    branch = dense_dot(mixed_rows, output_weight) + output_bias
    resid_one = token_rows.astype(jnp.float32) + branch
    normed, norm1_pull = jax.vjp(
        layer_norm, resid_one, norm1_gain.astype(jnp.float32), norm1_shift.astype(jnp.float32)
    )
    normed_low = normed.astype(jnp.bfloat16)
    inner_pre = dense_dot(normed_low, inner_weight) + inner_bias
    active, gelu_pull = jax.vjp(gelu_exact, inner_pre)
    active_low = active.astype(jnp.bfloat16)
    outer_out = dense_dot(active_low, outer_weight) + outer_bias
    final_rows, norm2_pull = jax.vjp(
        layer_norm,
        normed + outer_out,
        norm2_gain.astype(jnp.float32),
        norm2_shift.astype(jnp.float32),
    )
    activations = final_rows.astype(jnp.bfloat16).reshape(
        group_seqs, shards, stretch_len, model_width
    )
    back_weights = (
        lax.all_gather(params[0], "shard", axis=0, tiled=True),
        lax.all_gather(params[1], "shard", axis=0, tiled=True),
        lax.all_gather(params[2], "shard", axis=0, tiled=True),
        lax.all_gather(params[3], "shard", axis=0, tiled=True),
        lax.all_gather(params[4], "shard", axis=0, tiled=True),
        lax.all_gather(params[5], "shard", axis=0, tiled=True),
        lax.all_gather(params[6], "shard", axis=0, tiled=True),
        lax.all_gather(params[7], "shard", axis=0, tiled=True),
        lax.all_gather(params[8], "shard", axis=0, tiled=True),
        lax.all_gather(params[9], "shard", axis=0, tiled=True),
        lax.all_gather(params[10], "shard", axis=0, tiled=True),
        lax.all_gather(params[11], "shard", axis=0, tiled=True),
        lax.all_gather(params[12], "shard", axis=0, tiled=True),
        lax.all_gather(params[13], "shard", axis=0, tiled=True),
        lax.all_gather(params[14], "shard", axis=0, tiled=True),
    )
    scale_all = 1.0 / devices
    d_resid_two, d_norm2_gain, d_norm2_shift = norm2_pull(
        cotangent.reshape(-1, model_width).astype(jnp.float32)
    )
    d_outer = d_resid_two.astype(jnp.bfloat16)
    grad_w_outer = jnp.einsum("tf,td->fd", active_low, d_outer, preferred_element_type=jnp.float32)
    grad_b_outer = jnp.sum(d_outer.astype(jnp.float32), axis=0)
    d_active = jnp.einsum(
        "td,fd->tf", d_outer, back_weights[11], preferred_element_type=jnp.float32
    )
    (d_inner,) = gelu_pull(d_active)
    d_inner_low = d_inner.astype(jnp.bfloat16)
    grad_w_inner = jnp.einsum(
        "td,tf->df", normed_low, d_inner_low, preferred_element_type=jnp.float32
    )
    grad_b_inner = jnp.sum(d_inner_low.astype(jnp.float32), axis=0)
    d_normed = (
        jnp.einsum("tf,df->td", d_inner_low, back_weights[9], preferred_element_type=jnp.float32)
        + d_resid_two
    )
    d_resid_one, d_norm1_gain, d_norm1_shift = norm1_pull(d_normed)
    d_branch = d_resid_one.astype(jnp.bfloat16)
    grad_w_output = jnp.einsum(
        "te,td->ed", mixed_rows, d_branch, preferred_element_type=jnp.float32
    )
    grad_b_output = jnp.sum(d_branch.astype(jnp.float32), axis=0)
    d_mixed = jnp.einsum(
        "td,ed->te", d_branch, back_weights[3], preferred_element_type=jnp.float32
    ).astype(jnp.bfloat16)
    d_heads = as_slots(
        lax.all_to_all(to_heads(d_mixed), "seq", split_axis=3, concat_axis=2, tiled=True)
    )
    d_query, d_key, d_value = lax.map(
        attend_backward, (heads_q, heads_k, heads_v, counted, log_total, d_heads)
    )
    back_q, back_k, back_v = (
        lax.all_to_all(to_tokens(d_query), "seq", split_axis=2, concat_axis=3, tiled=True),
        lax.all_to_all(to_tokens(d_key), "seq", split_axis=2, concat_axis=3, tiled=True),
        lax.all_to_all(to_tokens(d_value), "seq", split_axis=2, concat_axis=3, tiled=True),
    )
    dq_rows = back_q.reshape(-1, model_width)
    dk_rows = back_k.reshape(-1, model_width)
    dv_rows = back_v.reshape(-1, model_width)
    grad_w_query = jnp.einsum("te,td->ed", token_rows, dq_rows, preferred_element_type=jnp.float32)
    grad_w_key = jnp.einsum("te,td->ed", token_rows, dk_rows, preferred_element_type=jnp.float32)
    grad_w_value = jnp.einsum("te,td->ed", token_rows, dv_rows, preferred_element_type=jnp.float32)
    grad_b_query = jnp.sum(dq_rows.astype(jnp.float32), axis=0)
    grad_b_value = jnp.sum(dv_rows.astype(jnp.float32), axis=0)
    d_rows = (
        d_resid_one
        + jnp.einsum("td,ed->te", dq_rows, back_weights[0], preferred_element_type=jnp.float32)
        + jnp.einsum("td,ed->te", dk_rows, back_weights[1], preferred_element_type=jnp.float32)
        + jnp.einsum("td,ed->te", dv_rows, back_weights[2], preferred_element_type=jnp.float32)
    )
    d_dealt = d_rows.astype(jnp.bfloat16).reshape(group_seqs, shards, stretch_len, model_width)
    returned = lax.all_to_all(d_dealt, "shard", split_axis=1, concat_axis=0, tiled=True)
    d_tokens = jnp.zeros_like(returned).at[deal_order].set(returned)
    all_terms = tuple(
        (
            partial_grad * scale_all
            for partial_grad in (
                grad_w_query,
                grad_w_key,
                grad_w_value,
                grad_w_output,
                grad_b_query,
                grad_b_value,
                grad_b_output,
                d_norm1_gain,
                d_norm1_shift,
                grad_w_inner,
                grad_b_inner,
                grad_w_outer,
                grad_b_outer,
                d_norm2_gain,
                d_norm2_shift,
            )
        )
    )
    all_part = lax.psum_scatter(all_terms, "shard", scatter_dimension=0, tiled=True)
    summed = tuple(
        jax.tree.map(lambda part: part.astype(jnp.float32), lax.psum(shortened(all_part), "seq"))
    )
    return (activations, d_tokens) + summed


def solution(mesh):
    return jax.shard_map(
        body,
        mesh=mesh,
        in_specs=(
            P(None, "shard", "seq", None),
            P(),
            P(),
            P("shard", None),
            P("shard", None),
            P("shard", None),
            P("shard", None),
            P("shard"),
            P("shard"),
            P("shard"),
            P("shard"),
            P("shard"),
            P("shard", None),
            P("shard"),
            P("shard", None),
            P("shard"),
            P("shard"),
            P("shard"),
            P("shard", None, "seq", None),
        ),
        out_specs=(
            P("shard", None, "seq", None),
            P(None, "shard", "seq", None),
            P("shard", None),
            P("shard", None),
            P("shard", None),
            P("shard", None),
            P("shard"),
            P("shard"),
            P("shard"),
            P("shard"),
            P("shard"),
            P("shard", None),
            P("shard"),
            P("shard", None),
            P("shard"),
            P("shard"),
            P("shard"),
        ),
        check_vma=False,
    )
```

profile of v0, /device:TPU:0, one launch (start us, length us, event | category | flops | bytes accessed | tf_op | source)
XLA Modules:
  0.0 1975.3 jit_solution(18432000550756671768)
XLA Ops:
  23.2 70.5 %all-reduce.18 = (bf16[768]{0:T(1024)(128)(2,1)}, bf16[768]{0:T(1024)(128)(2,1)S(1)}, bf16[768]{0:T(1024)(128)(2,1)S(1)}, bf16[768]{0:T(1024)(128)(2,1)}, bf16[7...) all-reduce(bf16[768]{0:T(1024)(128)(2,1)S(1)} %dynamic-update-slice, ...), channel_id=1, replica_groups=mesh['shard'=8,'seq'=4] {'shard'}, use_global_device_ids=true, to_apply=%add.2 | all-reduce | flops 6144 | bytes 24576
  131.1 23.6 %all-gather.10.cloned.1.call-done = bf16[768,768]{1,0:T(8,128)(2,1)} async-done(((bf16[96,768]{1,0:T(8,128)(2,1)}), bf16[768,768]{1,0:T(8,128)(2,1)}) %all-gather.10.cloned.1.call-update) | async-done | bytes 1179664 | tf_op jit(solution)/shard_map/all_gather | solution.py:160
  198.3 260.8 %while.48 = (s32[]{:T(128)}, bf16[8,512,3,64]{1,3,2,0:T(8,128)(2,1)}, f32[8,3,512]{2,1,0:T(4,128)}, bf16[8,512,3,64]{1,3,2,0:T(8,128)(2,1)}, bf16[4096,3,64]{0,2...) while((s32[]{:T(128)}, bf16[8,512,3,64]{1,3,2,0:T(8,128)(2,1)}, ...), condition=%wide.region_4.5_spmd.clone, body=%wide.region_1.4_spmd.clone.sunk | while | flops 1686211072 | bytes 179767440 | solution.py:59
  218.8 12.4 fusion.143
  251.5 12.4 fusion.143
  284.0 12.3 fusion.143
  316.4 12.3 fusion.143
  348.9 12.3 fusion.143
  381.4 12.3 fusion.143
  413.8 12.3 fusion.143
  446.3 12.3 fusion.143
  469.3 26.1 %all-gather = bf16[8,1,384]{2,1,0:T(2,128)(2,1)S(1)} all-gather(bf16[1,1,384]{2,1,0:T(2,128)(2,1)S(1)} %reshape.328), channel_id=1, replica_groups=mesh['shard'=8,'seq'=4] {'shard'}, dimensions={0}, use_global_device_ids=true | all-gather | bytes 6912 | tf_op jit(solution)/shard_map/all_gather | solution.py:169
  507.1 38.0 %multiply_convert_fusion.1 = (bf16[1024,3072]{1,0:T(8,128)(2,1)}, f32[1024,3072]{1,0:T(8,128)}, f32[1024,3072]{1,0:T(8,128)}) fusion(f32[3072]{0:T(1024)S(1)} %bitcast.256, bf16[768,3072]{1,0:T(8,128)(2,1)} %all-gather.16.cloned.1.call-done, f32[1024,768]{1,0:T(8,128)} %copy-done.6, f32[768]{0:T(1024)S(1)} %convert_element_type.216, ...), kind=kOutput, calls=%fused_computation.58 | convolution fusion | flops 5043388416 | bytes 39348224 | tf_op jit(solution)/shard_map/dot_general | solution.py:30
  567.7 17.5 convert_reduce_fusion
  617.1 15.7 all-to-all-done.5
  640.4 658.9 %while.49 = (s32[]{:T(128)}, f32[4096,3,64]{0,2,1:T(8,128)}, f32[4096,3,64]{0,2,1:T(8,128)}, bf16[8,512,3,64]{1,3,2,0:T(8,128)(2,1)}, bf16[8,512,3,64]{1,3,2,0:T...) while((s32[]{:T(128)}, f32[4096,3,64]{0,2,1:T(8,128)}, ...), condition=%wide.region_15.16_spmd.clone, body=%wide.region_13.15_spmd.clone.sunk | while | flops 4125035008 | bytes 207087776 | solution.py:100
  653.1 12.4 fusion.155
  665.5 16.6 multiply_reduce_fusion.6
  682.0 21.5 %multiply_convert_fusion.3 = bf16[3,512,4096]{2,1,0:T(8,128)(2,1)} fusion(f32[3,512,4096]{2,1,0:T(8,128)} %get-tuple-element.428, f32[3,512,4096]{2,1,0:T(8,128)} %fusion.153, f32[3,512]{1,0:T(4,128)S(1)} %get-tuple-element.429, f32[3,512]{1,0:T(4,128)S(1)} %dynamic-slice_bitcast_fusion.2, pred[4096]{0:T(1024)(128)(4,1)S(1)} %iota_compare_fusion.5), kind=kLoop, calls=%fused_computation.21.clone.1 | loop fusion | flops 37748736 | bytes 62930944 | tf_op jit(solution)/shard_map/while/body/eval_jaxpr/while/body/eval_jaxpr/convert_element_type | solution.py:87
  733.8 13.7 fusion.155
  747.4 16.3 multiply_reduce_fusion.6
  763.7 21.4 %multiply_convert_fusion.3 = bf16[3,512,4096]{2,1,0:T(8,128)(2,1)} fusion(f32[3,512,4096]{2,1,0:T(8,128)} %get-tuple-element.428, f32[3,512,4096]{2,1,0:T(8,128)} %fusion.153, f32[3,512]{1,0:T(4,128)S(1)} %get-tuple-element.429, f32[3,512]{1,0:T(4,128)S(1)} %dynamic-slice_bitcast_fusion.2, pred[4096]{0:T(1024)(128)(4,1)S(1)} %iota_compare_fusion.5), kind=kLoop, calls=%fused_computation.21.clone.1 | loop fusion | flops 37748736 | bytes 62930944 | tf_op jit(solution)/shard_map/while/body/eval_jaxpr/while/body/eval_jaxpr/convert_element_type | solution.py:87
  816.3 13.7 fusion.155
  829.9 16.3 multiply_reduce_fusion.6
  846.2 21.4 %multiply_convert_fusion.3 = bf16[3,512,4096]{2,1,0:T(8,128)(2,1)} fusion(f32[3,512,4096]{2,1,0:T(8,128)} %get-tuple-element.428, f32[3,512,4096]{2,1,0:T(8,128)} %fusion.153, f32[3,512]{1,0:T(4,128)S(1)} %get-tuple-element.429, f32[3,512]{1,0:T(4,128)S(1)} %dynamic-slice_bitcast_fusion.2, pred[4096]{0:T(1024)(128)(4,1)S(1)} %iota_compare_fusion.5), kind=kLoop, calls=%fused_computation.21.clone.1 | loop fusion | flops 37748736 | bytes 62930944 | tf_op jit(solution)/shard_map/while/body/eval_jaxpr/while/body/eval_jaxpr/convert_element_type | solution.py:87
  898.8 13.7 fusion.155
  912.4 16.3 multiply_reduce_fusion.6
  928.7 21.4 %multiply_convert_fusion.3 = bf16[3,512,4096]{2,1,0:T(8,128)(2,1)} fusion(f32[3,512,4096]{2,1,0:T(8,128)} %get-tuple-element.428, f32[3,512,4096]{2,1,0:T(8,128)} %fusion.153, f32[3,512]{1,0:T(4,128)S(1)} %get-tuple-element.429, f32[3,512]{1,0:T(4,128)S(1)} %dynamic-slice_bitcast_fusion.2, pred[4096]{0:T(1024)(128)(4,1)S(1)} %iota_compare_fusion.5), kind=kLoop, calls=%fused_computation.21.clone.1 | loop fusion | flops 37748736 | bytes 62930944 | tf_op jit(solution)/shard_map/while/body/eval_jaxpr/while/body/eval_jaxpr/convert_element_type | solution.py:87
  981.3 13.7 fusion.155
  994.9 16.3 multiply_reduce_fusion.6
  1011.2 21.4 %multiply_convert_fusion.3 = bf16[3,512,4096]{2,1,0:T(8,128)(2,1)} fusion(f32[3,512,4096]{2,1,0:T(8,128)} %get-tuple-element.428, f32[3,512,4096]{2,1,0:T(8,128)} %fusion.153, f32[3,512]{1,0:T(4,128)S(1)} %get-tuple-element.429, f32[3,512]{1,0:T(4,128)S(1)} %dynamic-slice_bitcast_fusion.2, pred[4096]{0:T(1024)(128)(4,1)S(1)} %iota_compare_fusion.5), kind=kLoop, calls=%fused_computation.21.clone.1 | loop fusion | flops 37748736 | bytes 62930944 | tf_op jit(solution)/shard_map/while/body/eval_jaxpr/while/body/eval_jaxpr/convert_element_type | solution.py:87
  1063.8 13.7 fusion.155
  1077.4 16.3 multiply_reduce_fusion.6
  1093.7 21.4 %multiply_convert_fusion.3 = bf16[3,512,4096]{2,1,0:T(8,128)(2,1)} fusion(f32[3,512,4096]{2,1,0:T(8,128)} %get-tuple-element.428, f32[3,512,4096]{2,1,0:T(8,128)} %fusion.153, f32[3,512]{1,0:T(4,128)S(1)} %get-tuple-element.429, f32[3,512]{1,0:T(4,128)S(1)} %dynamic-slice_bitcast_fusion.2, pred[4096]{0:T(1024)(128)(4,1)S(1)} %iota_compare_fusion.5), kind=kLoop, calls=%fused_computation.21.clone.1 | loop fusion | flops 37748736 | bytes 62930944 | tf_op jit(solution)/shard_map/while/body/eval_jaxpr/while/body/eval_jaxpr/convert_element_type | solution.py:87
  1146.3 13.7 fusion.155
  1159.9 16.3 multiply_reduce_fusion.6
  1176.2 21.4 %multiply_convert_fusion.3 = bf16[3,512,4096]{2,1,0:T(8,128)(2,1)} fusion(f32[3,512,4096]{2,1,0:T(8,128)} %get-tuple-element.428, f32[3,512,4096]{2,1,0:T(8,128)} %fusion.153, f32[3,512]{1,0:T(4,128)S(1)} %get-tuple-element.429, f32[3,512]{1,0:T(4,128)S(1)} %dynamic-slice_bitcast_fusion.2, pred[4096]{0:T(1024)(128)(4,1)S(1)} %iota_compare_fusion.5), kind=kLoop, calls=%fused_computation.21.clone.1 | loop fusion | flops 37748736 | bytes 62930944 | tf_op jit(solution)/shard_map/while/body/eval_jaxpr/while/body/eval_jaxpr/convert_element_type | solution.py:87
  1228.8 13.7 fusion.155
  1242.4 16.3 multiply_reduce_fusion.6
  1258.7 21.4 %multiply_convert_fusion.3 = bf16[3,512,4096]{2,1,0:T(8,128)(2,1)} fusion(f32[3,512,4096]{2,1,0:T(8,128)} %get-tuple-element.428, f32[3,512,4096]{2,1,0:T(8,128)} %fusion.153, f32[3,512]{1,0:T(4,128)S(1)} %get-tuple-element.429, f32[3,512]{1,0:T(4,128)S(1)} %dynamic-slice_bitcast_fusion.2, pred[4096]{0:T(1024)(128)(4,1)S(1)} %iota_compare_fusion.5), kind=kLoop, calls=%fused_computation.21.clone.1 | loop fusion | flops 37748736 | bytes 62930944 | tf_op jit(solution)/shard_map/while/body/eval_jaxpr/while/body/eval_jaxpr/convert_element_type | solution.py:87
  1305.3 30.2 %all_to_all.141 = bf16[1,8,512,1,192]{4,1,3,0,2:T(8,128)(2,1)} all-to-all(bf16[1,8,512,1,192]{4,1,3,0,2:T(8,128)(2,1)} %copy.126), channel_id=1, replica_groups=mesh['shard'=8,'seq'=4] {'seq'}, dimensions={2} | all-to-all | bytes 3145728 | tf_op jit(solution)/shard_map/all_to_all | solution.py:300
  1348.7 30.2 %all_to_all.142 = bf16[1,8,512,1,192]{4,1,3,0,2:T(8,128)(2,1)} all-to-all(bf16[1,8,512,1,192]{4,1,3,0,2:T(8,128)(2,1)} %copy.123), channel_id=1, replica_groups=mesh['shard'=8,'seq'=4] {'seq'}, dimensions={2} | all-to-all | bytes 3145728 | tf_op jit(solution)/shard_map/all_to_all | solution.py:299
  1393.6 30.2 %all_to_all.143 = bf16[1,8,512,1,192]{4,1,3,0,2:T(8,128)(2,1)} all-to-all(bf16[1,8,512,1,192]{4,1,3,0,2:T(8,128)(2,1)} %copy.129), channel_id=1, replica_groups=mesh['shard'=8,'seq'=4] {'seq'}, dimensions={2} | all-to-all | bytes 3145728 | tf_op jit(solution)/shard_map/all_to_all | solution.py:301
  1474.4 18.0 reduce-scatter.7.cloned.1.call-done
  1494.0 78.0 %reduce-scatter.11.cloned.1.call-done = f32[96,768]{1,0:T(8,128)} async-done(((f32[768,768]{1,0:T(8,128)}), f32[96,768]{1,0:T(8,128)}) %reduce-scatter.11.cloned.1.call-update) | async-done | bytes 294928 | tf_op jit(solution)/shard_map/reduce_scatter | solution.py:342
  1573.6 164.3 %reduce-scatter.15.cloned.1.call-done = f32[96,3072]{1,0:T(8,128)} async-done(((f32[768,3072]{1,0:T(8,128)}), f32[96,3072]{1,0:T(8,128)}) %reduce-scatter.15.cloned.1.call-update) | async-done | bytes 1179664 | tf_op jit(solution)/shard_map/reduce_scatter | solution.py:342
  1740.1 163.7 %reduce-scatter.17.cloned.1.call-done = f32[384,768]{1,0:T(8,128)} async-done(((f32[3072,768]{1,0:T(8,128)}), f32[384,768]{1,0:T(8,128)}) %reduce-scatter.17.cloned.1.call-update) | async-done | bytes 1179664 | tf_op jit(solution)/shard_map/reduce_scatter | solution.py:342
  1907.8 35.6 %all-reduce.17 = (bf16[768]{0:T(1024)(128)(2,1)S(1)}, bf16[768]{0:T(1024)(128)(2,1)S(1)}, bf16[768]{0:T(1024)(128)(2,1)S(1)}, bf16[768]{0:T(1024)(128)(2,1)S(1)}...) all-reduce(f32[768]{0:T(1024)S(1)} %mul.255, ...), channel_id=6, replica_groups=mesh['shard'=8,'seq'=4] {'shard'}, use_global_device_ids=true, to_apply=%region_26.27.clone | all-reduce | flops 9216 | bytes 55296
  (414 shorter events, 706.9 us)
Async XLA Ops:
  7.2 86.5 %all-gather.12.cloned.1.call-start = ((), (), s32[]{:S(2)}) async-start(), calls=%async_computation.18 | async-start | bytes 1327104 | tf_op jit(solution)/shard_map/all_gather | solution.py:161
  9.9 10.2 copy-start.52
  9.9 11.5 copy-start.56
  9.9 11.7 copy-start.57
  9.9 11.9 copy-start.58
  9.9 12.2 copy-start.59
  9.9 12.4 copy-start.60
  9.9 12.6 copy-start.61
  9.9 12.8 copy-start.62
  10.0 13.0 copy-start.63
  11.3 82.4 %all-to-all-start = ((bf16[8,1,128,768]{3,2,1,0:T(8,128)(2,1)}), bf16[8,1,128,768]{3,2,1,0:T(8,128)(2,1)S(1)}, u32[]{:S(2)}, u32[]{:S(2)}) async-start(bf16[8,1,128,768]{3,2,1,0:T(8,128)(2,1)} %bitcast_select_fusion), calls=%async_computation | async-start | bytes 3145728 | tf_op jit(solution)/shard_map/all_to_all | solution.py:193
  18.6 94.1 %all-gather.8.cloned.1.call-start = ((), (), s32[]{:S(2)}) async-start(), calls=%async_computation.16 | async-start | bytes 1327104 | tf_op jit(solution)/shard_map/all_gather | solution.py:159
  19.3 135.4 %all-gather.10.cloned.1.call-start = ((), (), s32[]{:S(2)}) async-start(), calls=%async_computation.17 | async-start | bytes 1327104 | tf_op jit(solution)/shard_map/all_gather | solution.py:160
  103.3 23.6 %all-to-all-start.3 = ((bf16[1,8,128,4,192]{2,1,4,0,3:T(8,128)(2,1)}), bf16[1,8,128,4,192]{2,1,4,0,3:T(8,128)(2,1)S(1)}, u32[]{:S(2)}, u32[]{:S(2)}) async-start(bf16[1,8,128,4,192]{2,1,4,0,3:T(8,128)(2,1)} %copy.115), calls=%async_computation.3 | async-start | bytes 3145728 | tf_op jit(solution)/shard_map/all_to_all | solution.py:217
  126.9 40.9 %all-to-all-start.1 = ((bf16[1,8,128,4,192]{2,1,4,0,3:T(8,128)(2,1)}), bf16[1,8,128,4,192]{2,1,4,0,3:T(8,128)(2,1)S(1)}, u32[]{:S(2)}, u32[]{:S(2)}) async-start(bf16[1,8,128,4,192]{2,1,4,0,3:T(8,128)(2,1)} %copy.109), calls=%async_computation.1 | async-start | bytes 3145728 | tf_op jit(solution)/shard_map/all_to_all | solution.py:215
  130.5 371.0 %all-gather.14.cloned.1.call-start = ((), (), s32[]{:S(2)}) async-start(), calls=%async_computation.19 | async-start | bytes 1327104 | tf_op jit(solution)/shard_map/all_gather | solution.py:162
  164.3 9.1 copy-start.65
  167.8 24.6 %all-to-all-start.2 = ((bf16[1,8,128,4,192]{2,1,4,0,3:T(8,128)(2,1)}), bf16[1,8,128,4,192]{2,1,4,0,3:T(8,128)(2,1)}, u32[]{:S(2)}, u32[]{:S(2)}) async-start(bf16[1,8,128,4,192]{2,1,4,0,3:T(8,128)(2,1)} %copy.112), calls=%async_computation.2 | async-start | bytes 3145728 | tf_op jit(solution)/shard_map/all_to_all | solution.py:216
  172.2 334.9 %all-gather.16.cloned.1.call-start = ((), (), s32[]{:S(2)}) async-start(), calls=%async_computation.20 | async-start | bytes 5308416 | tf_op jit(solution)/shard_map/all_gather | solution.py:168
  204.0 8.8 copy-start.2
  237.1 8.4 copy-start.2
  269.7 8.3 copy-start.2
  302.1 8.3 copy-start.2
  334.6 8.3 copy-start.2
  367.0 8.3 copy-start.2
  399.5 8.3 copy-start.2
  432.0 8.3 copy-start.2
  463.9 31.5 %all-to-all-start.4 = ((bf16[1,8,512,1,192]{4,1,3,0,2:T(8,128)(2,1)}), bf16[1,8,512,1,192]{4,1,3,0,2:T(8,128)(2,1)}, u32[]{:S(2)}, u32[]{:S(2)}) async-start(bf16[1,8,512,1,192]{4,1,3,0,2:T(8,128)(2,1)} %copy.117), calls=%async_computation.4 | async-start | bytes 4194304 | tf_op jit(solution)/shard_map/all_to_all | solution.py:223
  468.5 82.1 %all-gather.18.cloned.1.call-start = ((), (), s32[]{:S(2)}) async-start(), calls=%async_computation.21 | async-start | bytes 5308416 | tf_op jit(solution)/shard_map/all_gather | solution.py:170
  469.2 126.7 %copy-start.32 = (f32[768]{0:T(1024)}, f32[768]{0:T(1024)S(1)}, u32[]{:S(2)}) copy-start(f32[768]{0:T(1024)S(1)} %convert_element_type.215) | copy-start | bytes 9220
  469.2 81.4 %copy-start.34 = (f32[768]{0:T(1024)}, f32[768]{0:T(1024)S(1)}, u32[]{:S(2)}) copy-start(f32[768]{0:T(1024)S(1)} %convert_element_type.216) | copy-start | bytes 9220
  505.0 90.9 %copy-start.28 = (f32[1024]{0:T(1024)}, f32[1024]{0:T(1024)S(1)}, u32[]{:S(2)}) copy-start(f32[1024]{0:T(1024)S(1)} %broadcast_multiply_fusion.10) | copy-start | bytes 12292
  507.1 88.8 %copy-start.30 = (f32[1024]{0:T(1024)}, f32[1024]{0:T(1024)S(1)}, u32[]{:S(2)}) copy-start(f32[1024]{0:T(1024)S(1)} %fusion.76) | copy-start | bytes 12292
  567.3 18.0 copy-start.24
  567.7 17.5 copy-start.7
  609.1 23.6 %all-to-all-start.5 = ((bf16[1,8,128,4,192]{2,1,4,0,3:T(8,128)(2,1)}), bf16[1,8,128,4,192]{2,1,4,0,3:T(8,128)(2,1)S(1)}, u32[]{:S(2)}, u32[]{:S(2)}) async-start(bf16[1,8,128,4,192]{2,1,4,0,3:T(8,128)(2,1)} %copy.121), calls=%async_computation.5 | async-start | bytes 3145728 | tf_op jit(solution)/shard_map/all_to_all | solution.py:293
  612.7 858.4 %reduce-scatter.13.cloned.1.call-start = ((), (), s32[]{:S(2)}) async-start(), calls=%async_computation.25 | async-start | bytes 2654208 | tf_op jit(solution)/shard_map/reduce_scatter | solution.py:342
  617.1 855.7 %reduce-scatter.9.cloned.1.call-start = ((), (), s32[]{:S(2)}) async-start(), calls=%async_computation.23 | async-start | bytes 2654208 | tf_op jit(solution)/shard_map/reduce_scatter | solution.py:342
  1344.2 148.2 %reduce-scatter.7.cloned.1.call-start = ((), (), s32[]{:S(2)}) async-start(), calls=%async_computation.22 | async-start | bytes 2654208 | tf_op jit(solution)/shard_map/reduce_scatter | solution.py:342
  1387.5 184.5 %reduce-scatter.11.cloned.1.call-start = ((), (), s32[]{:S(2)}) async-start(), calls=%async_computation.24 | async-start | bytes 2654208 | tf_op jit(solution)/shard_map/reduce_scatter | solution.py:342
  1432.5 305.5 %reduce-scatter.15.cloned.1.call-start = ((), (), s32[]{:S(2)}) async-start(), calls=%async_computation.26 | async-start | bytes 10616832 | tf_op jit(solution)/shard_map/reduce_scatter | solution.py:342
  1443.9 460.0 %reduce-scatter.17.cloned.1.call-start = ((), (), s32[]{:S(2)}) async-start(), calls=%async_computation.27 | async-start | bytes 10616832 | tf_op jit(solution)/shard_map/reduce_scatter | solution.py:342
  1463.5 491.7 %all-to-all-start.9 = ((bf16[1,8,128,768]{3,2,0,1:T(8,128)(2,1)}), bf16[1,8,128,768]{3,2,0,1:T(8,128)(2,1)}, u32[]{:S(2)}, u32[]{:S(2)}) async-start(bf16[1,8,128,768]{3,2,0,1:T(8,128)(2,1)} %bitcast.227), calls=%async_computation.9 | async-start | bytes 3145728 | tf_op jit(solution)/shard_map/all_to_all | solution.py:318
  1467.9 490.6 %all-reduce.23.cloned.1.call-start = ((), (), s32[]{:S(2)}) async-start(), calls=%async_computation.28 | async-start | bytes 3538944 | tf_op jit(solution)/shard_map/psum | solution.py:344
  1906.0 49.3 %copy-start.45 = (s32[8]{0:T(128)S(1)}, s32[8]{0:T(128)}, u32[]{:S(2)}) copy-start(s32[8]{0:T(128)} %copy-done.44) | copy-start | bytes 100
  1955.3 13.2 copy-start.1
  1958.4 10.1 copy-start.15
  1958.5 9.0 copy-start.27
  (45 other events, 175.1 us)
Sparse Core Ops, SparseCore 0:
  10.2 60.7 all-gather.11
  73.2 39.4 all-gather.7
  114.8 39.8 all-gather.9
  156.7 39.8 all-gather.13
  198.6 78.6 all-gather.15
  471.3 79.3 all-gather.17
  617.2 67.5 reduce-scatter.12
  1344.4 66.2 reduce-scatter.8
  1414.2 78.1 reduce-scatter.6
  1495.7 76.2 reduce-scatter.10
  1575.6 162.3 reduce-scatter.14
  1741.4 162.3 reduce-scatter.16
  1907.8 46.3 all-reduce.22
where the time goes:
time: 1990 us; the launch traced here: 1980 us
  matrix products  745 us (37%)
  waiting for transfers between devices  490 us (25%)
  other arithmetic  280 us (14%)
  blocking collectives  229 us (12%)
  local copies, waits for them, and re-layouts  180 us (9%)
  starting transfers between devices  32.1 us (2%)
    reduce_scatter x6, waiting for transfers between devices, body(): lax.psum_scatter(all_terms, 'shard', scatter_dimension=0, tiled=True)  424 us
    convert_element_type x8, other arithmetic, one_block(): d_scores = (soft_probs * (d_probs - row_sum)).astype(jnp.bfloat16)  171 us
    dot_general x8, matrix products, one_block(): jnp.einsum('qhd,khd->hqk', g_block, value_rows, preferred_element_type=jn...  131 us
    dot_general x16, matrix products, masked_scores(): jnp.einsum('qhd,khd->hqk', q_block, key_rows, preferred_element_type=jnp....  125 us
    dot_general x8, matrix products, one_block(): jnp.einsum('hqk,qhd->khd', soft_probs.astype(jnp.bfloat16), g_block, pref...  108 us
    unnamed x2, blocking collectives  106 us
    dot_general x8, matrix products, one_block(): jnp.einsum('hqk,khd->qhd', soft_probs, value_rows, preferred_element_type...  98.6 us
    dot_general x8, matrix products, one_block(): jnp.einsum('hqk,qhd->khd', d_scores, q_block, preferred_element_type=jnp....  76 us
  transfers between devices with their start and end apart: 20, of which 10 were waited for; matrix products, arithmetic and copies ran while one was open for 54% of the time, Pallas kernels for 0%

commit v1 on v0

v1 whole, which is shorter than its diff:
```python
import functools, math
import jax
import jax.numpy as jnp
from jax import lax
from jax.experimental import pallas as pl
from jax.experimental.pallas import tpu as pltpu
from jax.sharding import Mesh, PartitionSpec as P

f32, bf16 = jnp.float32, jnp.bfloat16
LOG2E = 1.4426950408889634
LN2 = 0.6931471805599453
CH = 512
BQ = 1024
RB = 256
HD = 64
FAR = -1.0e30

def dg(a, b, ca, cb):
    return lax.dot_general(a, b, (((ca,), (cb,)), ((), ())), preferred_element_type=f32)


def three_parts(row):
    hi = row.astype(bf16).astype(f32)
    rest = row - hi
    mid = rest.astype(bf16).astype(f32)
    return hi, mid, rest - mid


def with_shift(top, shift):
    hi, mid, low = three_parts(shift)
    row = lax.broadcasted_iota(jnp.int32, (HD, top.shape[1]), 0)
    tail = jnp.where(row == 0, -hi, jnp.where(row == 1, -mid, jnp.where(row == 2, -low, jnp.where(row == 3, 1.0, 0.0))))
    return jnp.concatenate([top.astype(f32), tail], axis=0)


def qkv_kernel(stretch, spans_in, len_ref, x_ref, w_ref, b_ref, q_out, k_out, v_out, size_out):
    seq, owner, half = pl.program_id(0), pl.program_id(1), pl.program_id(2)
    rows = jnp.concatenate([x_ref[a, 0, z, 0] for z in range(spans_in) for a in range(2)], axis=0)
    made = dg(rows, w_ref[...], 1, 0) + b_ref[...]
    count = rows.shape[0]
    q_t = (made[:, :128] * (LOG2E / 8.0)).T
    q_out[0, 0, 0] = q_t[:HD].astype(bf16)
    q_out[0, 1, 0] = q_t[HD:].astype(bf16)
    lane = lax.broadcasted_iota(jnp.int32, (count, 128), 1)
    row = lax.broadcasted_iota(jnp.int32, (count, 128), 0) + half * count
    shift = int(math.log2(stretch))
    position = lax.shift_left(lax.shift_right_logical(row, shift), shift + 2) + owner * stretch + (row & (stretch - 1))
    hidden = jnp.where(position < len_ref[seq], 0.0, FAR)
    tail = jnp.where(lane == HD + 3, hidden, jnp.where(lane < HD + 3, 1.0, 0.0))
    keys = made[:, 128:256]
    picks = lax.broadcasted_iota(jnp.int32, (128, 128), 0) // HD == lax.broadcasted_iota(jnp.int32, (128, 128), 1)
    sizes = dg((keys * keys).astype(bf16), jnp.where(picks, 1.0, 0.0).astype(bf16), 1, 0)
    size_out[0, 0, 0] = jnp.max(sizes, axis=0, keepdims=True)
    for head in range(2):
        turned = keys if head == 0 else pltpu.roll(keys, HD, 1)
        full = jnp.where(lane < HD, turned, tail).astype(bf16)
        for j in range(count // 128):
            k_out[0, head, j] = full[j * 128:(j + 1) * 128]
    v_t = made[:, 256:384].T
    ones = jnp.where(lax.broadcasted_iota(jnp.int32, (HD, count), 0) < 3, 1.0, 0.0)
    for head in range(2):
        full = jnp.concatenate([v_t[head * HD:(head + 1) * HD], ones], axis=0).astype(bf16)
        for j in range(count // 128):
            v_out[0, head, j] = full[:, j * 128:(j + 1) * 128]


def project(gathered, weight, bias, lens):
    _, owners, zs, seqs, stretch, width = gathered.shape
    local = 2 * zs * stretch
    spans = 512 // (2 * stretch)
    halves = local // 512
    chunks = owners * local // CH
    per = chunks // halves
    return pl.pallas_call(
        functools.partial(qkv_kernel, stretch, spans),
        grid_spec=pltpu.PrefetchScalarGridSpec(
            num_scalar_prefetch=1, grid=(seqs, owners, halves),
            in_specs=[
                pl.BlockSpec((2, 1, spans, 1, stretch, width), lambda s, o, h, n: (0, o, h, s, 0, 0)),
                pl.BlockSpec((width, 384), lambda s, o, h, n: (0, 0)),
                pl.BlockSpec((1, 384), lambda s, o, h, n: (0, 0)),
            ],
            out_specs=[
                pl.BlockSpec((1, 2, 1, HD, 512), lambda s, o, h, n: (s, 0, o, 0, h)),
                pl.BlockSpec((1, 2, per, 128, 128), lambda s, o, h, n: (s, 0, h, o, 0)),
                pl.BlockSpec((1, 2, per, 128, 128), lambda s, o, h, n: (s, 0, h, 0, o)),
                pl.BlockSpec((1, 1, 1, 1, 128), lambda s, o, h, n: (s, o, h, 0, 0)),
            ]),
        out_shape=[
            jax.ShapeDtypeStruct((seqs, 2, owners, HD, local), bf16),
            jax.ShapeDtypeStruct((seqs, 2, chunks, CH, 128), bf16),
            jax.ShapeDtypeStruct((seqs, 2, chunks, 128, CH), bf16),
            jax.ShapeDtypeStruct((seqs, owners, halves, 1, 128), f32),
        ],
        compiler_params=pltpu.CompilerParams(vmem_limit_bytes=40 << 20),
        name="qkv",
    )(lens, gathered, weight, bias)


def step_on(q, j, count):
    last = j + 1 == count
    return jnp.where(last, q + 1, q), jnp.where(last, 0, j + 1)


def assemble(ref, q, head, core):
    if head == 0:
        return ref[0, 0, q]
    at = pl.multiple_of(core * 512, 512)
    return jnp.concatenate([ref[0, 0, 2 * q, :, pl.ds(at, 512)], ref[0, 0, 2 * q + 1, :, pl.ds(at, 512)]], axis=1)


def fwd_kernel(len_ref, core_ref, q_ref, k_ref, v_ref, size_ref, own_ref, sh_ref, lse_ref, acc, probs, qa, shifts):
    seq, head = pl.program_id(0), pl.program_id(1)
    count = lax.div(len_ref[seq] + (CH - 1), CH)
    parts = jnp.where(head == 0, 4, 2)
    lane = lax.broadcasted_iota(jnp.int32, (1, 128), 1)
    sizes = functools.reduce(jnp.maximum, [size_ref[0, o, h] for o in range(size_ref.shape[1]) for h in range(size_ref.shape[2])])
    widest = jnp.sqrt(jnp.max(jnp.where(lane == head, sizes, 0.0), axis=1, keepdims=True))

    def prepare(part, q_t):
        wide = q_t.astype(f32)
        shift = jnp.sqrt(jnp.sum(wide * wide, axis=0, keepdims=True)) * widest
        shifts[part] = shift
        qa[part] = with_shift(q_t, shift).astype(bf16)

    @pl.when(head == 0)
    def _():
        for part in range(4):
            prepare(part, assemble(q_ref, part, 0, 0))

    @pl.when(head == 1)
    def _():
        for part in range(2):
            prepare(part, assemble(q_ref, part, 1, core_ref[0]))

    def raised(part, j):
        return jnp.exp2(dg(k_ref[0, 0, j], qa[part], 1, 0)).astype(bf16)

    probs[0] = raised(0, 0)

    def body(t, carry):
        part, j = carry
        now = t & 1
        part_next, j_next = step_on(part, j, count)
        before = jnp.where(j == 0, 0.0, acc[...])
        acc[...] = before + dg(v_ref[0, 0, j], probs[now], 1, 0)
        probs[1 - now] = raised(jnp.minimum(part_next, parts - 1), j_next)

        @pl.when(j + 1 == count)
        def _():
            total = acc[HD:HD + 1]
            fine = (jnp.min(total) > 2.0 ** -90) & (jnp.max(total) < 2.0 ** 60)

            @pl.when(jnp.logical_not(fine))
            def _():
                plain = qa[part].astype(f32)
                row = lax.broadcasted_iota(jnp.int32, plain.shape, 0)
                qa[part] = jnp.where((row >= HD) & (row < HD + 3), 0.0, plain).astype(bf16)

                def peak(i, top):
                    return jnp.maximum(top, jnp.max(dg(k_ref[0, 0, i], qa[part], 1, 0), axis=0, keepdims=True))
                shift = lax.fori_loop(0, count, peak, jnp.full((1, BQ), FAR, f32))
                shifts[part] = shift
                qa[part] = with_shift(plain[:HD], shift).astype(bf16)
                acc[...] = jnp.zeros_like(acc)

                def again(i, carry):
                    acc[...] += dg(v_ref[0, 0, i], raised(part, i), 1, 0)
                    return carry
                lax.fori_loop(0, count, again, 0)

            total = acc[HD:HD + 1]
            mixed = (acc[:HD] * (1.0 / total)).astype(bf16)
            lse_ref[0, 0, part] = shifts[part] + jnp.log2(total)

            @pl.when(head == 0)
            def _():
                own_ref[0, part] = mixed

            @pl.when(head == 1)
            def _():
                sh_ref[0, 2 * part] = mixed[:, :512]
                sh_ref[0, 2 * part + 1] = mixed[:, 512:]
        return part_next, j_next

    lax.fori_loop(0, parts * count, body, (0, 0))


def head_spec(*dims):
    zeros = (0,) * len(dims)
    return pl.BlockSpec((1, 1) + dims, lambda s, h, n, c: (s, h) + zeros)


def seq_spec(*dims):
    zeros = (0,) * len(dims)
    return pl.BlockSpec((1,) + dims, lambda s, h, n, c: (s,) + zeros)


def attend_forward(q, k, v, sizes, lens, core):
    seqs, _, owners, _, local = q.shape
    chunks = k.shape[2]
    return pl.pallas_call(
        fwd_kernel,
        grid_spec=pltpu.PrefetchScalarGridSpec(
            num_scalar_prefetch=2, grid=(seqs, 2),
            in_specs=[
                head_spec(owners, HD, local), head_spec(chunks, CH, 128), head_spec(chunks, 128, CH),
                seq_spec(*sizes.shape[1:]),
            ],
            out_specs=[seq_spec(owners, HD, local), seq_spec(owners, HD, local // 2), head_spec(owners, 1, local)],
            scratch_shapes=[
                pltpu.VMEM((128, BQ), f32), pltpu.VMEM((2, CH, BQ), bf16), pltpu.VMEM((4, 128, BQ), bf16),
                pltpu.VMEM((4, 1, BQ), f32),
            ]),
        out_shape=[
            jax.ShapeDtypeStruct((seqs, owners, HD, local), bf16),
            jax.ShapeDtypeStruct((seqs, owners, HD, local // 2), bf16),
            jax.ShapeDtypeStruct((seqs, 2, owners, 1, local), f32),
        ],
        compiler_params=pltpu.CompilerParams(vmem_limit_bytes=48 << 20),
        name="attend_forward",
    )(lens, core, q, k, v, sizes)


def bwd_kernel(len_ref, core_ref, q_ref, k_ref, v_ref, lse_ref, own_ref, sh_ref, gown_ref, gsh_ref,
               dq_own, dq_sh, dkv_own, dkv_sh, dk_acc, dv_acc, dq_acc, qa, qat, ga, gat, pb, db):
    seq, head = pl.program_id(0), pl.program_id(1)
    count = lax.div(len_ref[seq] + (CH - 1), CH)
    chunks = k_ref.shape[2]
    parts = jnp.where(head == 0, 4, 2)
    dk_acc[...] = jnp.zeros_like(dk_acc)
    dv_acc[...] = jnp.zeros_like(dv_acc)

    def prepare(part, q_t, o_t, g_t):
        q_full = with_shift(q_t, lse_ref[0, 0, part])
        qat[part] = q_full.astype(bf16)
        qa[part] = q_full.T.astype(bf16)
        g_wide = g_t.astype(f32)
        meet = jnp.sum(g_wide * o_t.astype(f32), axis=0, keepdims=True)
        g_full = with_shift(g_t, meet)
        gat[part] = g_full.astype(bf16)
        ga[part] = g_full.T.astype(bf16)

    @pl.when(head == 0)
    def _():
        for part in range(4):
            prepare(part, assemble(q_ref, part, 0, 0), own_ref[0, part], gown_ref[0, part])

    @pl.when(head == 1)
    def _():
        for part in range(2):
            pair = [jnp.concatenate([ref[0, 2 * part], ref[0, 2 * part + 1]], axis=1) for ref in (sh_ref, gsh_ref)]
            prepare(part, assemble(q_ref, part, 1, core_ref[0]), *pair)

    def ahead(part, j, slot):
        raised = jnp.exp2(dg(qa[part], k_ref[0, 0, j], 1, 1))
        pb[slot] = raised.astype(bf16)
        db[slot] = (raised * dg(ga[part], v_ref[0, 0, j], 1, 0)).astype(bf16)

    ahead(0, 0, 0)

    def body(t, carry):
        part, j = carry
        now = t & 1
        part_next, j_next = step_on(part, j, count)
        dv_acc[j] += dg(gat[part], pb[now], 1, 0)[:HD]
        dk_acc[j] += dg(qat[part], db[now], 1, 0)[:HD]
        before = jnp.where(j == 0, 0.0, dq_acc[...])
        dq_acc[...] = before + dg(db[now], k_ref[0, 0, j], 1, 0)
        ahead(jnp.minimum(part_next, parts - 1), j_next, 1 - now)

        @pl.when(j + 1 == count)
        def _():
            dq_t = (dq_acc[...] * 0.125).T[:HD].astype(bf16)

            @pl.when(head == 0)
            def _():
                dq_own[0, part] = dq_t

            @pl.when(head == 1)
            def _():
                dq_sh[0, 2 * part] = dq_t[:, :512]
                dq_sh[0, 2 * part + 1] = dq_t[:, 512:]
        return part_next, j_next

    lax.fori_loop(0, parts * count, body, (0, 0))

    def flush(out):
        for j in range(chunks):
            for owner in range(4):
                cols = slice(owner * 128, (owner + 1) * 128)
                out[0, owner, 0, :, j * 128:(j + 1) * 128] = (dk_acc[j, :, cols] * LN2).astype(bf16)
                out[0, owner, 1, :, j * 128:(j + 1) * 128] = dv_acc[j, :, cols].astype(bf16)

    @pl.when(head == 0)
    def _():
        flush(dkv_own)

    @pl.when(head == 1)
    def _():
        flush(dkv_sh)


def attend_backward(q, k, v, lse, own, sh, g_own, g_sh, lens, core):
    seqs, _, owners, _, local = q.shape
    chunks = k.shape[2]
    own_spec, sh_spec = seq_spec(owners, HD, local), seq_spec(owners, HD, local // 2)
    return pl.pallas_call(
        bwd_kernel,
        grid_spec=pltpu.PrefetchScalarGridSpec(
            num_scalar_prefetch=2, grid=(seqs, 2),
            in_specs=[
                head_spec(owners, HD, local), head_spec(chunks, CH, 128), head_spec(chunks, 128, CH),
                head_spec(owners, 1, local), own_spec, sh_spec, own_spec, sh_spec,
            ],
            out_specs=[own_spec, sh_spec, seq_spec(owners, 2, HD, local), seq_spec(owners, 2, HD, local)],
            scratch_shapes=[
                pltpu.VMEM((chunks, HD, CH), f32), pltpu.VMEM((chunks, HD, CH), f32), pltpu.VMEM((BQ, 128), f32),
                pltpu.VMEM((4, BQ, 128), bf16), pltpu.VMEM((4, 128, BQ), bf16),
                pltpu.VMEM((4, BQ, 128), bf16), pltpu.VMEM((4, 128, BQ), bf16),
                pltpu.VMEM((2, BQ, CH), bf16), pltpu.VMEM((2, BQ, CH), bf16),
            ]),
        out_shape=[
            jax.ShapeDtypeStruct((seqs, owners, HD, local), bf16),
            jax.ShapeDtypeStruct((seqs, owners, HD, local // 2), bf16),
            jax.ShapeDtypeStruct((seqs, owners, 2, HD, local), bf16),
            jax.ShapeDtypeStruct((seqs, owners, 2, HD, local), bf16),
        ],
        compiler_params=pltpu.CompilerParams(vmem_limit_bytes=56 << 20),
        name="attend_backward",
    )(lens, core, q, k, v, lse, own, sh, g_own, g_sh)


def gelu_pair(u):
    half = 0.5 * (1.0 + lax.erf(u * 0.7071067811865476))
    return u * half, half + u * (0.3989422804014327 * jnp.exp2(u * u * (-0.5 * LOG2E)))


def norm_stats(v):
    mean = jnp.mean(v, axis=-1, keepdims=True)
    centred = v - mean
    inverse = lax.rsqrt(jnp.mean(centred * centred, axis=-1, keepdims=True) + 1e-12)
    return centred * inverse, inverse


def norm_back(grad, xhat, inverse, gain):
    g = grad * gain
    return (g - jnp.mean(g, axis=-1, keepdims=True) - xhat * jnp.mean(g * xhat, axis=-1, keepdims=True)) * inverse


def weight_part(ref, first, rows):
    part = ref[:, first:first + rows, :]
    return part.reshape(part.shape[0] * rows, part.shape[2])


def ffn_kernel(spans, at_ref, x_ref, own_ref, sh_ref, cot_ref, w_ref, bin_ref, vec_ref,
               act_out, resid_out, gown_out, gsh_out, active_out, dinner_out, normed_out, douter_out, dbranch_out,
               vec_sum, bin_sum, slope):
    step = pl.program_id(0)
    width = x_ref.shape[-1]
    rows = jnp.concatenate([x_ref[a, 0, z, 0] for z in range(spans) for a in range(2)], axis=0).astype(f32)
    mixed_t = jnp.concatenate(
        [part for p in range(4) for part in (own_ref[p, 0], sh_ref[p, 0], own_ref[p, 1])], axis=0)
    vec = vec_ref[...]
    branch = dg(mixed_t, weight_part(w_ref, 768, 96), 0, 0) + vec[0:1]
    xhat1, inv1 = norm_stats(rows + branch)
    normed = xhat1 * vec[1:2] + vec[2:3]
    low = normed.astype(bf16)
    normed_out[...] = low
    outer = normed + vec[3:4]
    for n in range(4):
        cols = slice(n * 768, (n + 1) * 768)
        inner = dg(low, weight_part(w_ref, 384 + 96 * n, 96), 1, 0) + bin_ref[:, cols]
        value, bend = gelu_pair(inner)
        active_out[:, cols] = value.astype(bf16)
        slope[:, cols] = bend.astype(bf16)
    outer = outer + dg(active_out[...], weight_part(w_ref, 0, 384), 1, 0)
    xhat2, inv2 = norm_stats(outer)
    act_out[...] = (xhat2 * vec[4:5] + vec[5:6]).astype(bf16)
    cot = cot_ref[...].astype(f32)
    d2 = norm_back(cot, xhat2, inv2, vec[4:5])
    d_outer = d2.astype(bf16)
    douter_out[...] = d_outer
    d_normed = d2
    sums_in = []
    for n in range(4):
        cols = slice(n * 768, (n + 1) * 768)
        d_active = dg(d_outer, weight_part(w_ref.at[2 * n:2 * n + 2], 0, 384), 1, 1)
        d_inner = (d_active * slope[:, cols].astype(f32)).astype(bf16)
        dinner_out[:, cols] = d_inner
        sums_in.append(jnp.sum(d_inner.astype(f32), axis=0, keepdims=True))
        d_normed = d_normed + dg(d_inner, weight_part(w_ref, 384 + 96 * n, 96), 1, 1)
    d1 = norm_back(d_normed, xhat1, inv1, vec[1:2])
    resid_out[...] = d1
    d_branch = d1.astype(bf16)
    dbranch_out[...] = d_branch
    g_t = dg(weight_part(w_ref, 768, 96), d_branch, 1, 1).astype(bf16)
    for p in range(4):
        gown_out[p, 0] = g_t[192 * p:192 * p + 64]
        gsh_out[p, 0] = g_t[192 * p + 64:192 * p + 128]
        gown_out[p, 1] = g_t[192 * p + 128:192 * p + 192]
    total = lambda a: jnp.sum(a, axis=0, keepdims=True)
    sums = jnp.concatenate([
        total(d_branch.astype(f32)), total(d_normed * xhat1), total(d_normed),
        total(d_outer.astype(f32)), total(cot * xhat2), total(cot), jnp.zeros((2, width), f32)], axis=0)

    @pl.when(step == 0)
    def _():
        vec_sum[...] = sums
        for n in range(4):
            bin_sum[:, n * 768:(n + 1) * 768] = sums_in[n]

    @pl.when(step > 0)
    def _():
        vec_sum[...] += sums
        for n in range(4):
            bin_sum[:, n * 768:(n + 1) * 768] += sums_in[n]


def feed_forward(gathered, own, sh, cotangent, weights, inner_bias, vectors, at):
    _, _, _, _, stretch, width = gathered.shape
    local = cotangent.shape[0]
    spans = RB // (2 * stretch)
    steps = local // RB
    half_steps = steps // 2
    wide = inner_bias.shape[1]
    rows = lambda n: pl.BlockSpec((RB, n), lambda r, a: (r, 0))
    fixed = lambda *dims: pl.BlockSpec(dims, lambda r, a: (0,) * len(dims))
    own_spec = pl.BlockSpec((4, 2, HD, RB), lambda r, a: (0, 0, 0, r))
    sh_spec = pl.BlockSpec((4, 1, HD, RB), lambda r, a: (0, r // half_steps, 0, r % half_steps))
    shape = jax.ShapeDtypeStruct
    return pl.pallas_call(
        functools.partial(ffn_kernel, spans),
        grid_spec=pltpu.PrefetchScalarGridSpec(
            num_scalar_prefetch=1, grid=(steps,),
            in_specs=[
                pl.BlockSpec((2, 1, spans, 1, stretch, width), lambda r, a: (0, a[1], r, a[0], 0, 0)),
                own_spec, sh_spec, rows(width),
                pl.BlockSpec(weights.shape, lambda r, a: (0, 0, 0), pipeline_mode=pl.Buffered(1)),
                fixed(1, wide), fixed(8, width),
            ],
            out_specs=[
                rows(width), rows(width), own_spec, sh_spec, rows(wide), rows(wide), rows(width), rows(width), rows(width),
                fixed(8, width), fixed(1, wide),
            ],
            scratch_shapes=[pltpu.VMEM((RB, wide), bf16)]),
        out_shape=[
            shape((local, width), bf16), shape((local, width), f32), shape(own.shape, bf16), shape(sh.shape, bf16),
            shape((local, wide), bf16), shape((local, wide), bf16), shape((local, width), bf16),
            shape((local, width), bf16), shape((local, width), bf16), shape((8, width), f32), shape((1, wide), f32),
        ],
        compiler_params=pltpu.CompilerParams(vmem_limit_bytes=60 << 20),
        name="feed_forward",
    )(at, gathered, own, sh, cotangent, weights, inner_bias, vectors)


def outer_grad_kernel(scale, active_ref, douter_ref, out_ref):
    made = (dg(active_ref[...], douter_ref[...], 0, 0) * scale).astype(bf16)
    out_ref[...] = made.reshape(out_ref.shape)


def inner_grad_kernel(scale, packed_ref, normed_ref, dinner_ref, own_ref, sh_ref, dbranch_ref, out_ref):
    step = pl.program_id(0)

    @pl.when(step < 4)
    def _():
        out_ref[...] = (dg(normed_ref[...], dinner_ref[...], 0, 0) * scale).astype(bf16).reshape(out_ref.shape)

    @pl.when(step == 4)
    def _():
        mixed_t = jnp.concatenate([
            part for p in range(4)
            for part in (own_ref[p, 0], jnp.concatenate([sh_ref[p, 0], sh_ref[p, 1]], axis=1), own_ref[p, 1])], axis=0)
        out_ref[...] = (dg(mixed_t, dbranch_ref[...], 1, 0) * scale).astype(bf16).reshape(out_ref.shape)


def weight_grads(scale, active, d_outer, normed, d_inner, own, sh, d_branch):
    local, wide = active.shape
    width = normed.shape[1]
    packed = pl.pallas_call(
        functools.partial(outer_grad_kernel, scale), grid=(4,),
        in_specs=[pl.BlockSpec((local, width), lambda m: (0, m)), pl.BlockSpec((local, width), lambda m: (0, 0))],
        out_specs=pl.BlockSpec((2, 384, width), lambda m: (m, 0, 0)),
        out_shape=jax.ShapeDtypeStruct((8, 896, width), bf16),
        compiler_params=pltpu.CompilerParams(vmem_limit_bytes=40 << 20), name="outer_grad",
    )(active, d_outer)
    fixed = lambda a: pl.BlockSpec(a.shape, lambda n: (0,) * a.ndim)
    return pl.pallas_call(
        functools.partial(inner_grad_kernel, scale), grid=(5,),
        in_specs=[
            pl.BlockSpec(memory_space=pl.ANY), fixed(normed),
            pl.BlockSpec((local, width), lambda n: (0, jnp.minimum(n, 3))), fixed(own), fixed(sh), fixed(d_branch)],
        out_specs=pl.BlockSpec((8, 96, width), lambda n: (0, 4 + n, 0)),
        out_shape=jax.ShapeDtypeStruct((8, 896, width), bf16), input_output_aliases={0: 0},
        compiler_params=pltpu.CompilerParams(vmem_limit_bytes=40 << 20), name="inner_grad",
    )(packed, normed, d_inner, own, sh, d_branch)


def head_grad_kernel(scale, spans, core_ref, x_ref, dqo_ref, dqs_ref, dko_ref, dks_ref, out_ref, bias_out, acc, bias_acc, stack):
    seq, owner, half = pl.program_id(0), pl.program_id(1), pl.program_id(2)
    first = (seq == 0) & (owner == 0) & (half == 0)
    last = (seq == pl.num_programs(0) - 1) & (owner == pl.num_programs(1) - 1) & (half == pl.num_programs(2) - 1)
    rows = jnp.concatenate([x_ref[a, 0, z, 0] for z in range(spans) for a in range(2)], axis=0)
    d_t = jnp.concatenate([
        dqo_ref[0, 0], jnp.where(half == core_ref[0], dqs_ref[0, 0].astype(f32), 0.0).astype(bf16),
        dko_ref[0, 0, 0], dks_ref[0, 0, 0], dko_ref[0, 0, 1], dks_ref[0, 0, 1]], axis=0)

    @pl.when(first)
    def _():
        acc[...] = jnp.zeros_like(acc)
        bias_acc[...] = jnp.zeros_like(bias_acc)
    acc[...] += dg(d_t, rows, 1, 0)
    bias_acc[...] += dg(jnp.ones((8, d_t.shape[1]), bf16), d_t, 1, 1)

    @pl.when(last)
    def _():
        out_ref[...] = (acc[...] * scale).T.astype(bf16)
        bias_out[...] = bias_acc[...] * scale


def head_grads(scale, gathered, dq_own, dq_sh, dkv_own, dkv_sh, core):
    _, owners, zs, seqs, stretch, width = gathered.shape
    local = 2 * zs * stretch
    spans = 512 // (2 * stretch)
    pair = pl.BlockSpec((1, 1, 2, HD, 512), lambda s, o, h, c: (s, o, 0, 0, h))
    return pl.pallas_call(
        functools.partial(head_grad_kernel, scale, spans),
        grid_spec=pltpu.PrefetchScalarGridSpec(
            num_scalar_prefetch=1, grid=(seqs, owners, local // 512),
            in_specs=[
                pl.BlockSpec((2, 1, spans, 1, stretch, width), lambda s, o, h, c: (0, o, h, s, 0, 0)),
                pl.BlockSpec((1, 1, HD, 512), lambda s, o, h, c: (s, o, 0, h)),
                pl.BlockSpec((1, 1, HD, 512), lambda s, o, h, c: (s, o, 0, 0)),
                pair, pair],
            out_specs=[pl.BlockSpec((width, 384), lambda s, o, h, c: (0, 0)), pl.BlockSpec((8, 384), lambda s, o, h, c: (0, 0))],
            scratch_shapes=[pltpu.VMEM((384, width), f32), pltpu.VMEM((8, 384), f32), pltpu.VMEM((8, 128), f32)]),
        out_shape=[jax.ShapeDtypeStruct((width, 384), bf16), jax.ShapeDtypeStruct((8, 384), f32)],
        compiler_params=pltpu.CompilerParams(vmem_limit_bytes=40 << 20), name="head_grads",
    )(core, gathered, dq_own, dq_sh, dkv_own, dkv_sh)


def token_grad_kernel(dqo_ref, dqs_ref, dko_ref, dks_ref, w_ref, resid_ref, out_ref):
    total = resid_ref[...]
    made = [[part for p in range(4) for part in (dqo_ref[p, 0], dqs_ref[p, 0], dqo_ref[p, 1])]]
    for kind in range(2):
        made.append([part for p in range(4) for part in (
            dko_ref[p, 0, kind],
            (dks_ref[p, 0, kind].astype(f32) + dks_ref[p, 1, kind].astype(f32)).astype(bf16),
            dko_ref[p, 1, kind])])
    for kind in range(3):
        total = total + dg(jnp.concatenate(made[kind], axis=0), weight_part(w_ref, 96 * kind, 96), 0, 1)
    out_ref[...] = total.astype(bf16)


def token_grad(dq_own, dq_sh, dkv_own, dkv_sh, weights, resid):
    local, width = resid.shape
    steps = local // RB
    half_steps = steps // 2
    rows = pl.BlockSpec((RB, width), lambda r: (r, 0))
    pair = pl.BlockSpec((4, 2, 2, HD, RB), lambda r: (0, 0, 0, 0, r))
    return pl.pallas_call(
        token_grad_kernel, grid=(steps,),
        in_specs=[
            pl.BlockSpec((4, 2, HD, RB), lambda r: (0, 0, 0, r)),
            pl.BlockSpec((4, 1, HD, RB), lambda r: (0, r // half_steps, 0, r % half_steps)),
            pair, pair, pl.BlockSpec(weights.shape, lambda r: (0, 0, 0)), rows],
        out_specs=rows, out_shape=jax.ShapeDtypeStruct((local, width), bf16),
        compiler_params=pltpu.CompilerParams(vmem_limit_bytes=40 << 20), name="token_grad",
    )(dq_own, dq_sh, dkv_own, dkv_sh, weights, resid)


PAIR = ("x", "y", "c")
ALL = ("z", "x", "y", "c")
SHARD = ("z", "x")


def canonical(packed, shards):
    if shards == 8:
        return packed
    width = packed.shape[2]
    per, keep = 96 * 8 // shards, shards // 8
    outer = packed[:, :4 * per].reshape(8, 384, width)
    inner = packed[:, 4 * per:8 * per].reshape(8, keep, 4, per, width).transpose(0, 2, 1, 3, 4).reshape(8, 384, width)
    output = packed[:, 8 * per:9 * per].reshape(8, 96, width)
    return jnp.concatenate([outer, inner, output, jnp.zeros((8, 32, width), packed.dtype)], axis=1)


def from_canonical(packed, shards):
    if shards == 8:
        return packed
    width = packed.shape[2]
    per, keep = 96 * 8 // shards, shards // 8
    outer = packed[:, :384].reshape(shards, 4 * per, width)
    inner = packed[:, 384:768].reshape(8, 4, keep, per, width).transpose(0, 2, 1, 3, 4).reshape(shards, 4 * per, width)
    output = packed[:, 768:864].reshape(shards, per, width)
    return jnp.concatenate([outer, inner, output, jnp.zeros((shards, 32, width), packed.dtype)], axis=1)


def canonical_heads(packed, shards):
    if shards == 8:
        return packed
    width = packed.shape[2]
    per = 96 * 8 // shards
    parts = [packed[:, k * per:(k + 1) * per].reshape(8, 96, width) for k in range(3)]
    return jnp.concatenate(parts + [jnp.zeros((8, 32, width), packed.dtype)], axis=1)


def quarter(rows):
    place = lax.axis_index("y") * 2 + lax.axis_index("c")
    part = rows.shape[0] // 4
    return lax.dynamic_slice_in_dim(rows, place * part, part)


def body(tokens, lengths, deal_order, w_query, w_key, w_value, w_output, b_query, b_value, b_output,
         ln1_gain, ln1_shift, w_inner, b_inner, w_outer, b_outer, ln2_gain, ln2_shift, cotangent):
    zs = lax.axis_size("z")
    shards = 2 * zs
    devices = shards * 4
    scale = 1.0 / devices
    seq_count, _, stretch, width = tokens.shape
    per = w_query.shape[0]
    x, y, c = lax.axis_index("x"), lax.axis_index("y"), lax.axis_index("c")
    core = c.astype(jnp.int32)[None]

    ordered = jnp.take(tokens[:, 0], deal_order, axis=0).reshape(zs, 2, stretch, width)
    spread = lax.all_to_all(ordered, "z", split_axis=0, concat_axis=0, tiled=True)

    def head_columns(matrix):
        heads = matrix.reshape(per, 2, 2, 3, HD)
        mine = lax.dynamic_index_in_dim(heads, y, axis=2, keepdims=False)
        own = lax.dynamic_index_in_dim(mine, 2 * c, axis=2, keepdims=False)
        return [own, mine[:, :, 1]]
    columns = jnp.concatenate(
        [col for matrix in (w_query, w_key, w_value) for col in head_columns(matrix)], axis=2).reshape(per, 768)
    pad = lambda v, n: jnp.pad(v, (0, n - v.shape[0]))[None]
    head_pack = jnp.concatenate(
        [columns, pad(b_query, width), pad(b_value, width), jnp.zeros((14, width), bf16)], axis=0)
    head_all = lax.all_gather(head_pack, SHARD, axis=0, tiled=False)
    head_weight = lax.dynamic_index_in_dim(
        head_all[:, :per].reshape(width, 2, 384), x, axis=1, keepdims=False)

    def head_bias(row):
        heads = head_all[:, per + row, :per].reshape(2, 2, 3, HD)
        mine = lax.dynamic_slice(heads, (x, y, 0, 0), (1, 1, 3, HD))[0, 0]
        return [lax.dynamic_index_in_dim(mine, 2 * c, axis=0, keepdims=False), mine[1]]
    bias_row = jnp.concatenate(head_bias(0) + [jnp.zeros((2 * HD,), bf16)] + head_bias(1)).astype(f32)[None]

    gathered = lax.all_gather(spread, PAIR, axis=0, tiled=False).reshape(2, 4, zs, 2, stretch, width)

    panels = w_inner.reshape(per, 4, 768)
    vectors = (b_output, ln1_gain, ln1_shift, b_outer, ln2_gain, ln2_shift)
    layer_pack = jnp.concatenate(
        [w_outer] + [panels[:, n] for n in range(4)] + [w_output]
        + [pad(b_inner, width)] + [pad(v, width) for v in vectors] + [jnp.zeros((25, width), bf16)], axis=0)
    layer_all = lax.all_gather(quarter(layer_pack), ALL, axis=0, tiled=True).reshape(shards, 9 * per + 32, width)
    layer_weights = canonical(layer_all, shards)
    inner_bias = layer_all[:, 9 * per, :4 * per].reshape(1, 3072).astype(f32)
    vector_rows = jnp.concatenate(
        [layer_all[:, 9 * per + 1 + n, :per].reshape(1, width) for n in range(6)] + [jnp.zeros((2, width), bf16)],
        axis=0).astype(f32)
    back_pack = jnp.concatenate([w_query, w_key, w_value, jnp.zeros((32, width), bf16)], axis=0)
    back_all = lax.all_gather(quarter(back_pack), ALL, axis=0, tiled=True).reshape(shards, 3 * per + 32, width)
    back_weights = canonical_heads(back_all, shards)

    group = lax.axis_index("z")
    slots = lax.dynamic_slice_in_dim(deal_order, group * 2, 2)
    matches = slots[:, None] == jnp.arange(seq_count, dtype=jnp.int32)[None, :]
    lens = jnp.sum(jnp.where(matches, lengths[None, :], 0), axis=1).astype(jnp.int32)

    q, k, v, sizes = project(gathered, head_weight, bias_row, lens)
    own, sh, lse = attend_forward(q, k, v, sizes, lens, core)

    def swap(array):
        flat = array.reshape((8,) + array.shape[2:])
        return lax.all_to_all(flat, PAIR, split_axis=0, concat_axis=0, tiled=True)

    def to_tokens(array):
        return swap(array).reshape((4, 2) + array.shape[2:])

    def to_heads(array):
        return swap(array).reshape((2, 4) + array.shape[2:])

    own_t, sh_t = to_tokens(own), to_tokens(sh)
    at = jnp.stack([x, y * 2 + c]).astype(jnp.int32)
    (act, resid, g_own, g_sh, active, d_inner, normed, d_outer, d_branch, vec_sums, bin_sums) = feed_forward(
        gathered, own_t, sh_t, cotangent.reshape(-1, width), layer_weights, inner_bias, vector_rows, at)
    g_own_h, g_sh_h = to_heads(g_own), to_heads(g_sh)
    packed = weight_grads(scale, active, d_outer, normed, d_inner, own_t, sh_t, d_branch)
    sums = jnp.concatenate([bin_sums.reshape(4, width), vec_sums, jnp.zeros((20, width), f32)], axis=0) * scale
    packed = packed.at[:, 864:].set(jnp.broadcast_to(sums.astype(bf16)[None], (8, 32, width)))
    ready = from_canonical(packed, shards)
    if shards != 8:
        ready = ready.at[:, 9 * per:].set(jnp.broadcast_to(sums.astype(bf16)[None], (shards, 32, width)))
    layer_part = lax.psum_scatter(ready.reshape(-1, width), ALL, scatter_dimension=0, tiled=True)
    layer_grads = lax.all_gather(layer_part, ("y", "c"), axis=0, tiled=True)

    dq_own, dq_sh, dkv_own, dkv_sh = attend_backward(q, k, v, lse, own, sh, g_own_h, g_sh_h, lens, core)
    back = (to_tokens(dq_own), to_tokens(dq_sh), to_tokens(dkv_own), to_tokens(dkv_sh))
    d_heads, d_bias = head_grads(scale, gathered, dq_own, dq_sh, dkv_own, dkv_sh, core)
    chunk = width // zs
    head_ready = jnp.concatenate([
        d_heads.reshape(zs, chunk, 384),
        jnp.broadcast_to(d_bias[:1].astype(bf16)[None], (zs, 16, 384))], axis=1)
    head_part = lax.psum_scatter(head_ready.reshape(-1, 384), "z", scatter_dimension=0, tiled=True)
    head_grads_all = lax.all_gather(head_part, PAIR, axis=0, tiled=False).reshape(4, 2, chunk + 16, 6, HD).astype(f32)

    d_rows = token_grad(*back, back_weights, resid)
    returned = lax.all_to_all(
        d_rows.reshape(shards, stretch, width), SHARD, split_axis=0, concat_axis=0, tiled=True)
    d_tokens = jnp.zeros_like(returned).at[deal_order].set(returned)[:, None]

    mine = lax.dynamic_slice_in_dim(head_grads_all, x * per, per, axis=2)

    def full(part, kind):
        own_part, shared = part[:, :, :, 2 * kind], part[:, :, :, 2 * kind + 1]
        both = shared[:, 0] + shared[:, 1]
        joined = jnp.stack([own_part[:, 0], both, own_part[:, 1]], axis=1)
        return joined.transpose(2, 0, 1, 3).reshape(part.shape[2], width)
    d_wq, d_wk, d_wv = (full(mine, kind) for kind in range(3))
    bias_part = head_grads_all[:, :, chunk:chunk + 1]
    place = lax.axis_index("z") * 2 + x
    own_slice = lambda row, n: lax.dynamic_slice_in_dim(row, place * n, n)
    d_bq = own_slice(full(bias_part, 0)[0], per)
    d_bv = own_slice(full(bias_part, 2)[0], per)

    layer_grads = layer_grads.astype(f32)
    d_wouter = layer_grads[:4 * per]
    d_winner = layer_grads[4 * per:8 * per].reshape(4, per, width).transpose(1, 0, 2).reshape(per, 4 * width)
    d_woutput = layer_grads[8 * per:9 * per]
    d_binner = own_slice(layer_grads[9 * per:9 * per + 4].reshape(-1), 4 * per)
    d_bo, d_g1, d_s1, d_bout, d_g2, d_s2 = (own_slice(layer_grads[9 * per + 4 + n], per) for n in range(6))
    return (act.reshape(1, shards, stretch, width), d_tokens, d_wq, d_wk, d_wv, d_woutput, d_bq, d_bv, d_bo,
            d_g1, d_s1, d_winner, d_binner, d_wouter, d_bout, d_g2, d_s2)


def solution(mesh):
    shards, splits = mesh.devices.shape
    fine = Mesh(mesh.devices.reshape(shards // 2, 2, splits // 2, 2), ALL)
    S, Q = SHARD, ("y", "c")
    row, mat = P(S), P(S, None)
    return jax.shard_map(
        body, mesh=fine,
        in_specs=(P(None, S, Q, None), P(), P(), mat, mat, mat, mat, row, row, row, row, row, mat, row, mat, row, row, row,
                  P(S, None, Q, None)),
        out_specs=(P(S, None, Q, None), P(None, S, Q, None), mat, mat, mat, mat, row, row, row, row, row, mat, row, mat,
                   row, row, row),
        check_vma=False)
```

time: 1990 us -> 830 us (0.42)
  matrix products: 745 us -> 0 us
  Pallas kernels: 0 us -> 291 us
  other arithmetic: 280 us -> 9.48 us
  waiting for transfers between devices: 490 us -> 250 us
  local copies, waits for them, and re-layouts: 180 us -> 82.6 us
  blocking collectives: 229 us -> 170 us
    dot_general x74 -> x0, matrix products: 745 us -> none  [the longest x8 131 us: one_block(): jnp.einsum('qhd,khd->hqk', g_block, value_rows, preferred_element_type=jn...]
    pallas_call x0 -> x8, Pallas kernels: none -> 291 us  [the longest x1 105 us: attend_forward(): pl.pallas_call(fwd_kernel, grid_spec=pltpu.PrefetchScalarGridSpec(num_sca...]
    reduce_scatter x6 -> x2, waiting for transfers between devices: 424 us -> 148 us  [the longest x1 110 us: body(): lax.psum_scatter(ready.reshape(-1, width), ALL, scatter_dimension=0, tile...]
    convert_element_type x40 -> x4, other arithmetic: 201 us -> 1.31 us  [the longest x1 0.61 us: body(): vector_rows = jnp.concatenate([layer_all[:, 9 * per + 1 + n, :per].reshap...]
    unnamed x2 -> x0, blocking collectives: 106 us -> none
    all_to_all x3 -> x7, blocking collectives: 90.5 us -> 170 us  [the longest x6 110 us: swap(): return lax.all_to_all(flat, PAIR, split_axis=0, concat_axis=0, tiled=True)]
    while x16 -> x0, local copies, waits for them, and re-layouts: 67 us -> none
    reduce_sum x19 -> x1, other arithmetic: 61.4 us -> 0.18 us  [body(): jnp.sum(jnp.where(matches, lengths[None, :], 0), axis=1).astype(jnp.int32)]
  transfers between devices with their start and end apart: 20 -> 11, of which waited for: 10 -> 6; matrix products, arithmetic and copies ran while one was open for 54% -> 6% of each run, Pallas kernels for 0% -> 17%
where the time goes in v1:
time: 830 us; the launch traced here: 832 us
  Pallas kernels  291 us (35%)
  waiting for transfers between devices  250 us (30%)
  blocking collectives  170 us (20%)
  local copies, waits for them, and re-layouts  82.6 us (10%)
  between operations  15.5 us (2%)
  starting transfers between devices  14.3 us (2%)
  other arithmetic  9.48 us (1%)
    all_to_all x6, blocking collectives, swap(): return lax.all_to_all(flat, PAIR, split_axis=0, concat_axis=0, tiled=True)  110 us
    reduce_scatter x1, waiting for transfers between devices, body(): lax.psum_scatter(ready.reshape(-1, width), ALL, scatter_dimension=0, tile...  110 us
    pallas_call x1, Pallas kernels, attend_forward(): pl.pallas_call(fwd_kernel, grid_spec=pltpu.PrefetchScalarGridSpec(num_sca...  105 us
    pallas_call x1, Pallas kernels, attend_backward(): pl.pallas_call(bwd_kernel, grid_spec=pltpu.PrefetchScalarGridSpec(num_sca...  89.3 us
    all_gather x1, waiting for transfers between devices, body(): lax.all_gather(spread, PAIR, axis=0, tiled=False)  62.2 us
    all_to_all x1, blocking collectives, body(): lax.all_to_all(ordered, 'z', split_axis=0, concat_axis=0, tiled=True)  59.8 us
    pallas_call x1, Pallas kernels, feed_forward(): pl.pallas_call(functools.partial(ffn_kernel, spans), grid_spec=pltpu.Pref...  41.1 us
    reduce_scatter x1, waiting for transfers between devices, body(): lax.psum_scatter(head_ready.reshape(-1, 384), 'z', scatter_dimension=0, t...  38.9 us
  transfers between devices with their start and end apart: 11, of which 6 were waited for; matrix products, arithmetic and copies ran while one was open for 6% of the time, Pallas kernels for 17%

profile of v1, /device:TPU:0, one launch (start us, length us, event | category | flops | bytes accessed | tf_op | source)
XLA Modules:
  0.0 832.3 jit_solution(9139484423899207477)
XLA Ops:
  14.2 59.8 %all_to_all.50 = bf16[4,2,128,768]{3,2,1,0:T(8,128)(2,1)} all-to-all(bf16[4,2,128,768]{3,2,1,0:T(8,128)(2,1)S(1)} %broadcast_select_fusion), channel_id=1, replica_groups=mesh['z'=4,'x'=2,'y'=2,'c'=2] {'z'}, dimensions={0} | all-to-all | bytes 3145728 | tf_op jit(solution)/shard_map/all_to_all | solution.py:626
  78.9 1.5 slice.275
  80.7 1.2 constant_dynamic-slice_fusion.11
  83.3 62.2 %all-gather.16.cloned.1.call-done = bf16[32,2,128,768]{3,2,1,0:T(8,128)(2,1)} async-done(((bf16[4,2,128,768]{3,2,1,0:T(8,128)(2,1)}), bf16[32,2,128,768]{3,2,1,0:T(8,128)(2,1)}) %all-gather.16.cloned.1.call-update) | async-done | bytes 12582928 | tf_op jit(solution)/shard_map/all_gather | solution.py:648
  145.5 17.3 %qkv.1 = (bf16[2,2,4,64,1024]{4,3,2,1,0:T(8,128)(2,1)S(1)}, bf16[2,2,8,512,128]{4,3,2,1,0:T(8,128)(2,1)S(1)}, bf16[2,2,8,128,512]{4,3,2,1,0:T(8,128)(2,1)S(1)}, f32[2,4,2,1,128]{4,3,2,1,0:T(1,128)S(1)}) custom-call(s32[2]{0:T(128)S(1)} %fusion.8.len_ref, bf16[2,4,4,2,128,768]{5,4,3,2,1,0:T(8,128)(2,1)} %bitcast.151, bf16[768,384]{1,0:T(8,128)(2,1)S(1)} %bitcast.146, ...), custom_call_target="tpu_custom_call" | custom-call | tf_op jit(solution)/shard_map/qkv/pallas_call | solution.py:74
  162.8 2.0 copy-done.2
  164.8 2.0 copy-done.3
  166.8 104.9 %attend_forward.1 = (bf16[2,4,64,1024]{3,2,1,0:T(8,128)(2,1)S(1)}, bf16[2,4,64,512]{3,2,1,0:T(8,128)(2,1)S(1)}, f32[2,2,4,1,1024]{4,3,2,1,0:T(1,128)S(1)}) custom-call(s32[2]{0:T(128)S(1)} %fusion.8.len_ref, s32[1]{0:T(128)} %bitcast.5.core_ref, bf16[2,2,4,64,1024]{4,3,2,1,0:T(8,128)(2,1)S(1)} %get-tuple-element.53.q_ref, ...), custom_call_target="tpu_custom_call" | custom-call | tf_op jit(solution)/shard_map/attend_forward/pallas_call | solution.py:202
  273.1 12.0 %all_to_all.51 = bf16[8,64,512]{2,1,0:T(8,128)(2,1)} all-to-all(bf16[8,64,512]{2,1,0:T(8,128)(2,1)S(1)} %bitcast.148), channel_id=1, replica_groups=mesh['z'=4,'x'=2,'y'=2,'c'=2] {'x','y','c'}, dimensions={0} | all-to-all | bytes 1048576 | tf_op jit(solution)/shard_map/all_to_all | solution.py:675
  285.1 3.6 all-to-all-start.1
  293.2 9.8 %all-to-all-done.1 = bf16[8,64,1024]{2,1,0:T(8,128)(2,1)S(1)} async-done(((bf16[8,64,1024]{2,1,0:T(8,128)(2,1)}), bf16[8,64,1024]{2,1,0:T(8,128)(2,1)S(1)}, u32[]{:S(2)}, u32[]{:S(2)}) %all-to-all-start.1) | async-done | bytes 1048608 | tf_op jit(solution)/shard_map/all_to_all | solution.py:675
  304.0 41.1 %feed_forward.1 = (bf16[1024,768]{1,0:T(8,128)(2,1)}, f32[1024,768]{1,0:T(8,128)}, bf16[4,2,64,1024]{3,2,1,0:T(8,128)(2,1)}, bf16[4,2,64,512]{3,2,1,0:T(8,128)(2...) custom-call(s32[2]{0:T(128)} %pad_add_fusion.at_ref, ...), custom_call_target="tpu_custom_call" | custom-call | tf_op jit(solution)/shard_map/feed_forward/pallas_call | solution.py:432
  345.2 13.2 %all_to_all.52 = bf16[8,64,512]{2,1,0:T(8,128)(2,1)} all-to-all(bf16[8,64,512]{2,1,0:T(8,128)(2,1)} %bitcast.178), channel_id=1, replica_groups=mesh['z'=4,'x'=2,'y'=2,'c'=2] {'x','y','c'}, dimensions={0} | all-to-all | bytes 1048576 | tf_op jit(solution)/shard_map/all_to_all | solution.py:675
  358.3 17.9 %all_to_all.53 = bf16[8,64,1024]{2,1,0:T(8,128)(2,1)} all-to-all(bf16[8,64,1024]{2,1,0:T(8,128)(2,1)S(1)} %bitcast.169), channel_id=1, replica_groups=mesh['z'=4,'x'=2,'y'=2,'c'=2] {'x','y','c'}, dimensions={0} | all-to-all | bytes 2097152 | tf_op jit(solution)/shard_map/all_to_all | solution.py:675
  376.3 89.3 %attend_backward.1 = (bf16[2,4,64,1024]{3,2,1,0:T(8,128)(2,1)}, bf16[2,4,64,512]{3,2,1,0:T(8,128)(2,1)}, bf16[2,4,2,64,1024]{4,3,2,1,0:T(8,128)(2,1)}, bf16[2,4,2,64,1024]{4,3,2,1,0:T(8,128)(2,1)}) custom-call(s32[2]{0:T(128)} %copy-done.27, s32[1]{0:T(128)} %bitcast.5.core_ref, bf16[2,2,4,64,1024]{4,3,2,1,0:T(8,128)(2,1)} %copy-done.6, ...), custom_call_target="tpu_custom_call" | custom-call | tf_op jit(solution)/shard_map/attend_backward/pallas_call | solution.py:308
  465.6 1.6 copy-done.7
  467.1 1.6 copy-done.8
  468.7 1.2 copy-done.15
  471.0 15.9 %head_grads.1 = (bf16[768,384]{1,0:T(8,128)(2,1)S(1)}, f32[8,384]{1,0:T(8,128)S(1)}) custom-call(s32[1]{0:T(128)} %bitcast.5.core_ref, bf16[2,4,4,2,128,768]{5,4,3,2,1,0:T(8,128)(2,1)} %bitcast.153, bf16[2,4,64,1024]{3,2,1,0:T(8,128)(2,1)S(1)} %copy-done.15, bf16[2,4,64,512]{3,2,1,0:T(8,128)(2,1)S(1)} %copy-done.21, ...), custom_call_target="tpu_custom_call" | custom-call | tf_op jit(solution)/shard_map/head_grads/pallas_call | solution.py:526
  488.9 38.9 %reduce-scatter.3.cloned.1.call-done = bf16[208,384]{1,0:T(8,128)(2,1)} async-done(((bf16[832,384]{1,0:T(8,128)(2,1)}), bf16[208,384]{1,0:T(8,128)(2,1)}) %reduce-scatter.3.cloned.1.call-update) | async-done | bytes 159760 | tf_op jit(solution)/shard_map/reduce_scatter | solution.py:704
  529.2 2.8 copy-done.11
  532.0 7.3 outer_grad.1.packed_ref
  539.3 2.8 copy-done.12
  542.1 8.7 %inner_grad.1 = bf16[8,896,768]{2,1,0:T(8,128)(2,1)} custom-call(bf16[8,896,768]{2,1,0:T(8,128)(2,1)} %outer_grad.1.packed_ref, bf16[1024,768]{1,0:T(8,128)(2,1)S(1)} %copy-done.23, bf16[1024,3072]{1,0:T(8,128)(2,1)S(1)} %copy-done.12, bf16[4,2,64,1024]{3,2,1,0:T(8,128)(2,1)S(1)} %bitcast.135, ...), custom_call_target="tpu_custom_call", output_to_operand_aliasing={{}: (0, {})} | custom-call | tf_op jit(solution)/shard_map/inner_grad/pallas_call | solution.py:488
  552.7 13.6 %all_to_all.54 = bf16[8,64,512]{2,1,0:T(8,128)(2,1)} all-to-all(bf16[8,64,512]{2,1,0:T(8,128)(2,1)S(1)} %bitcast.149), channel_id=1, replica_groups=mesh['z'=4,'x'=2,'y'=2,'c'=2] {'x','y','c'}, dimensions={0} | all-to-all | bytes 1048576 | tf_op jit(solution)/shard_map/all_to_all | solution.py:675
  566.4 23.4 %all_to_all.55 = bf16[8,64,1024]{2,1,0:T(8,128)(2,1)S(1)} all-to-all(bf16[8,64,1024]{2,1,0:T(8,128)(2,1)S(1)} %bitcast.144), channel_id=1, replica_groups=mesh['z'=4,'x'=2,'y'=2,'c'=2] {'x','y','c'}, dimensions={0} | all-to-all | bytes 2097152 | tf_op jit(solution)/shard_map/all_to_all | solution.py:675
  589.8 30.2 %all_to_all.56 = bf16[8,2,64,1024]{3,2,1,0:T(8,128)(2,1)S(1)} all-to-all(bf16[8,2,64,1024]{3,2,1,0:T(8,128)(2,1)S(1)} %bitcast.138), channel_id=1, replica_groups=mesh['z'=4,'x'=2,'y'=2,'c'=2] {'x','y','c'}, dimensions={0} | all-to-all | bytes 4194304 | tf_op jit(solution)/shard_map/all_to_all | solution.py:675
  620.0 4.4 all-to-all-start.8
  624.4 25.7 %all-to-all-done.8 = bf16[8,2,64,1024]{3,2,1,0:T(8,128)(2,1)} async-done(((bf16[8,2,64,1024]{3,2,1,0:T(8,128)(2,1)}), bf16[8,2,64,1024]{3,2,1,0:T(8,128)(2,1)}, u32[]{:S(2)}, u32[]{:S(2)}) %all-to-all-start.8) | async-done | bytes 2097184 | tf_op jit(solution)/shard_map/all_to_all | solution.py:675
  650.1 2.3 copy-done.17
  652.4 2.0 copy-done.18
  655.5 6.0 token_grad.1
  661.5 1.1 copy-done.10
  662.7 5.6 all-to-all-start.9
  668.6 3.0 copy.122
  671.6 6.8 reshape.359
  678.4 2.6 dynamic-slice_bitcast_fusion
  682.9 1.2 slice_add_fusion.1
  684.1 1.3 fusion.22
  685.4 109.6 %reduce-scatter.5.cloned.1.call-done = bf16[224,768]{1,0:T(8,128)(2,1)} async-done(((bf16[7168,768]{1,0:T(8,128)(2,1)}), bf16[224,768]{1,0:T(8,128)(2,1)}) %reduce-scatter.5.cloned.1.call-update) | async-done | bytes 344080 | tf_op jit(solution)/shard_map/reduce_scatter | solution.py:694
  796.5 1.3 slice_add_fusion
  797.7 1.3 fusion.21
  800.5 2.0 fusion.17
  802.5 1.2 copy.126
  807.5 3.1 scatter_fusion
  810.6 3.3 all-gather.14.cloned.1.call-done
  816.6 2.5 fusion.19
  823.4 1.6 slice.302
  (229 shorter events, 43.0 us)
Async XLA Ops:
  7.2 6.1 copy-start
  7.2 6.0 copy-start.45
  7.2 71.6 %all-gather.18.cloned.1.call-start = ((), (), s32[]{:S(2)}) async-start(), calls=%async_computation.18 | async-start | bytes 1548288 | tf_op jit(solution)/shard_map/all_gather | solution.py:638
  13.1 132.4 %all-gather.16.cloned.1.call-start = ((), (), s32[]{:S(2)}) async-start(), calls=%async_computation.17 | async-start | bytes 14155776 | tf_op jit(solution)/shard_map/all_gather | solution.py:648
  74.0 1.5 copy-start.38
  74.0 1.5 copy-start.39
  74.0 1.6 copy-start.40
  74.0 1.6 copy-start.41
  74.0 1.6 copy-start.42
  74.0 1.6 copy-start.43
  74.0 1.7 copy-start.44
  74.1 215.4 %all-gather.10.cloned.1.call-start = ((), (), s32[]{:S(2)}) async-start(), calls=%async_computation.12 | async-start | bytes 11354112 | tf_op jit(solution)/shard_map/all_gather | solution.py:655
  76.8 1.8 copy-start.46
  78.8 87.9 %copy-start.27 = (s32[2]{0:T(128)}, s32[2]{0:T(128)S(1)}, u32[]{:S(2)}) copy-start(s32[2]{0:T(128)S(1)} %fusion.8.len_ref) | copy-start | bytes 28
  162.8 2.0 copy-start.2
  164.8 2.0 copy-start.3
  166.8 104.9 %copy-start.6 = (bf16[2,2,4,64,1024]{4,3,2,1,0:T(8,128)(2,1)}, bf16[2,2,4,64,1024]{4,3,2,1,0:T(8,128)(2,1)S(1)}, u32[]{:S(2)}) copy-start(bf16[2,2,4,64,1024]{4,3,2,1,0:T(8,128)(2,1)S(1)} %get-tuple-element.53.q_ref) | copy-start | bytes 6291460
  272.3 12.8 %copy-start.14 = (bf16[2,4,64,1024]{3,2,1,0:T(8,128)(2,1)}, bf16[2,4,64,1024]{3,2,1,0:T(8,128)(2,1)S(1)}, u32[]{:S(2)}) copy-start(bf16[2,4,64,1024]{3,2,1,0:T(8,128)(2,1)S(1)} %get-tuple-element.57.own_ref) | copy-start | bytes 3145732
  285.1 17.9 %all-to-all-start.1 = ((bf16[8,64,1024]{2,1,0:T(8,128)(2,1)}), bf16[8,64,1024]{2,1,0:T(8,128)(2,1)S(1)}, u32[]{:S(2)}, u32[]{:S(2)}) async-start(bf16[8,64,1024]{2,1,0:T(8,128)(2,1)} %bitcast.143), calls=%async_computation.1 | async-start | bytes 2097152 | tf_op jit(solution)/shard_map/all_to_all | solution.py:675
  288.7 239.1 %reduce-scatter.3.cloned.1.call-start = ((), (), s32[]{:S(2)}) async-start(), calls=%async_computation.14 | async-start | bytes 798720 | tf_op jit(solution)/shard_map/reduce_scatter | solution.py:704
  345.2 13.2 %copy-start.29 = (bf16[4,2,64,1024]{3,2,1,0:T(8,128)(2,1)S(1)}, bf16[4,2,64,1024]{3,2,1,0:T(8,128)(2,1)}, u32[]{:S(2)}) copy-start(bf16[4,2,64,1024]{3,2,1,0:T(8,128)(2,1)} %get-tuple-element.61) | copy-start | bytes 3145732
  465.5 1.6 copy-start.7
  467.1 1.6 copy-start.8
  468.7 1.2 copy-start.15
  471.0 17.1 %copy-start.34 = (bf16[96,768]{1,0:T(8,128)(2,1)S(1)}, bf16[96,768]{1,0:T(8,128)(2,1)}, u32[]{:S(2)}) copy-start(bf16[96,768]{1,0:T(8,128)(2,1)} %param.26) | copy-start | bytes 442372
  486.9 1.2 copy-start.32
  487.0 41.5 %copy-start.37 = (f32[1,3072]{1,0:T(1,128)S(1)}, f32[1,3072]{1,0:T(1,128)}, u32[]{:S(2)}) copy-start(f32[1,3072]{1,0:T(1,128)} %get-tuple-element.75) | copy-start | bytes 36868
  487.0 42.2 %copy-start.25 = (bf16[1024,768]{1,0:T(8,128)(2,1)S(1)}, bf16[1024,768]{1,0:T(8,128)(2,1)}, u32[]{:S(2)}) copy-start(bf16[1024,768]{1,0:T(8,128)(2,1)} %get-tuple-element.71.douter_ref) | copy-start | bytes 4718596
  487.9 136.5 %all-gather.12.cloned.1.call-start = ((), (), s32[]{:S(2)}) async-start(), calls=%async_computation.13 | async-start | bytes 4055040 | tf_op jit(solution)/shard_map/all_gather | solution.py:662
  488.9 179.7 %all-gather.20.cloned.1.call-start = ((), (), s32[]{:S(2)}) async-start(), calls=%async_computation.19 | async-start | bytes 1437696 | tf_op jit(solution)/shard_map/all_gather | solution.py:705
  527.8 267.1 %reduce-scatter.5.cloned.1.call-start = ((), (), s32[]{:S(2)}) async-start(), calls=%async_computation.15 | async-start | bytes 11354112 | tf_op jit(solution)/shard_map/reduce_scatter | solution.py:694
  529.2 2.8 copy-start.11
  532.0 7.3 copy-start.5
  532.0 7.3 copy-start.13
  532.0 7.3 copy-start.23
  532.0 7.3 copy-start.24
  539.3 2.8 copy-start.12
  542.1 8.7 %copy-start.36 = (f32[8,768]{1,0:T(8,128)S(1)}, f32[8,768]{1,0:T(8,128)}, u32[]{:S(2)}) copy-start(f32[8,768]{1,0:T(8,128)} %get-tuple-element.76) | copy-start | bytes 73732
  551.7 14.7 %copy-start.16 = (bf16[2,4,64,1024]{3,2,1,0:T(8,128)(2,1)S(1)}, bf16[2,4,64,1024]{3,2,1,0:T(8,128)(2,1)}, u32[]{:S(2)}) copy-start(bf16[2,4,64,1024]{3,2,1,0:T(8,128)(2,1)} %get-tuple-element.63.dqo_ref) | copy-start | bytes 3145732
  552.7 37.1 %copy-start.9 = (bf16[2,4,2,64,1024]{4,3,2,1,0:T(8,128)(2,1)S(1)}, bf16[2,4,2,64,1024]{4,3,2,1,0:T(8,128)(2,1)}, u32[]{:S(2)}) copy-start(bf16[2,4,2,64,1024]{4,3,2,1,0:T(8,128)(2,1)} %get-tuple-element.65.dko_ref) | copy-start | bytes 6291460
  620.0 30.1 %all-to-all-start.8 = ((bf16[8,2,64,1024]{3,2,1,0:T(8,128)(2,1)}), bf16[8,2,64,1024]{3,2,1,0:T(8,128)(2,1)}, u32[]{:S(2)}, u32[]{:S(2)}) async-start(bf16[8,2,64,1024]{3,2,1,0:T(8,128)(2,1)} %bitcast.137), calls=%async_computation.8 | async-start | bytes 4194304 | tf_op jit(solution)/shard_map/all_to_all | solution.py:675
  650.1 2.3 copy-start.17
  652.4 2.0 copy-start.18
  661.5 1.1 copy-start.10
  662.7 144.7 %all-to-all-start.9 = ((bf16[8,128,768]{2,1,0:T(8,128)(2,1)}), bf16[8,128,768]{2,1,0:T(8,128)(2,1)}, u32[]{:S(2)}, u32[]{:S(2)}) async-start(bf16[8,128,768]{2,1,0:T(8,128)(2,1)} %bitcast.139), calls=%async_computation.9 | async-start | bytes 3145728 | tf_op jit(solution)/shard_map/all_to_all | solution.py:708
  668.3 145.7 %all-gather.14.cloned.1.call-start = ((), (), s32[]{:S(2)}) async-start(), calls=%async_computation.16 | async-start | bytes 1720320 | tf_op jit(solution)/shard_map/all_gather | solution.py:695
  810.6 8.5 %copy-start.28 = (bf16[8,128,768]{2,1,0:T(8,128)(2,1)}, bf16[8,128,768]{2,1,0:T(8,128)(2,1)S(1)}, u32[]{:S(2)}) copy-start(bf16[8,128,768]{2,1,0:T(8,128)(2,1)S(1)} %scatter_fusion) | copy-start | bytes 4718596
  816.6 8.4 %copy-start.1 = (bf16[8,1,128,768]{3,2,1,0:T(8,128)(2,1)S(1)}, bf16[8,1,128,768]{3,2,1,0:T(8,128)(2,1)}, u32[]{:S(2)}) copy-start(bf16[8,1,128,768]{3,2,1,0:T(8,128)(2,1)} %param.21) | copy-start | bytes 4718596
  (10 other events, 9.9 us)
Sparse Core Ops, SparseCore 0:
  13.3 57.6 all-gather.17
  74.2 71.2 all-gather.15
  149.0 89.1 all-gather.9
  488.0 39.7 reduce-scatter.2
  531.1 67.8 all-gather.11
  600.8 26.8 all-gather.19
  633.7 161.2 reduce-scatter.4
  796.5 17.4 all-gather.13

commit v2 on v1

--- a/solution.py
+++ b/solution.py
@@ -94,6 +94,7 @@
         ],
         compiler_params=pltpu.CompilerParams(vmem_limit_bytes=40 << 20),
         name="qkv",
+        cost_estimate=cost(2 * gathered.size * 384, gathered.size * 4),
     )(lens, gathered, weight, bias)
 
 
@@ -103,35 +104,26 @@
 
 
 def assemble(ref, q, head, core):
-    if head == 0:
+    if not head:
         return ref[0, 0, q]
     at = pl.multiple_of(core * 512, 512)
     return jnp.concatenate([ref[0, 0, 2 * q, :, pl.ds(at, 512)], ref[0, 0, 2 * q + 1, :, pl.ds(at, 512)]], axis=1)
 
 
-def fwd_kernel(len_ref, core_ref, q_ref, k_ref, v_ref, size_ref, own_ref, sh_ref, lse_ref, acc, probs, qa, shifts):
-    seq, head = pl.program_id(0), pl.program_id(1)
+def fwd_kernel(shared, len_ref, core_ref, q_ref, k_ref, v_ref, size_ref, out_ref, lse_ref, acc, probs, qa, shifts):
+    seq = pl.program_id(0)
     count = lax.div(len_ref[seq] + (CH - 1), CH)
-    parts = jnp.where(head == 0, 4, 2)
+    parts = 2 if shared else 4
     lane = lax.broadcasted_iota(jnp.int32, (1, 128), 1)
     sizes = functools.reduce(jnp.maximum, [size_ref[0, o, h] for o in range(size_ref.shape[1]) for h in range(size_ref.shape[2])])
-    widest = jnp.sqrt(jnp.max(jnp.where(lane == head, sizes, 0.0), axis=1, keepdims=True))
-
-    def prepare(part, q_t):
+    widest = jnp.sqrt(jnp.max(jnp.where(lane == int(shared), sizes, 0.0), axis=1, keepdims=True))
+
+    for part in range(parts):
+        q_t = assemble(q_ref, part, shared, core_ref[0])
         wide = q_t.astype(f32)
         shift = jnp.sqrt(jnp.sum(wide * wide, axis=0, keepdims=True)) * widest
         shifts[part] = shift
         qa[part] = with_shift(q_t, shift).astype(bf16)
-
-    @pl.when(head == 0)
-    def _():
-        for part in range(4):
-            prepare(part, assemble(q_ref, part, 0, 0))
-
-    @pl.when(head == 1)
-    def _():
-        for part in range(2):
-            prepare(part, assemble(q_ref, part, 1, core_ref[0]))
 
     def raised(part, j):
         return jnp.exp2(dg(k_ref[0, 0, j], qa[part], 1, 0)).astype(bf16)
@@ -171,86 +163,86 @@
 
             total = acc[HD:HD + 1]
             mixed = (acc[:HD] * (1.0 / total)).astype(bf16)
-            lse_ref[0, 0, part] = shifts[part] + jnp.log2(total)
-
-            @pl.when(head == 0)
-            def _():
-                own_ref[0, part] = mixed
-
-            @pl.when(head == 1)
-            def _():
-                sh_ref[0, 2 * part] = mixed[:, :512]
-                sh_ref[0, 2 * part + 1] = mixed[:, 512:]
+            lse_ref[0, part] = shifts[part] + jnp.log2(total)
+            if shared:
+                out_ref[0, 2 * part] = mixed[:, :512]
+                out_ref[0, 2 * part + 1] = mixed[:, 512:]
+            else:
+                out_ref[0, part] = mixed
         return part_next, j_next
 
     lax.fori_loop(0, parts * count, body, (0, 0))
 
 
-def head_spec(*dims):
+def head_spec(shared, *dims):
     zeros = (0,) * len(dims)
-    return pl.BlockSpec((1, 1) + dims, lambda s, h, n, c: (s, h) + zeros)
+    return pl.BlockSpec((1, 1) + dims, lambda s, n, c: (s, int(shared)) + zeros)
 
 
 def seq_spec(*dims):
     zeros = (0,) * len(dims)
-    return pl.BlockSpec((1,) + dims, lambda s, h, n, c: (s,) + zeros)
-
-
-def attend_forward(q, k, v, sizes, lens, core):
+    return pl.BlockSpec((1,) + dims, lambda s, n, c: (s,) + zeros)
+
+
+def cost(flops, moved, exps=0):
+    return pl.CostEstimate(flops=int(flops), bytes_accessed=int(moved), transcendentals=int(exps))
+
+
+def attend_forward(shared, q, k, v, sizes, lens, core):
     seqs, _, owners, _, local = q.shape
     chunks = k.shape[2]
+    held = local // 2 if shared else local
+    parts = owners * held // BQ
+    pairs = seqs * parts * BQ * chunks * CH * 0.6
     return pl.pallas_call(
-        fwd_kernel,
+        functools.partial(fwd_kernel, shared),
         grid_spec=pltpu.PrefetchScalarGridSpec(
-            num_scalar_prefetch=2, grid=(seqs, 2),
+            num_scalar_prefetch=2, grid=(seqs,),
             in_specs=[
-                head_spec(owners, HD, local), head_spec(chunks, CH, 128), head_spec(chunks, 128, CH),
+                head_spec(shared, owners, HD, local), head_spec(shared, chunks, CH, 128), head_spec(shared, chunks, 128, CH),
                 seq_spec(*sizes.shape[1:]),
             ],
-            out_specs=[seq_spec(owners, HD, local), seq_spec(owners, HD, local // 2), head_spec(owners, 1, local)],
+            out_specs=[seq_spec(owners, HD, held), seq_spec(parts, 1, BQ)],
             scratch_shapes=[
-                pltpu.VMEM((128, BQ), f32), pltpu.VMEM((2, CH, BQ), bf16), pltpu.VMEM((4, 128, BQ), bf16),
-                pltpu.VMEM((4, 1, BQ), f32),
+                pltpu.VMEM((128, BQ), f32), pltpu.VMEM((2, CH, BQ), bf16), pltpu.VMEM((parts, 128, BQ), bf16),
+                pltpu.VMEM((parts, 1, BQ), f32),
             ]),
         out_shape=[
-            jax.ShapeDtypeStruct((seqs, owners, HD, local), bf16),
-            jax.ShapeDtypeStruct((seqs, owners, HD, local // 2), bf16),
-            jax.ShapeDtypeStruct((seqs, 2, owners, 1, local), f32),
+            jax.ShapeDtypeStruct((seqs, owners, HD, held), bf16),
+            jax.ShapeDtypeStruct((seqs, parts, 1, BQ), f32),
         ],
         compiler_params=pltpu.CompilerParams(vmem_limit_bytes=48 << 20),
-        name="attend_forward",
+        cost_estimate=cost(pairs * 1024, seqs * chunks * CH * 512, pairs),
+        name="attend_forward_shared" if shared else "attend_forward_own",
     )(lens, core, q, k, v, sizes)
 
 
-def bwd_kernel(len_ref, core_ref, q_ref, k_ref, v_ref, lse_ref, own_ref, sh_ref, gown_ref, gsh_ref,
-               dq_own, dq_sh, dkv_own, dkv_sh, dk_acc, dv_acc, dq_acc, qa, qat, ga, gat, pb, db):
-    seq, head = pl.program_id(0), pl.program_id(1)
+def bwd_kernel(shared, len_ref, core_ref, q_ref, k_ref, v_ref, lse_ref, out_ref, gout_ref, *rest):
+    if shared:
+        dq_ref, dkv_ref, dk_acc, dv_acc, dq_acc, qa, qat, ga, gat, pb, db = rest
+    else:
+        dqkv_ref, dk_acc, dv_acc, dq_acc, qa, qat, ga, gat, pb, db = rest
+    seq = pl.program_id(0)
     count = lax.div(len_ref[seq] + (CH - 1), CH)
     chunks = k_ref.shape[2]
-    parts = jnp.where(head == 0, 4, 2)
+    parts = 2 if shared else 4
     dk_acc[...] = jnp.zeros_like(dk_acc)
     dv_acc[...] = jnp.zeros_like(dv_acc)
 
-    def prepare(part, q_t, o_t, g_t):
-        q_full = with_shift(q_t, lse_ref[0, 0, part])
+    def piece(ref, part):
+        if shared:
+            return jnp.concatenate([ref[0, 2 * part], ref[0, 2 * part + 1]], axis=1)
+        return ref[0, part]
+
+    for part in range(parts):
+        q_full = with_shift(assemble(q_ref, part, shared, core_ref[0]), lse_ref[0, part])
         qat[part] = q_full.astype(bf16)
         qa[part] = q_full.T.astype(bf16)
-        g_wide = g_t.astype(f32)
-        meet = jnp.sum(g_wide * o_t.astype(f32), axis=0, keepdims=True)
+        g_t = piece(gout_ref, part)
+        meet = jnp.sum(g_t.astype(f32) * piece(out_ref, part).astype(f32), axis=0, keepdims=True)
         g_full = with_shift(g_t, meet)
         gat[part] = g_full.astype(bf16)
         ga[part] = g_full.T.astype(bf16)
-
-    @pl.when(head == 0)
-    def _():
-        for part in range(4):
-            prepare(part, assemble(q_ref, part, 0, 0), own_ref[0, part], gown_ref[0, part])
-
-    @pl.when(head == 1)
-    def _():
-        for part in range(2):
-            pair = [jnp.concatenate([ref[0, 2 * part], ref[0, 2 * part + 1]], axis=1) for ref in (sh_ref, gsh_ref)]
-            prepare(part, assemble(q_ref, part, 1, core_ref[0]), *pair)
 
     def ahead(part, j, slot):
         raised = jnp.exp2(dg(qa[part], k_ref[0, 0, j], 1, 1))
@@ -272,63 +264,60 @@
         @pl.when(j + 1 == count)
         def _():
             dq_t = (dq_acc[...] * 0.125).T[:HD].astype(bf16)
-
-            @pl.when(head == 0)
-            def _():
-                dq_own[0, part] = dq_t
-
-            @pl.when(head == 1)
-            def _():
-                dq_sh[0, 2 * part] = dq_t[:, :512]
-                dq_sh[0, 2 * part + 1] = dq_t[:, 512:]
+            if shared:
+                dq_ref[0, 2 * part] = dq_t[:, :512]
+                dq_ref[0, 2 * part + 1] = dq_t[:, 512:]
+            else:
+                dqkv_ref[0, part, 0] = dq_t
         return part_next, j_next
 
     lax.fori_loop(0, parts * count, body, (0, 0))
-
-    def flush(out):
-        for j in range(chunks):
-            for owner in range(4):
-                cols = slice(owner * 128, (owner + 1) * 128)
-                out[0, owner, 0, :, j * 128:(j + 1) * 128] = (dk_acc[j, :, cols] * LN2).astype(bf16)
-                out[0, owner, 1, :, j * 128:(j + 1) * 128] = dv_acc[j, :, cols].astype(bf16)
-
-    @pl.when(head == 0)
-    def _():
-        flush(dkv_own)
-
-    @pl.when(head == 1)
-    def _():
-        flush(dkv_sh)
-
-
-def attend_backward(q, k, v, lse, own, sh, g_own, g_sh, lens, core):
+    for j in range(chunks):
+        for owner in range(4):
+            cols = slice(owner * 128, (owner + 1) * 128)
+            dk = (dk_acc[j, :, cols] * LN2).astype(bf16)
+            dv = dv_acc[j, :, cols].astype(bf16)
+            if shared:
+                dkv_ref[0, 0, owner, :, j * 128:(j + 1) * 128] = dk
+                dkv_ref[1, 0, owner, :, j * 128:(j + 1) * 128] = dv
+            else:
+                dqkv_ref[0, owner, 1, :, j * 128:(j + 1) * 128] = dk
+                dqkv_ref[0, owner, 2, :, j * 128:(j + 1) * 128] = dv
+
+
+def attend_backward(shared, q, k, v, lse, out, g_out, lens, core):
     seqs, _, owners, _, local = q.shape
     chunks = k.shape[2]
-    own_spec, sh_spec = seq_spec(owners, HD, local), seq_spec(owners, HD, local // 2)
+    held = out.shape[3]
+    parts = owners * held // BQ
+    pairs = seqs * parts * BQ * chunks * CH * 0.6
+    shape = jax.ShapeDtypeStruct
+    if shared:
+        out_specs = [seq_spec(owners, HD, held), pl.BlockSpec((2, 1, owners, HD, local), lambda s, n, c: (0, s, 0, 0, 0))]
+        out_shape = [shape((seqs, owners, HD, held), bf16), shape((2, seqs, owners, HD, local), bf16)]
+    else:
+        out_specs = [seq_spec(owners, 3, HD, local)]
+        out_shape = [shape((seqs, owners, 3, HD, local), bf16)]
     return pl.pallas_call(
-        bwd_kernel,
+        functools.partial(bwd_kernel, shared),
         grid_spec=pltpu.PrefetchScalarGridSpec(
-            num_scalar_prefetch=2, grid=(seqs, 2),
+            num_scalar_prefetch=2, grid=(seqs,),
             in_specs=[
-                head_spec(owners, HD, local), head_spec(chunks, CH, 128), head_spec(chunks, 128, CH),
-                head_spec(owners, 1, local), own_spec, sh_spec, own_spec, sh_spec,
+                head_spec(shared, owners, HD, local), head_spec(shared, chunks, CH, 128), head_spec(shared, chunks, 128, CH),
+                seq_spec(parts, 1, BQ), seq_spec(owners, HD, held), seq_spec(owners, HD, held),
             ],
-            out_specs=[own_spec, sh_spec, seq_spec(owners, 2, HD, local), seq_spec(owners, 2, HD, local)],
+            out_specs=out_specs,
             scratch_shapes=[
                 pltpu.VMEM((chunks, HD, CH), f32), pltpu.VMEM((chunks, HD, CH), f32), pltpu.VMEM((BQ, 128), f32),
-                pltpu.VMEM((4, BQ, 128), bf16), pltpu.VMEM((4, 128, BQ), bf16),
-                pltpu.VMEM((4, BQ, 128), bf16), pltpu.VMEM((4, 128, BQ), bf16),
+                pltpu.VMEM((parts, BQ, 128), bf16), pltpu.VMEM((parts, 128, BQ), bf16),
+                pltpu.VMEM((parts, BQ, 128), bf16), pltpu.VMEM((parts, 128, BQ), bf16),
                 pltpu.VMEM((2, BQ, CH), bf16), pltpu.VMEM((2, BQ, CH), bf16),
             ]),
-        out_shape=[
-            jax.ShapeDtypeStruct((seqs, owners, HD, local), bf16),
-            jax.ShapeDtypeStruct((seqs, owners, HD, local // 2), bf16),
-            jax.ShapeDtypeStruct((seqs, owners, 2, HD, local), bf16),
-            jax.ShapeDtypeStruct((seqs, owners, 2, HD, local), bf16),
-        ],
+        out_shape=out_shape,
         compiler_params=pltpu.CompilerParams(vmem_limit_bytes=56 << 20),
-        name="attend_backward",
-    )(lens, core, q, k, v, lse, own, sh, g_own, g_sh)
+        cost_estimate=cost(pairs * 100, seqs * chunks * CH * 2048),
+        name="attend_backward_shared" if shared else "attend_backward_own",
+    )(lens, core, q, k, v, lse, out, g_out)
 
 
 def gelu_pair(u):
@@ -451,6 +440,7 @@
         ],
         compiler_params=pltpu.CompilerParams(vmem_limit_bytes=60 << 20),
         name="feed_forward",
+        cost_estimate=cost(local * width * (width + 2 * wide) * 4, local * wide * 20),
     )(at, gathered, own, sh, cotangent, weights, inner_bias, vectors)
 
 
@@ -483,6 +473,7 @@
         out_specs=pl.BlockSpec((2, 384, width), lambda m: (m, 0, 0)),
         out_shape=jax.ShapeDtypeStruct((8, 896, width), bf16),
         compiler_params=pltpu.CompilerParams(vmem_limit_bytes=40 << 20), name="outer_grad",
+        cost_estimate=cost(2 * local * wide * width, 2 * wide * (local + width)),
     )(active, d_outer)
     fixed = lambda a: pl.BlockSpec(a.shape, lambda n: (0,) * a.ndim)
     return pl.pallas_call(
@@ -493,17 +484,18 @@
         out_specs=pl.BlockSpec((8, 96, width), lambda n: (0, 4 + n, 0)),
         out_shape=jax.ShapeDtypeStruct((8, 896, width), bf16), input_output_aliases={0: 0},
         compiler_params=pltpu.CompilerParams(vmem_limit_bytes=40 << 20), name="inner_grad",
+        cost_estimate=cost(2 * local * (wide + width) * width, 2 * (wide + width) * (local + width)),
     )(packed, normed, d_inner, own, sh, d_branch)
 
 
-def head_grad_kernel(scale, spans, core_ref, x_ref, dqo_ref, dqs_ref, dko_ref, dks_ref, out_ref, bias_out, acc, bias_acc, stack):
+def head_grad_kernel(scale, spans, core_ref, x_ref, own_ref, dqs_ref, dks_ref, out_ref, bias_out, acc, bias_acc):
     seq, owner, half = pl.program_id(0), pl.program_id(1), pl.program_id(2)
     first = (seq == 0) & (owner == 0) & (half == 0)
     last = (seq == pl.num_programs(0) - 1) & (owner == pl.num_programs(1) - 1) & (half == pl.num_programs(2) - 1)
     rows = jnp.concatenate([x_ref[a, 0, z, 0] for z in range(spans) for a in range(2)], axis=0)
     d_t = jnp.concatenate([
-        dqo_ref[0, 0], jnp.where(half == core_ref[0], dqs_ref[0, 0].astype(f32), 0.0).astype(bf16),
-        dko_ref[0, 0, 0], dks_ref[0, 0, 0], dko_ref[0, 0, 1], dks_ref[0, 0, 1]], axis=0)
+        own_ref[0, 0, 0], jnp.where(half == core_ref[0], dqs_ref[0, 0].astype(f32), 0.0).astype(bf16),
+        own_ref[0, 0, 1], dks_ref[0, 0, 0], own_ref[0, 0, 2], dks_ref[1, 0, 0]], axis=0)
 
     @pl.when(first)
     def _():
@@ -518,55 +510,52 @@
         bias_out[...] = bias_acc[...] * scale
 
 
-def head_grads(scale, gathered, dq_own, dq_sh, dkv_own, dkv_sh, core):
+def head_grads(scale, gathered, dqkv_own, dq_sh, dkv_sh, core):
     _, owners, zs, seqs, stretch, width = gathered.shape
     local = 2 * zs * stretch
     spans = 512 // (2 * stretch)
-    pair = pl.BlockSpec((1, 1, 2, HD, 512), lambda s, o, h, c: (s, o, 0, 0, h))
     return pl.pallas_call(
         functools.partial(head_grad_kernel, scale, spans),
         grid_spec=pltpu.PrefetchScalarGridSpec(
             num_scalar_prefetch=1, grid=(seqs, owners, local // 512),
             in_specs=[
                 pl.BlockSpec((2, 1, spans, 1, stretch, width), lambda s, o, h, c: (0, o, h, s, 0, 0)),
-                pl.BlockSpec((1, 1, HD, 512), lambda s, o, h, c: (s, o, 0, h)),
+                pl.BlockSpec((1, 1, 3, HD, 512), lambda s, o, h, c: (s, o, 0, 0, h)),
                 pl.BlockSpec((1, 1, HD, 512), lambda s, o, h, c: (s, o, 0, 0)),
-                pair, pair],
+                pl.BlockSpec((2, 1, 1, HD, 512), lambda s, o, h, c: (0, s, o, 0, h))],
             out_specs=[pl.BlockSpec((width, 384), lambda s, o, h, c: (0, 0)), pl.BlockSpec((8, 384), lambda s, o, h, c: (0, 0))],
-            scratch_shapes=[pltpu.VMEM((384, width), f32), pltpu.VMEM((8, 384), f32), pltpu.VMEM((8, 128), f32)]),
+            scratch_shapes=[pltpu.VMEM((384, width), f32), pltpu.VMEM((8, 384), f32)]),
         out_shape=[jax.ShapeDtypeStruct((width, 384), bf16), jax.ShapeDtypeStruct((8, 384), f32)],
         compiler_params=pltpu.CompilerParams(vmem_limit_bytes=40 << 20), name="head_grads",
-    )(core, gathered, dq_own, dq_sh, dkv_own, dkv_sh)
-
-
-def token_grad_kernel(dqo_ref, dqs_ref, dko_ref, dks_ref, w_ref, resid_ref, out_ref):
+        cost_estimate=cost(seqs * owners * local * 768 * width, gathered.size * 2),
+    )(core, gathered, dqkv_own, dq_sh, dkv_sh)
+
+
+def token_grad_kernel(own_ref, dqs_ref, dks_ref, w_ref, resid_ref, out_ref):
     total = resid_ref[...]
-    made = [[part for p in range(4) for part in (dqo_ref[p, 0], dqs_ref[p, 0], dqo_ref[p, 1])]]
-    for kind in range(2):
-        made.append([part for p in range(4) for part in (
-            dko_ref[p, 0, kind],
-            (dks_ref[p, 0, kind].astype(f32) + dks_ref[p, 1, kind].astype(f32)).astype(bf16),
-            dko_ref[p, 1, kind])])
     for kind in range(3):
-        total = total + dg(jnp.concatenate(made[kind], axis=0), weight_part(w_ref, 96 * kind, 96), 0, 1)
+        made = jnp.concatenate([part for p in range(4) for part in (
+            own_ref[p, 0, kind], dqs_ref[p, 0] if kind == 0 else dks_ref[p, kind - 1], own_ref[p, 1, kind])], axis=0)
+        total = total + dg(made, weight_part(w_ref, 96 * kind, 96), 0, 1)
     out_ref[...] = total.astype(bf16)
 
 
-def token_grad(dq_own, dq_sh, dkv_own, dkv_sh, weights, resid):
+def token_grad(own, dq_sh, dkv_sh, weights, resid):
     local, width = resid.shape
     steps = local // RB
     half_steps = steps // 2
     rows = pl.BlockSpec((RB, width), lambda r: (r, 0))
-    pair = pl.BlockSpec((4, 2, 2, HD, RB), lambda r: (0, 0, 0, 0, r))
     return pl.pallas_call(
         token_grad_kernel, grid=(steps,),
         in_specs=[
+            pl.BlockSpec((4, 2, 3, HD, RB), lambda r: (0, 0, 0, 0, r)),
+            pl.BlockSpec((4, 1, HD, RB), lambda r: (0, r // half_steps, 0, r % half_steps)),
             pl.BlockSpec((4, 2, HD, RB), lambda r: (0, 0, 0, r)),
-            pl.BlockSpec((4, 1, HD, RB), lambda r: (0, r // half_steps, 0, r % half_steps)),
-            pair, pair, pl.BlockSpec(weights.shape, lambda r: (0, 0, 0)), rows],
+            pl.BlockSpec(weights.shape, lambda r: (0, 0, 0)), rows],
         out_specs=rows, out_shape=jax.ShapeDtypeStruct((local, width), bf16),
         compiler_params=pltpu.CompilerParams(vmem_limit_bytes=40 << 20), name="token_grad",
-    )(dq_own, dq_sh, dkv_own, dkv_sh, weights, resid)
+        cost_estimate=cost(local * width * width * 6, local * width * 12),
+    )(own, dq_sh, dkv_sh, weights, resid)
 
 
 PAIR = ("x", "y", "c")
@@ -660,7 +649,6 @@
         axis=0).astype(f32)
     back_pack = jnp.concatenate([w_query, w_key, w_value, jnp.zeros((32, width), bf16)], axis=0)
     back_all = lax.all_gather(quarter(back_pack), ALL, axis=0, tiled=True).reshape(shards, 3 * per + 32, width)
-    back_weights = canonical_heads(back_all, shards)
 
     group = lax.axis_index("z")
     slots = lax.dynamic_slice_in_dim(deal_order, group * 2, 2)
@@ -668,7 +656,6 @@
     lens = jnp.sum(jnp.where(matches, lengths[None, :], 0), axis=1).astype(jnp.int32)
 
     q, k, v, sizes = project(gathered, head_weight, bias_row, lens)
-    own, sh, lse = attend_forward(q, k, v, sizes, lens, core)
 
     def swap(array):
         flat = array.reshape((8,) + array.shape[2:])
@@ -680,31 +667,48 @@
     def to_heads(array):
         return swap(array).reshape((2, 4) + array.shape[2:])
 
-    own_t, sh_t = to_tokens(own), to_tokens(sh)
+    own, lse_own = attend_forward(False, q, k, v, sizes, lens, core)
+    own_t = to_tokens(own)
+    own, later_core = lax.optimization_barrier((own, core))
+    sh, lse_sh = attend_forward(True, q, k, v, sizes, lens, later_core)
+    sh_sent, own_t = lax.optimization_barrier((sh, own_t))
+    sh_t = to_tokens(sh_sent)
     at = jnp.stack([x, y * 2 + c]).astype(jnp.int32)
     (act, resid, g_own, g_sh, active, d_inner, normed, d_outer, d_branch, vec_sums, bin_sums) = feed_forward(
         gathered, own_t, sh_t, cotangent.reshape(-1, width), layer_weights, inner_bias, vector_rows, at)
     g_own_h, g_sh_h = to_heads(g_own), to_heads(g_sh)
+    active, back_all = lax.optimization_barrier((active, back_all))
     packed = weight_grads(scale, active, d_outer, normed, d_inner, own_t, sh_t, d_branch)
     sums = jnp.concatenate([bin_sums.reshape(4, width), vec_sums, jnp.zeros((20, width), f32)], axis=0) * scale
     packed = packed.at[:, 864:].set(jnp.broadcast_to(sums.astype(bf16)[None], (8, 32, width)))
     ready = from_canonical(packed, shards)
     if shards != 8:
         ready = ready.at[:, 9 * per:].set(jnp.broadcast_to(sums.astype(bf16)[None], (shards, 32, width)))
+    ready, g_own_h = lax.optimization_barrier((ready, g_own_h))
+    back_weights = canonical_heads(back_all, shards)
     layer_part = lax.psum_scatter(ready.reshape(-1, width), ALL, scatter_dimension=0, tiled=True)
-    layer_grads = lax.all_gather(layer_part, ("y", "c"), axis=0, tiled=True)
-
-    dq_own, dq_sh, dkv_own, dkv_sh = attend_backward(q, k, v, lse, own, sh, g_own_h, g_sh_h, lens, core)
-    back = (to_tokens(dq_own), to_tokens(dq_sh), to_tokens(dkv_own), to_tokens(dkv_sh))
-    d_heads, d_bias = head_grads(scale, gathered, dq_own, dq_sh, dkv_own, dkv_sh, core)
+
+    dqkv_own, = attend_backward(False, q, k, v, lse_own, own, g_own_h, lens, core)
+    back_own = to_tokens(dqkv_own)
+    dqkv_own, later_core = lax.optimization_barrier((dqkv_own, core))
+    dq_sh, dkv_sh = attend_backward(True, q, k, v, lse_sh, sh, g_sh_h, lens, later_core)
+    dq_sent, back_own = lax.optimization_barrier((dq_sh, back_own))
+    back_q = to_tokens(dq_sent)
+    kept = lax.dynamic_index_in_dim(dkv_sh, c, axis=0, keepdims=False)
+    given = lax.dynamic_index_in_dim(dkv_sh, 1 - c, axis=0, keepdims=False)
+    taken = lax.ppermute(given, "c", [(0, 1), (1, 0)])
+    back_kv = to_tokens((kept.astype(f32) + taken.astype(f32)).astype(bf16))
+    d_heads, d_bias = head_grads(scale, gathered, dqkv_own, dq_sh, dkv_sh, core)
     chunk = width // zs
     head_ready = jnp.concatenate([
         d_heads.reshape(zs, chunk, 384),
         jnp.broadcast_to(d_bias[:1].astype(bf16)[None], (zs, 16, 384))], axis=1)
+    head_ready, layer_part = lax.optimization_barrier((head_ready, layer_part))
     head_part = lax.psum_scatter(head_ready.reshape(-1, 384), "z", scatter_dimension=0, tiled=True)
     head_grads_all = lax.all_gather(head_part, PAIR, axis=0, tiled=False).reshape(4, 2, chunk + 16, 6, HD).astype(f32)
 
-    d_rows = token_grad(*back, back_weights, resid)
+    layer_grads = lax.all_gather(layer_part, ("y", "c"), axis=0, tiled=True)
+    d_rows = token_grad(back_own, back_q, back_kv, back_weights, resid)
     returned = lax.all_to_all(
         d_rows.reshape(shards, stretch, width), SHARD, split_axis=0, concat_axis=0, tiled=True)
     d_tokens = jnp.zeros_like(returned).at[deal_order].set(returned)[:, None]

time: 830 us -> 680 us (0.82)
  blocking collectives: 170 us -> 59.8 us
  waiting for transfers between devices: 250 us -> 192 us
  starting transfers between devices: 14.3 us -> 33.3 us
    all_to_all x6 -> x0, blocking collectives: 110 us -> none  [swap(): return lax.all_to_all(flat, PAIR, split_axis=0, concat_axis=0, tiled=True)]
    reduce_scatter x1, waiting for transfers between devices: 38.9 us -> 0.02 us  [body(): lax.psum_scatter(head_ready.reshape(-1, 384), 'z', scatter_dimension=0, t...]
    all_to_all x1, waiting for transfers between devices: 0.01 us -> 35.7 us  [body(): lax.all_to_all(d_rows.reshape(shards, stretch, width), SHARD, split_axis=...]
    reduce_scatter x1, waiting for transfers between devices: 110 us -> 79.8 us  [body(): lax.psum_scatter(ready.reshape(-1, width), ALL, scatter_dimension=0, tile...]
    all_to_all x2 -> x7, starting transfers between devices: 7.92 us -> 27.6 us  [swap(): return lax.all_to_all(flat, PAIR, split_axis=0, concat_axis=0, tiled=True)]
    all_to_all x2 -> x7, waiting for transfers between devices: 35.5 us -> 17.3 us  [swap(): return lax.all_to_all(flat, PAIR, split_axis=0, concat_axis=0, tiled=True)]
    unnamed x108 -> x100, local copies, waits for them, and re-layouts: 32.2 us -> 25.7 us
    pallas_call x2 -> x4, Pallas kernels: 194 us -> 198 us  [the longest x2 107 us: attend_forward(): pl.pallas_call(functools.partial(fwd_kernel, shared), grid_spec=pltpu.Pre...]
  transfers between devices with their start and end apart: 11 -> 17, of which waited for: 6 -> 5; matrix products, arithmetic and copies ran while one was open for 6% -> 6% of each run, Pallas kernels for 17% -> 43%
where the time goes in v2:
time: 680 us; the launch traced here: 682 us
  Pallas kernels  295 us (43%)
  waiting for transfers between devices  192 us (28%)
  local copies, waits for them, and re-layouts  75.1 us (11%)
  blocking collectives  59.8 us (9%)
  starting transfers between devices  33.3 us (5%)
  between operations  15.7 us (2%)
  other arithmetic  10.6 us (2%)
    pallas_call x2, Pallas kernels, attend_forward(): pl.pallas_call(functools.partial(fwd_kernel, shared), grid_spec=pltpu.Pre...  107 us
    pallas_call x2, Pallas kernels, attend_backward(): pl.pallas_call(functools.partial(bwd_kernel, shared), grid_spec=pltpu.Pre...  90.9 us
    reduce_scatter x1, waiting for transfers between devices, body(): lax.psum_scatter(ready.reshape(-1, width), ALL, scatter_dimension=0, tile...  79.8 us
    all_to_all x1, blocking collectives, body(): lax.all_to_all(ordered, 'z', split_axis=0, concat_axis=0, tiled=True)  59.8 us
    all_gather x1, waiting for transfers between devices, body(): lax.all_gather(spread, PAIR, axis=0, tiled=False)  57.7 us
    pallas_call x1, Pallas kernels, feed_forward(): pl.pallas_call(functools.partial(ffn_kernel, spans), grid_spec=pltpu.Pref...  41.2 us
    all_to_all x1, waiting for transfers between devices, body(): lax.all_to_all(d_rows.reshape(shards, stretch, width), SHARD, split_axis=...  35.7 us
    all_to_all x7, starting transfers between devices, swap(): return lax.all_to_all(flat, PAIR, split_axis=0, concat_axis=0, tiled=True)  27.6 us
  transfers between devices with their start and end apart: 17, of which 5 were waited for; matrix products, arithmetic and copies ran while one was open for 6% of the time, Pallas kernels for 43%

profile of v2, /device:TPU:0, one launch (start us, length us, event | category | flops | bytes accessed | tf_op | source)
XLA Modules:
  0.0 681.7 jit_solution(5719447733037296926)
XLA Ops:
  7.3 1.2 copy.116
  13.0 59.8 %all_to_all.45 = bf16[4,2,128,768]{3,2,1,0:T(8,128)(2,1)} all-to-all(bf16[4,2,128,768]{3,2,1,0:T(8,128)(2,1)S(1)} %broadcast_select_fusion), channel_id=1, replica_groups=mesh['z'=4,'x'=2,'y'=2,'c'=2] {'z'}, dimensions={0} | all-to-all | bytes 3145728 | tf_op jit(solution)/shard_map/all_to_all | solution.py:615
  78.6 2.5 slice.275
  82.4 2.8 reshape.322
  85.2 1.2 constant_dynamic-slice_fusion.11
  86.5 57.7 %all-gather.16.cloned.1.call-done = bf16[32,2,128,768]{3,2,1,0:T(8,128)(2,1)} async-done(((bf16[4,2,128,768]{3,2,1,0:T(8,128)(2,1)}), bf16[32,2,128,768]{3,2,1,0:T(8,128)(2,1)}) %all-gather.16.cloned.1.call-update) | async-done | bytes 12582928 | tf_op jit(solution)/shard_map/all_gather | solution.py:637
  144.2 17.3 %qkv.1 = (bf16[2,2,4,64,1024]{4,3,2,1,0:T(8,128)(2,1)S(1)}, bf16[2,2,8,512,128]{4,3,2,1,0:T(8,128)(2,1)S(1)}, bf16[2,2,8,128,512]{4,3,2,1,0:T(8,128)(2,1)S(1)}, f32[2,4,2,1,128]{4,3,2,1,0:T(1,128)S(1)}) custom-call(s32[2]{0:T(128)S(1)} %fusion.9.len_ref, bf16[2,4,4,2,128,768]{5,4,3,2,1,0:T(8,128)(2,1)} %bitcast.148, bf16[768,384]{1,0:T(8,128)(2,1)S(1)} %bitcast.143, ...), custom_call_target="tpu_custom_call" | custom-call | flops 4831838208 | bytes 25165824 | tf_op jit(solution)/shard_map/qkv/pallas_call | solution.py:74
  161.5 1.9 copy-done.3
  163.5 1.9 copy-done.4
  165.4 70.3 %attend_forward_own.1 = (bf16[2,4,64,1024]{3,2,1,0:T(8,128)(2,1)}, f32[2,4,1,1024]{3,2,1,0:T(1,128)S(1)}) custom-call(s32[2]{0:T(128)S(1)} %fusion.9.len_ref, s32[1]{0:T(128)} %bitcast.5.core_ref, bf16[2,2,4,64,1024]{4,3,2,1,0:T(8,128)(2,1)S(1)} %get-tuple-element.66.q_ref, bf16[2,2,8,512,128]{4,3,2,1,0:T(8,128)(2,1)} %copy-done.3, ...), custom_call_target="tpu_custom_call" | custom-call | flops 20615843840 | bytes 4194304 | tf_op jit(solution)/shard_map/attend_forward_own/pallas_call | solution.py:197
  235.7 3.6 all-to-all-start.1
  239.3 1.6 copy-done.6
  240.8 37.0 %attend_forward_shared.1 = (bf16[2,4,64,512]{3,2,1,0:T(8,128)(2,1)}, f32[2,2,1,1024]{3,2,1,0:T(1,128)S(1)}) custom-call(s32[2]{0:T(128)S(1)} %fusion.9.len_ref, s32[1]{0:T(128)} %bitcast.5.core_ref, bf16[2,2,4,64,1024]{4,3,2,1,0:T(8,128)(2,1)S(1)} %copy-done.6, bf16[2,2,8,512,128]{4,3,2,1,0:T(8,128)(2,1)} %copy-done.3, ...), custom_call_target="tpu_custom_call" | custom-call | flops 10307921920 | bytes 4194304 | tf_op jit(solution)/shard_map/attend_forward_shared/pallas_call | solution.py:197
  277.9 4.3 all-to-all-start.2
  283.7 1.2 slice_reduce_fusion
  286.7 9.3 %all-to-all-done.2 = bf16[8,64,512]{2,1,0:T(8,128)(2,1)S(1)} async-done(((bf16[8,64,512]{2,1,0:T(8,128)(2,1)}), bf16[8,64,512]{2,1,0:T(8,128)(2,1)S(1)}, u32[]{:S(2)}, u32[]{:S(2)}) %all-to-all-start.2) | async-done | bytes 524320 | tf_op jit(solution)/shard_map/all_to_all | solution.py:662
  296.8 41.2 %feed_forward.1 = (bf16[1024,768]{1,0:T(8,128)(2,1)}, f32[1024,768]{1,0:T(8,128)}, bf16[4,2,64,1024]{3,2,1,0:T(8,128)(2,1)}, bf16[4,2,64,512]{3,2,1,0:T(8,128)(2...) custom-call(s32[2]{0:T(128)} %pad_add_fusion.at_ref, ...), custom_call_target="tpu_custom_call" | custom-call | flops 21743271936 | bytes 62914560 | tf_op jit(solution)/shard_map/feed_forward/pallas_call | solution.py:421
  338.6 1.4 reduce.23
  340.0 3.6 all-to-all-start.3
  343.7 2.8 copy-done.8
  346.5 7.3 %outer_grad.1.packed_ref = bf16[8,896,768]{2,1,0:T(8,128)(2,1)} custom-call(bf16[1024,3072]{1,0:T(8,128)(2,1)S(1)} %copy-done.8, bf16[1024,768]{1,0:T(8,128)(2,1)S(1)} %copy-done.16), custom_call_target="tpu_custom_call" | custom-call | flops 4831838208 | bytes 11010048 | tf_op jit(solution)/shard_map/outer_grad/pallas_call | solution.py:470
  353.9 8.7 %inner_grad.1 = bf16[8,896,768]{2,1,0:T(8,128)(2,1)} custom-call(bf16[8,896,768]{2,1,0:T(8,128)(2,1)} %outer_grad.1.packed_ref, bf16[1024,768]{1,0:T(8,128)(2,1)S(1)} %copy-done.14, bf16[1024,3072]{1,0:T(8,128)(2,1)S(1)} %copy-done.9, bf16[4,2,64,1024]{3,2,1,0:T(8,128)(2,1)S(1)} %bitcast.139, ...), custom_call_target="tpu_custom_call", output_to_operand_aliasing={{}: (0, {})} | custom-call | flops 6039797760 | bytes 13762560 | tf_op jit(solution)/shard_map/inner_grad/pallas_call | solution.py:479
  364.4 4.3 all-to-all-start.4
  368.7 58.9 %attend_backward_own.1.own_ref = bf16[2,4,3,64,1024]{4,3,2,1,0:T(8,128)(2,1)} custom-call(s32[2]{0:T(128)} %copy-done.19, s32[1]{0:T(128)} %bitcast.5.core_ref, bf16[2,2,4,64,1024]{4,3,2,1,0:T(8,128)(2,1)} %copy-done.5, bf16[2,2,8,512,128]{4,3,2,1,0:T(8,128)(2,1)} %copy-done.3, bf16[2,2,8,128,512]{4,3,2,1,0:T(8,128)(2,1)} %copy-done.4, ...), custom_call_target="tpu_custom_call" | custom-call | flops 2013265920 | bytes 16777216 | tf_op jit(solution)/shard_map/attend_backward_own/pallas_call | solution.py:301
  428.3 4.5 all-to-all-start.5
  432.8 32.0 %attend_backward_shared.1 = (bf16[2,4,64,512]{3,2,1,0:T(8,128)(2,1)}, bf16[2,2,4,64,1024]{4,3,2,1,0:T(8,128)(2,1)}) custom-call(s32[2]{0:T(128)} %copy-done.19, s32[1]{0:T(128)} %bitcast.5.core_ref, bf16[2,2,4,64,1024]{4,3,2,1,0:T(8,128)(2,1)} %copy-done.5, bf16[2,2,8,512,128]{4,3,2,1,0:T(8,128)(2,1)} %copy-done.3, bf16[2,2,8,128,512]{4,3,2,1,0:T(8,128)(2,1)} %copy-done.4, ...), custom_call_target="tpu_custom_call" | custom-call | flops 1006632960 | bytes 16777216 | tf_op jit(solution)/shard_map/attend_backward_shared/pallas_call | solution.py:301
  464.8 1.3 dynamic-slice_bitcast_fusion
  466.7 1.9 copy-done.2
  468.6 1.6 copy-done.7
  470.2 16.1 %head_grads.1 = (bf16[768,384]{1,0:T(8,128)(2,1)S(1)}, f32[8,384]{1,0:T(8,128)S(1)}) custom-call(s32[1]{0:T(128)} %bitcast.5.core_ref, bf16[2,4,4,2,128,768]{5,4,3,2,1,0:T(8,128)(2,1)} %bitcast.150, bf16[2,4,3,64,1024]{4,3,2,1,0:T(8,128)(2,1)S(1)} %copy-done.2, bf16[2,4,64,512]{3,2,1,0:T(8,128)(2,1)} %get-tuple-element.93.dqs_ref, ...), custom_call_target="tpu_custom_call" | custom-call | flops 4831838208 | bytes 12582912 | tf_op jit(solution)/shard_map/head_grads/pallas_call | solution.py:517
  486.4 2.6 fusion
  489.0 3.9 all-to-all-start.7
  493.8 79.8 %reduce-scatter.3.cloned.1.call-done = bf16[224,768]{1,0:T(8,128)(2,1)} async-done(((bf16[7168,768]{1,0:T(8,128)(2,1)}), bf16[224,768]{1,0:T(8,128)(2,1)}) %reduce-scatter.3.cloned.1.call-update) | async-done | bytes 344080 | tf_op jit(solution)/shard_map/reduce_scatter | solution.py:689
  573.7 3.5 all-to-all-start.6
  578.0 8.0 %all-to-all-done.6 = bf16[8,64,512]{2,1,0:T(8,128)(2,1)S(1)} async-done(((bf16[8,64,512]{2,1,0:T(8,128)(2,1)}), bf16[8,64,512]{2,1,0:T(8,128)(2,1)S(1)}, u32[]{:S(2)}, u32[]{:S(2)}) %all-to-all-start.6) | async-done | bytes 524320 | tf_op jit(solution)/shard_map/all_to_all | solution.py:662
  586.0 2.1 copy-done.20
  588.1 1.9 copy-done.21
  590.0 6.7 token_grad.1
  596.7 4.5 all-to-all-start.8
  602.0 35.7 %all-to-all-done.8 = bf16[8,128,768]{2,1,0:T(8,128)(2,1)S(1)} async-done(((bf16[8,128,768]{2,1,0:T(8,128)(2,1)}), bf16[8,128,768]{2,1,0:T(8,128)(2,1)S(1)}, u32[]{:S(2)}, u32[]{:S(2)}) %all-to-all-start.8) | async-done | bytes 1572896 | tf_op jit(solution)/shard_map/all_to_all | solution.py:712
  637.8 1.1 scatter_fusion
  639.0 3.0 fusion.20
  642.0 1.1 copy.141
  644.5 1.6 slice.302
  650.5 2.9 copy.122
  653.4 7.7 %reshape.354 = f32[4,2,208,6,64]{2,1,0,4,3:T(2,128)} reshape(f32[1664,384]{0,1:T(8,128)} %copy.122) | data formatting | bytes 5111808 | tf_op jit(solution)/shard_map/convert_element_type | solution.py:708
  661.0 2.3 fusion.18
  665.4 3.5 dynamic-slice_bitcast_fusion.1
  (231 shorter events, 34.8 us)
Async XLA Ops:
  7.2 4.9 copy-start
  7.2 3.7 copy-start.33
  7.2 3.8 copy-start.34
  7.2 4.7 copy-start.41
  7.2 71.4 %all-gather.18.cloned.1.call-start = ((), (), s32[]{:S(2)}) async-start(), calls=%async_computation.17 | async-start | bytes 1548288 | tf_op jit(solution)/shard_map/all_gather | solution.py:627
  11.9 132.3 %all-gather.16.cloned.1.call-start = ((), (), s32[]{:S(2)}) async-start(), calls=%async_computation.16 | async-start | bytes 14155776 | tf_op jit(solution)/shard_map/all_gather | solution.py:637
  72.8 1.6 copy-start.38
  72.8 1.6 copy-start.39
  72.8 1.7 copy-start.40
  72.8 210.1 %all-gather.10.cloned.1.call-start = ((), (), s32[]{:S(2)}) async-start(), calls=%async_computation.11 | async-start | bytes 11354112 | tf_op jit(solution)/shard_map/all_gather | solution.py:644
  75.6 1.9 copy-start.27
  75.6 1.9 copy-start.28
  75.6 1.9 copy-start.29
  76.5 1.9 copy-start.42
  77.3 262.7 %all-gather.12.cloned.1.call-start = ((), (), s32[]{:S(2)}) async-start(), calls=%async_computation.12 | async-start | bytes 4055040 | tf_op jit(solution)/shard_map/all_gather | solution.py:651
  78.6 160.7 %copy-start.19 = (s32[2]{0:T(128)}, s32[2]{0:T(128)S(1)}, u32[]{:S(2)}) copy-start(s32[2]{0:T(128)S(1)} %fusion.9.len_ref) | copy-start | bytes 28
  161.5 2.0 copy-start.3
  163.5 1.9 copy-start.4
  165.4 70.3 %copy-start.5 = (bf16[2,2,4,64,1024]{4,3,2,1,0:T(8,128)(2,1)}, bf16[2,2,4,64,1024]{4,3,2,1,0:T(8,128)(2,1)S(1)}, u32[]{:S(2)}) copy-start(bf16[2,2,4,64,1024]{4,3,2,1,0:T(8,128)(2,1)S(1)} %get-tuple-element.66.q_ref) | copy-start | bytes 6291460
  235.7 42.2 %copy-start.17 = (f32[2,4,1,1024]{3,2,1,0:T(1,128)}, f32[2,4,1,1024]{3,2,1,0:T(1,128)S(1)}, u32[]{:S(2)}) copy-start(f32[2,4,1,1024]{3,2,1,0:T(1,128)S(1)} %get-tuple-element.76.lse_ref) | copy-start | bytes 98308
  235.7 42.2 %all-to-all-start.1 = ((bf16[8,64,1024]{2,1,0:T(8,128)(2,1)}), bf16[8,64,1024]{2,1,0:T(8,128)(2,1)S(1)}, u32[]{:S(2)}, u32[]{:S(2)}) async-start(bf16[8,64,1024]{2,1,0:T(8,128)(2,1)} %bitcast.24), calls=%async_computation.1 | async-start | bytes 2097152 | tf_op jit(solution)/shard_map/all_to_all | solution.py:662
  277.9 18.1 %copy-start.18 = (f32[2,2,1,1024]{3,2,1,0:T(1,128)}, f32[2,2,1,1024]{3,2,1,0:T(1,128)S(1)}, u32[]{:S(2)}) copy-start(f32[2,2,1,1024]{3,2,1,0:T(1,128)S(1)} %get-tuple-element.89.lse_ref) | copy-start | bytes 49156
  277.9 18.1 %copy-start.10 = (bf16[8,64,1024]{2,1,0:T(8,128)(2,1)}, bf16[8,64,1024]{2,1,0:T(8,128)(2,1)S(1)}, u32[]{:S(2)}) copy-start(bf16[8,64,1024]{2,1,0:T(8,128)(2,1)S(1)} %all-to-all-done.1) | copy-start | bytes 3145732
  277.9 18.1 %all-to-all-start.2 = ((bf16[8,64,512]{2,1,0:T(8,128)(2,1)}), bf16[8,64,512]{2,1,0:T(8,128)(2,1)S(1)}, u32[]{:S(2)}, u32[]{:S(2)}) async-start(bf16[8,64,512]{2,1,0:T(8,128)(2,1)} %bitcast.26), calls=%async_computation.2 | async-start | bytes 1048576 | tf_op jit(solution)/shard_map/all_to_all | solution.py:662
  338.1 5.6 copy-start.16
  340.0 23.4 %all-to-all-start.3 = ((bf16[8,64,1024]{2,1,0:T(8,128)(2,1)}), bf16[8,64,1024]{2,1,0:T(8,128)(2,1)S(1)}, u32[]{:S(2)}, u32[]{:S(2)}) async-start(bf16[8,64,1024]{2,1,0:T(8,128)(2,1)} %bitcast.161), calls=%async_computation.3 | async-start | bytes 2097152 | tf_op jit(solution)/shard_map/all_to_all | solution.py:662
  343.6 230.1 %reduce-scatter.3.cloned.1.call-start = ((), (), s32[]{:S(2)}) async-start(), calls=%async_computation.13 | async-start | bytes 11354112 | tf_op jit(solution)/shard_map/reduce_scatter | solution.py:689
  343.6 2.8 copy-start.8
  346.4 7.3 %copy-start.31 = (f32[8,768]{1,0:T(8,128)S(1)}, f32[8,768]{1,0:T(8,128)}, u32[]{:S(2)}) copy-start(f32[8,768]{1,0:T(8,128)} %get-tuple-element.85) | copy-start | bytes 73732
  346.4 7.4 %copy-start.9 = (bf16[1024,3072]{1,0:T(8,128)(2,1)S(1)}, bf16[1024,3072]{1,0:T(8,128)(2,1)}, u32[]{:S(2)}) copy-start(bf16[1024,3072]{1,0:T(8,128)(2,1)} %get-tuple-element.82.dinner_ref) | copy-start | bytes 18874372
  346.4 7.4 %copy-start.11 = (bf16[8,64,1024]{2,1,0:T(8,128)(2,1)S(1)}, bf16[8,64,1024]{2,1,0:T(8,128)(2,1)}, u32[]{:S(2)}) copy-start(bf16[8,64,1024]{2,1,0:T(8,128)(2,1)} %copy-done.10) | copy-start | bytes 3145732
  346.4 7.4 %copy-start.13 = (bf16[8,64,512]{2,1,0:T(8,128)(2,1)S(1)}, bf16[8,64,512]{2,1,0:T(8,128)(2,1)}, u32[]{:S(2)}) copy-start(bf16[8,64,512]{2,1,0:T(8,128)(2,1)} %copy-done.12) | copy-start | bytes 1572868
  346.4 7.4 %copy-start.14 = (bf16[1024,768]{1,0:T(8,128)(2,1)S(1)}, bf16[1024,768]{1,0:T(8,128)(2,1)}, u32[]{:S(2)}) copy-start(bf16[1024,768]{1,0:T(8,128)(2,1)} %get-tuple-element.81.normed_ref) | copy-start | bytes 4718596
  346.5 7.4 %copy-start.15 = (bf16[1024,768]{1,0:T(8,128)(2,1)S(1)}, bf16[1024,768]{1,0:T(8,128)(2,1)}, u32[]{:S(2)}) copy-start(bf16[1024,768]{1,0:T(8,128)(2,1)} %get-tuple-element.83.dbranch_ref) | copy-start | bytes 4718596
  364.4 63.2 %all-to-all-start.4 = ((bf16[8,64,512]{2,1,0:T(8,128)(2,1)}), bf16[8,64,512]{2,1,0:T(8,128)(2,1)S(1)}, u32[]{:S(2)}, u32[]{:S(2)}) async-start(bf16[8,64,512]{2,1,0:T(8,128)(2,1)} %bitcast.35), calls=%async_computation.4 | async-start | bytes 1048576 | tf_op jit(solution)/shard_map/all_to_all | solution.py:662
  428.3 60.6 %all-to-all-start.5 = ((bf16[8,3,64,1024]{3,2,1,0:T(8,128)(2,1)}), bf16[8,3,64,1024]{3,2,1,0:T(8,128)(2,1)}, u32[]{:S(2)}, u32[]{:S(2)}) async-start(bf16[8,3,64,1024]{3,2,1,0:T(8,128)(2,1)} %bitcast.137), calls=%async_computation.5 | async-start | bytes 6291456 | tf_op jit(solution)/shard_map/all_to_all | solution.py:662
  466.2 20.2 %collective-permute-start = (bf16[2,4,64,1024]{3,2,1,0:T(8,128)(2,1)S(1)}, bf16[2,4,64,1024]{3,2,1,0:T(8,128)(2,1)}, u32[]{:S(2)}, u32[]{:S(2)}) collective-permute-start(bf16[2,4,64,1024]{3,2,1,0:T(8,128)(2,1)S(1)} %dynamic-slice_bitcast_fusion), channel_id=1, source_target_pairs={{0,1},{1,0},{2,3},{3,2},{4,5},{5,4},{6,7},{7,6},{8,9},{9,8},{10,11... | collective-permute-start | bytes 3145736 | tf_op jit(solution)/shard_map/ppermute | solution.py:699
  466.7 1.9 copy-start.2
  489.0 84.7 %all-to-all-start.7 = ((bf16[8,64,1024]{2,1,0:T(8,128)(2,1)}), bf16[8,64,1024]{2,1,0:T(8,128)(2,1)S(1)}, u32[]{:S(2)}, u32[]{:S(2)}) async-start(bf16[8,64,1024]{2,1,0:T(8,128)(2,1)} %bitcast.43), calls=%async_computation.7 | async-start | bytes 2097152 | tf_op jit(solution)/shard_map/all_to_all | solution.py:662
  492.9 108.6 %reduce-scatter.5.cloned.1.call-start = ((), (), s32[]{:S(2)}) async-start(), calls=%async_computation.14 | async-start | bytes 798720 | tf_op jit(solution)/shard_map/reduce_scatter | solution.py:707
  573.7 12.3 %all-to-all-start.6 = ((bf16[8,64,512]{2,1,0:T(8,128)(2,1)}), bf16[8,64,512]{2,1,0:T(8,128)(2,1)S(1)}, u32[]{:S(2)}, u32[]{:S(2)}) async-start(bf16[8,64,512]{2,1,0:T(8,128)(2,1)} %bitcast.39), calls=%async_computation.6 | async-start | bytes 1048576 | tf_op jit(solution)/shard_map/all_to_all | solution.py:662
  577.2 61.7 %all-gather.14.cloned.1.call-start = ((), (), s32[]{:S(2)}) async-start(), calls=%async_computation.15 | async-start | bytes 1720320 | tf_op jit(solution)/shard_map/all_gather | solution.py:710
  586.0 2.1 copy-start.20
  588.1 1.9 copy-start.21
  596.7 41.0 %all-to-all-start.8 = ((bf16[8,128,768]{2,1,0:T(8,128)(2,1)}), bf16[8,128,768]{2,1,0:T(8,128)(2,1)S(1)}, u32[]{:S(2)}, u32[]{:S(2)}) async-start(bf16[8,128,768]{2,1,0:T(8,128)(2,1)} %bitcast.45), calls=%async_computation.8 | async-start | bytes 3145728 | tf_op jit(solution)/shard_map/all_to_all | solution.py:712
  601.2 49.3 %all-gather.20.cloned.1.call-start = ((), (), s32[]{:S(2)}) async-start(), calls=%async_computation.18 | async-start | bytes 1437696 | tf_op jit(solution)/shard_map/all_gather | solution.py:708
  638.9 3.0 copy-start.22
  672.6 1.8 copy-start.1
  (12 other events, 15.2 us)
Sparse Core Ops, SparseCore 0:
  12.0 57.6 all-gather.17
  72.9 71.2 all-gather.15
  147.7 89.0 all-gather.9
  240.2 65.1 all-gather.11
  363.5 210.0 reduce-scatter.2
  576.4 21.3 reduce-scatter.4
  599.3 17.2 all-gather.13
  618.5 28.6 all-gather.19

commit v3 on v2

--- a/solution.py
+++ b/solution.py
@@ -33,69 +33,92 @@
     return jnp.concatenate([top.astype(f32), tail], axis=0)
 
 
-def qkv_kernel(stretch, spans_in, len_ref, x_ref, w_ref, b_ref, q_out, k_out, v_out, size_out):
-    seq, owner, half = pl.program_id(0), pl.program_id(1), pl.program_id(2)
-    rows = jnp.concatenate([x_ref[a, 0, z, 0] for z in range(spans_in) for a in range(2)], axis=0)
-    made = dg(rows, w_ref[...], 1, 0) + b_ref[...]
+def load_rows(rows, ref, spans, x):
+    stretch = ref.shape[3]
+    for z in range(spans):
+        for a in range(2):
+            at = (2 * z + a) * stretch
+            rows[at:at + stretch] = ref[0, a ^ x, z]
+
+
+def qkv_kernel(stretch, spans, info, near_ref, far_ref, w_ref, b_ref, q_out, k_out, v_out, size_out, rows):
+    away, half = pl.program_id(0), pl.program_id(2)
+    owner = ((pl.program_id(1) ^ info[2]) << 1) | (away ^ info[3])
+
+    @pl.when(away == 0)
+    def _():
+        load_rows(rows, near_ref, spans, info[1])
+
+    @pl.when(away == 1)
+    def _():
+        load_rows(rows, far_ref, spans, info[1])
+    made = dg(rows[...], w_ref[...], 1, 0) + b_ref[...]
     count = rows.shape[0]
     q_t = (made[:, :128] * (LOG2E / 8.0)).T
-    q_out[0, 0, 0] = q_t[:HD].astype(bf16)
-    q_out[0, 1, 0] = q_t[HD:].astype(bf16)
+    q_out[0, 0] = q_t[:HD].astype(bf16)
+    q_out[1, 0] = q_t[HD:].astype(bf16)
     lane = lax.broadcasted_iota(jnp.int32, (count, 128), 1)
     row = lax.broadcasted_iota(jnp.int32, (count, 128), 0) + half * count
     shift = int(math.log2(stretch))
     position = lax.shift_left(lax.shift_right_logical(row, shift), shift + 2) + owner * stretch + (row & (stretch - 1))
-    hidden = jnp.where(position < len_ref[seq], 0.0, FAR)
+    hidden = jnp.where(position < info[0], 0.0, FAR)
     tail = jnp.where(lane == HD + 3, hidden, jnp.where(lane < HD + 3, 1.0, 0.0))
     keys = made[:, 128:256]
     picks = lax.broadcasted_iota(jnp.int32, (128, 128), 0) // HD == lax.broadcasted_iota(jnp.int32, (128, 128), 1)
     sizes = dg((keys * keys).astype(bf16), jnp.where(picks, 1.0, 0.0).astype(bf16), 1, 0)
-    size_out[0, 0, 0] = jnp.max(sizes, axis=0, keepdims=True)
+    size_out[0, 0] = jnp.max(sizes, axis=0, keepdims=True)
     for head in range(2):
         turned = keys if head == 0 else pltpu.roll(keys, HD, 1)
         full = jnp.where(lane < HD, turned, tail).astype(bf16)
         for j in range(count // 128):
-            k_out[0, head, j] = full[j * 128:(j + 1) * 128]
+            k_out[head, j] = full[j * 128:(j + 1) * 128]
     v_t = made[:, 256:384].T
     ones = jnp.where(lax.broadcasted_iota(jnp.int32, (HD, count), 0) < 3, 1.0, 0.0)
     for head in range(2):
         full = jnp.concatenate([v_t[head * HD:(head + 1) * HD], ones], axis=0).astype(bf16)
         for j in range(count // 128):
-            v_out[0, head, j] = full[:, j * 128:(j + 1) * 128]
-
-
-def project(gathered, weight, bias, lens):
-    _, owners, zs, seqs, stretch, width = gathered.shape
+            v_out[head, j] = full[:, j * 128:(j + 1) * 128]
+
+
+def owner_of(away, across, info):
+    return ((across ^ info[2]) << 1) | (away ^ info[3])
+
+
+def project(near, far, weight, bias, info):
+    _, _, zs, stretch, width = near.shape
     local = 2 * zs * stretch
     spans = 512 // (2 * stretch)
     halves = local // 512
-    chunks = owners * local // CH
+    chunks = 4 * local // CH
     per = chunks // halves
+    block = (1, 2, spans, stretch, width)
     return pl.pallas_call(
         functools.partial(qkv_kernel, stretch, spans),
         grid_spec=pltpu.PrefetchScalarGridSpec(
-            num_scalar_prefetch=1, grid=(seqs, owners, halves),
+            num_scalar_prefetch=1, grid=(2, 2, halves),
             in_specs=[
-                pl.BlockSpec((2, 1, spans, 1, stretch, width), lambda s, o, h, n: (0, o, h, s, 0, 0)),
-                pl.BlockSpec((width, 384), lambda s, o, h, n: (0, 0)),
-                pl.BlockSpec((1, 384), lambda s, o, h, n: (0, 0)),
+                pl.BlockSpec(block, lambda a, o, h, n: (jnp.where(a == 0, o, 1), 0, jnp.where(a == 0, h, halves - 1), 0, 0)),
+                pl.BlockSpec(block, lambda a, o, h, n: (jnp.where(a == 0, 0, o), 0, jnp.where(a == 0, 0, h), 0, 0)),
+                pl.BlockSpec((width, 384), lambda a, o, h, n: (0, 0)),
+                pl.BlockSpec((1, 384), lambda a, o, h, n: (0, 0)),
             ],
             out_specs=[
-                pl.BlockSpec((1, 2, 1, HD, 512), lambda s, o, h, n: (s, 0, o, 0, h)),
-                pl.BlockSpec((1, 2, per, 128, 128), lambda s, o, h, n: (s, 0, h, o, 0)),
-                pl.BlockSpec((1, 2, per, 128, 128), lambda s, o, h, n: (s, 0, h, 0, o)),
-                pl.BlockSpec((1, 1, 1, 1, 128), lambda s, o, h, n: (s, o, h, 0, 0)),
-            ]),
+                pl.BlockSpec((2, 1, HD, 512), lambda a, o, h, n: (0, owner_of(a, o, n), 0, h)),
+                pl.BlockSpec((2, per, 128, 128), lambda a, o, h, n: (0, h, owner_of(a, o, n), 0)),
+                pl.BlockSpec((2, per, 128, 128), lambda a, o, h, n: (0, h, 0, owner_of(a, o, n))),
+                pl.BlockSpec((1, 1, 1, 128), lambda a, o, h, n: (owner_of(a, o, n), h, 0, 0)),
+            ],
+            scratch_shapes=[pltpu.VMEM((512, width), bf16)]),
         out_shape=[
-            jax.ShapeDtypeStruct((seqs, 2, owners, HD, local), bf16),
-            jax.ShapeDtypeStruct((seqs, 2, chunks, CH, 128), bf16),
-            jax.ShapeDtypeStruct((seqs, 2, chunks, 128, CH), bf16),
-            jax.ShapeDtypeStruct((seqs, owners, halves, 1, 128), f32),
+            jax.ShapeDtypeStruct((2, 4, HD, local), bf16),
+            jax.ShapeDtypeStruct((2, chunks, CH, 128), bf16),
+            jax.ShapeDtypeStruct((2, chunks, 128, CH), bf16),
+            jax.ShapeDtypeStruct((4, halves, 1, 128), f32),
         ],
         compiler_params=pltpu.CompilerParams(vmem_limit_bytes=40 << 20),
         name="qkv",
-        cost_estimate=cost(2 * gathered.size * 384, gathered.size * 4),
-    )(lens, gathered, weight, bias)
+        cost_estimate=cost(4 * near.size * 384, near.size * 8),
+    )(info, near, far, weight, bias)
 
 
 def step_on(q, j, count):
@@ -103,30 +126,29 @@
     return jnp.where(last, q + 1, q), jnp.where(last, 0, j + 1)
 
 
-def assemble(ref, q, head, core):
-    if not head:
-        return ref[0, 0, q]
+def assemble(ref, q, shared, core):
+    if not shared:
+        return ref[0, q]
     at = pl.multiple_of(core * 512, 512)
-    return jnp.concatenate([ref[0, 0, 2 * q, :, pl.ds(at, 512)], ref[0, 0, 2 * q + 1, :, pl.ds(at, 512)]], axis=1)
-
-
-def fwd_kernel(shared, len_ref, core_ref, q_ref, k_ref, v_ref, size_ref, out_ref, lse_ref, acc, probs, qa, shifts):
-    seq = pl.program_id(0)
-    count = lax.div(len_ref[seq] + (CH - 1), CH)
+    return jnp.concatenate([ref[0, 2 * q, :, pl.ds(at, 512)], ref[0, 2 * q + 1, :, pl.ds(at, 512)]], axis=1)
+
+
+def fwd_kernel(shared, info, q_ref, k_ref, v_ref, size_ref, held_ref, out_ref, lse_ref, acc, probs, qa, shifts):
+    count = lax.div(info[0] + (CH - 1), CH)
     parts = 2 if shared else 4
     lane = lax.broadcasted_iota(jnp.int32, (1, 128), 1)
-    sizes = functools.reduce(jnp.maximum, [size_ref[0, o, h] for o in range(size_ref.shape[1]) for h in range(size_ref.shape[2])])
+    sizes = functools.reduce(jnp.maximum, [size_ref[o, h] for o in range(size_ref.shape[0]) for h in range(size_ref.shape[1])])
     widest = jnp.sqrt(jnp.max(jnp.where(lane == int(shared), sizes, 0.0), axis=1, keepdims=True))
 
     for part in range(parts):
-        q_t = assemble(q_ref, part, shared, core_ref[0])
+        q_t = assemble(q_ref, part, shared, info[3])
         wide = q_t.astype(f32)
         shift = jnp.sqrt(jnp.sum(wide * wide, axis=0, keepdims=True)) * widest
         shifts[part] = shift
         qa[part] = with_shift(q_t, shift).astype(bf16)
 
     def raised(part, j):
-        return jnp.exp2(dg(k_ref[0, 0, j], qa[part], 1, 0)).astype(bf16)
+        return jnp.exp2(dg(k_ref[0, j], qa[part], 1, 0)).astype(bf16)
 
     probs[0] = raised(0, 0)
 
@@ -135,7 +157,7 @@
         now = t & 1
         part_next, j_next = step_on(part, j, count)
         before = jnp.where(j == 0, 0.0, acc[...])
-        acc[...] = before + dg(v_ref[0, 0, j], probs[now], 1, 0)
+        acc[...] = before + dg(v_ref[0, j], probs[now], 1, 0)
         probs[1 - now] = raised(jnp.minimum(part_next, parts - 1), j_next)
 
         @pl.when(j + 1 == count)
@@ -150,20 +172,20 @@
                 qa[part] = jnp.where((row >= HD) & (row < HD + 3), 0.0, plain).astype(bf16)
 
                 def peak(i, top):
-                    return jnp.maximum(top, jnp.max(dg(k_ref[0, 0, i], qa[part], 1, 0), axis=0, keepdims=True))
+                    return jnp.maximum(top, jnp.max(dg(k_ref[0, i], qa[part], 1, 0), axis=0, keepdims=True))
                 shift = lax.fori_loop(0, count, peak, jnp.full((1, BQ), FAR, f32))
                 shifts[part] = shift
                 qa[part] = with_shift(plain[:HD], shift).astype(bf16)
                 acc[...] = jnp.zeros_like(acc)
 
                 def again(i, carry):
-                    acc[...] += dg(v_ref[0, 0, i], raised(part, i), 1, 0)
+                    acc[...] += dg(v_ref[0, i], raised(part, i), 1, 0)
                     return carry
                 lax.fori_loop(0, count, again, 0)
 
             total = acc[HD:HD + 1]
             mixed = (acc[:HD] * (1.0 / total)).astype(bf16)
-            lse_ref[0, part] = shifts[part] + jnp.log2(total)
+            lse_ref[part] = shifts[part] + jnp.log2(total)
             if shared:
                 out_ref[0, 2 * part] = mixed[:, :512]
                 out_ref[0, 2 * part + 1] = mixed[:, 512:]
@@ -176,55 +198,58 @@
 
 def head_spec(shared, *dims):
     zeros = (0,) * len(dims)
-    return pl.BlockSpec((1, 1) + dims, lambda s, n, c: (s, int(shared)) + zeros)
-
-
-def seq_spec(*dims):
-    zeros = (0,) * len(dims)
-    return pl.BlockSpec((1,) + dims, lambda s, n, c: (s,) + zeros)
+    return pl.BlockSpec((1,) + dims, lambda i, n: (int(shared),) + zeros)
+
+
+def whole_spec(*dims):
+    return pl.BlockSpec(dims, lambda i, n: (0,) * len(dims))
 
 
 def cost(flops, moved, exps=0):
     return pl.CostEstimate(flops=int(flops), bytes_accessed=int(moved), transcendentals=int(exps))
 
 
-def attend_forward(shared, q, k, v, sizes, lens, core):
-    seqs, _, owners, _, local = q.shape
-    chunks = k.shape[2]
-    held = local // 2 if shared else local
-    parts = owners * held // BQ
-    pairs = seqs * parts * BQ * chunks * CH * 0.6
+def attend_forward(shared, seq, q, k, v, sizes, info, held):
+    _, owners, _, local = q.shape
+    chunks = k.shape[1]
+    wide = local // 2 if shared else local
+    parts = owners * wide // BQ
+    pairs = parts * BQ * chunks * CH * 0.6
+    shape = jax.ShapeDtypeStruct((2, owners, HD, wide), bf16)
+    first = held is None
+    if first:
+        kernel = lambda info, q, k, v, size, *rest: fwd_kernel(shared, info, q, k, v, size, None, *rest)
+    else:
+        kernel = functools.partial(fwd_kernel, shared)
     return pl.pallas_call(
-        functools.partial(fwd_kernel, shared),
+        kernel,
         grid_spec=pltpu.PrefetchScalarGridSpec(
-            num_scalar_prefetch=2, grid=(seqs,),
+            num_scalar_prefetch=1, grid=(1,),
             in_specs=[
                 head_spec(shared, owners, HD, local), head_spec(shared, chunks, CH, 128), head_spec(shared, chunks, 128, CH),
-                seq_spec(*sizes.shape[1:]),
-            ],
-            out_specs=[seq_spec(owners, HD, held), seq_spec(parts, 1, BQ)],
+                whole_spec(*sizes.shape),
+            ] + ([] if first else [pl.BlockSpec(memory_space=pl.ANY)]),
+            out_specs=[pl.BlockSpec((1, owners, HD, wide), lambda i, n: (seq, 0, 0, 0)), whole_spec(parts, 1, BQ)],
             scratch_shapes=[
                 pltpu.VMEM((128, BQ), f32), pltpu.VMEM((2, CH, BQ), bf16), pltpu.VMEM((parts, 128, BQ), bf16),
                 pltpu.VMEM((parts, 1, BQ), f32),
             ]),
-        out_shape=[
-            jax.ShapeDtypeStruct((seqs, owners, HD, held), bf16),
-            jax.ShapeDtypeStruct((seqs, parts, 1, BQ), f32),
-        ],
+        out_shape=[shape, jax.ShapeDtypeStruct((parts, 1, BQ), f32)],
+        input_output_aliases={} if first else {5: 0},
         compiler_params=pltpu.CompilerParams(vmem_limit_bytes=48 << 20),
-        cost_estimate=cost(pairs * 1024, seqs * chunks * CH * 512, pairs),
+        cost_estimate=cost(pairs * 1024, chunks * CH * 512, pairs),
         name="attend_forward_shared" if shared else "attend_forward_own",
-    )(lens, core, q, k, v, sizes)
-
-
-def bwd_kernel(shared, len_ref, core_ref, q_ref, k_ref, v_ref, lse_ref, out_ref, gout_ref, *rest):
+    )(*((info, q, k, v, sizes) + (() if first else (held,))))
+
+
+def bwd_kernel(shared, first, info, q_ref, k_ref, v_ref, lse_ref, out_ref, gout_ref, *rest):
+    rest = rest if first else rest[2 if shared else 1:]
     if shared:
         dq_ref, dkv_ref, dk_acc, dv_acc, dq_acc, qa, qat, ga, gat, pb, db = rest
     else:
         dqkv_ref, dk_acc, dv_acc, dq_acc, qa, qat, ga, gat, pb, db = rest
-    seq = pl.program_id(0)
-    count = lax.div(len_ref[seq] + (CH - 1), CH)
-    chunks = k_ref.shape[2]
+    count = lax.div(info[0] + (CH - 1), CH)
+    chunks = k_ref.shape[1]
     parts = 2 if shared else 4
     dk_acc[...] = jnp.zeros_like(dk_acc)
     dv_acc[...] = jnp.zeros_like(dv_acc)
@@ -235,7 +260,7 @@
         return ref[0, part]
 
     for part in range(parts):
-        q_full = with_shift(assemble(q_ref, part, shared, core_ref[0]), lse_ref[0, part])
+        q_full = with_shift(assemble(q_ref, part, shared, info[3]), lse_ref[part])
         qat[part] = q_full.astype(bf16)
         qa[part] = q_full.T.astype(bf16)
         g_t = piece(gout_ref, part)
@@ -245,9 +270,9 @@
         ga[part] = g_full.T.astype(bf16)
 
     def ahead(part, j, slot):
-        raised = jnp.exp2(dg(qa[part], k_ref[0, 0, j], 1, 1))
+        raised = jnp.exp2(dg(qa[part], k_ref[0, j], 1, 1))
         pb[slot] = raised.astype(bf16)
-        db[slot] = (raised * dg(ga[part], v_ref[0, 0, j], 1, 0)).astype(bf16)
+        db[slot] = (raised * dg(ga[part], v_ref[0, j], 1, 0)).astype(bf16)
 
     ahead(0, 0, 0)
 
@@ -258,15 +283,16 @@
         dv_acc[j] += dg(gat[part], pb[now], 1, 0)[:HD]
         dk_acc[j] += dg(qat[part], db[now], 1, 0)[:HD]
         before = jnp.where(j == 0, 0.0, dq_acc[...])
-        dq_acc[...] = before + dg(db[now], k_ref[0, 0, j], 1, 0)
+        dq_acc[...] = before + dg(db[now], k_ref[0, j], 1, 0)
         ahead(jnp.minimum(part_next, parts - 1), j_next, 1 - now)
 
         @pl.when(j + 1 == count)
         def _():
             dq_t = (dq_acc[...] * 0.125).T[:HD].astype(bf16)
             if shared:
-                dq_ref[0, 2 * part] = dq_t[:, :512]
-                dq_ref[0, 2 * part + 1] = dq_t[:, 512:]
+                for a in range(2):
+                    dq_ref[0, 2 * part + a, :, :512] = dq_t[:32, a * 512:(a + 1) * 512]
+                    dq_ref[0, 2 * part + a, :, 512:] = dq_t[32:, a * 512:(a + 1) * 512]
             else:
                 dqkv_ref[0, part, 0] = dq_t
         return part_next, j_next
@@ -285,27 +311,31 @@
                 dqkv_ref[0, owner, 2, :, j * 128:(j + 1) * 128] = dv
 
 
-def attend_backward(shared, q, k, v, lse, out, g_out, lens, core):
-    seqs, _, owners, _, local = q.shape
-    chunks = k.shape[2]
-    held = out.shape[3]
-    parts = owners * held // BQ
-    pairs = seqs * parts * BQ * chunks * CH * 0.6
+def attend_backward(shared, seq, q, k, v, lse, out, g_out, info, held):
+    _, owners, _, local = q.shape
+    chunks = k.shape[1]
+    wide = out.shape[3]
+    parts = owners * wide // BQ
+    pairs = parts * BQ * chunks * CH * 0.6
     shape = jax.ShapeDtypeStruct
+    first = held is None
     if shared:
-        out_specs = [seq_spec(owners, HD, held), pl.BlockSpec((2, 1, owners, HD, local), lambda s, n, c: (0, s, 0, 0, 0))]
-        out_shape = [shape((seqs, owners, HD, held), bf16), shape((2, seqs, owners, HD, local), bf16)]
+        out_specs = [pl.BlockSpec((1, owners, 32, local), lambda i, n: (seq, 0, 0, 0)),
+                     pl.BlockSpec((2, 1, owners, HD, local), lambda i, n: (0, seq, 0, 0, 0))]
+        out_shape = [shape((2, owners, 32, local), bf16), shape((2, 2, owners, HD, local), bf16)]
     else:
-        out_specs = [seq_spec(owners, 3, HD, local)]
-        out_shape = [shape((seqs, owners, 3, HD, local), bf16)]
+        out_specs = [pl.BlockSpec((1, owners, 3, HD, local), lambda i, n: (seq, 0, 0, 0, 0))]
+        out_shape = [shape((2, owners, 3, HD, local), bf16)]
+    kept = () if first else tuple(held)
+    of_seq = pl.BlockSpec((1, owners, HD, wide), lambda i, n: (seq, 0, 0, 0))
     return pl.pallas_call(
-        functools.partial(bwd_kernel, shared),
+        functools.partial(bwd_kernel, shared, first),
         grid_spec=pltpu.PrefetchScalarGridSpec(
-            num_scalar_prefetch=2, grid=(seqs,),
+            num_scalar_prefetch=1, grid=(1,),
             in_specs=[
                 head_spec(shared, owners, HD, local), head_spec(shared, chunks, CH, 128), head_spec(shared, chunks, 128, CH),
-                seq_spec(parts, 1, BQ), seq_spec(owners, HD, held), seq_spec(owners, HD, held),
-            ],
+                whole_spec(parts, 1, BQ), of_seq, of_seq,
+            ] + [pl.BlockSpec(memory_space=pl.ANY)] * len(kept),
             out_specs=out_specs,
             scratch_shapes=[
                 pltpu.VMEM((chunks, HD, CH), f32), pltpu.VMEM((chunks, HD, CH), f32), pltpu.VMEM((BQ, 128), f32),
@@ -314,10 +344,11 @@
                 pltpu.VMEM((2, BQ, CH), bf16), pltpu.VMEM((2, BQ, CH), bf16),
             ]),
         out_shape=out_shape,
+        input_output_aliases={7 + n: n for n in range(len(kept))},
         compiler_params=pltpu.CompilerParams(vmem_limit_bytes=56 << 20),
-        cost_estimate=cost(pairs * 100, seqs * chunks * CH * 2048),
+        cost_estimate=cost(pairs * 100, chunks * CH * 2048),
         name="attend_backward_shared" if shared else "attend_backward_own",
-    )(lens, core, q, k, v, lse, out, g_out)
+    )(info, q, k, v, lse, out, g_out, *kept)
 
 
 def gelu_pair(u):
@@ -342,12 +373,13 @@
     return part.reshape(part.shape[0] * rows, part.shape[2])
 
 
-def ffn_kernel(spans, at_ref, x_ref, own_ref, sh_ref, cot_ref, w_ref, bin_ref, vec_ref,
+def ffn_kernel(spans, info, x_ref, own_ref, sh_ref, cot_ref, w_ref, bin_ref, vec_ref,
                act_out, resid_out, gown_out, gsh_out, active_out, dinner_out, normed_out, douter_out, dbranch_out,
-               vec_sum, bin_sum, slope):
+               vec_sum, bin_sum, slope, row_block):
     step = pl.program_id(0)
     width = x_ref.shape[-1]
-    rows = jnp.concatenate([x_ref[a, 0, z, 0] for z in range(spans) for a in range(2)], axis=0).astype(f32)
+    load_rows(row_block, x_ref, spans, info[1])
+    rows = row_block[...].astype(f32)
     mixed_t = jnp.concatenate(
         [part for p in range(4) for part in (own_ref[p, 0], sh_ref[p, 0], own_ref[p, 1])], axis=0)
     vec = vec_ref[...]
@@ -406,8 +438,8 @@
             bin_sum[:, n * 768:(n + 1) * 768] += sums_in[n]
 
 
-def feed_forward(gathered, own, sh, cotangent, weights, inner_bias, vectors, at):
-    _, _, _, _, stretch, width = gathered.shape
+def feed_forward(rows_in, own, sh, cotangent, weights, inner_bias, vectors, info):
+    _, _, _, stretch, width = rows_in.shape
     local = cotangent.shape[0]
     spans = RB // (2 * stretch)
     steps = local // RB
@@ -423,7 +455,7 @@
         grid_spec=pltpu.PrefetchScalarGridSpec(
             num_scalar_prefetch=1, grid=(steps,),
             in_specs=[
-                pl.BlockSpec((2, 1, spans, 1, stretch, width), lambda r, a: (0, a[1], r, a[0], 0, 0)),
+                pl.BlockSpec((1, 2, spans, stretch, width), lambda r, a: (0, 0, r, 0, 0)),
                 own_spec, sh_spec, rows(width),
                 pl.BlockSpec(weights.shape, lambda r, a: (0, 0, 0), pipeline_mode=pl.Buffered(1)),
                 fixed(1, wide), fixed(8, width),
@@ -432,7 +464,7 @@
                 rows(width), rows(width), own_spec, sh_spec, rows(wide), rows(wide), rows(width), rows(width), rows(width),
                 fixed(8, width), fixed(1, wide),
             ],
-            scratch_shapes=[pltpu.VMEM((RB, wide), bf16)]),
+            scratch_shapes=[pltpu.VMEM((RB, wide), bf16), pltpu.VMEM((RB, width), bf16)]),
         out_shape=[
             shape((local, width), bf16), shape((local, width), f32), shape(own.shape, bf16), shape(sh.shape, bf16),
             shape((local, wide), bf16), shape((local, wide), bf16), shape((local, width), bf16),
@@ -441,7 +473,7 @@
         compiler_params=pltpu.CompilerParams(vmem_limit_bytes=60 << 20),
         name="feed_forward",
         cost_estimate=cost(local * width * (width + 2 * wide) * 4, local * wide * 20),
-    )(at, gathered, own, sh, cotangent, weights, inner_bias, vectors)
+    )(info, rows_in, own, sh, cotangent, weights, inner_bias, vectors)
 
 
 def outer_grad_kernel(scale, active_ref, douter_ref, out_ref):
@@ -488,20 +520,23 @@
     )(packed, normed, d_inner, own, sh, d_branch)
 
 
-def head_grad_kernel(scale, spans, core_ref, x_ref, own_ref, dqs_ref, dks_ref, out_ref, bias_out, acc, bias_acc):
-    seq, owner, half = pl.program_id(0), pl.program_id(1), pl.program_id(2)
-    first = (seq == 0) & (owner == 0) & (half == 0)
-    last = (seq == pl.num_programs(0) - 1) & (owner == pl.num_programs(1) - 1) & (half == pl.num_programs(2) - 1)
-    rows = jnp.concatenate([x_ref[a, 0, z, 0] for z in range(spans) for a in range(2)], axis=0)
+def head_grad_kernel(scale, spans, info, *refs):
+    x_refs, (own_ref, dq_ref, dkv_ref, out_ref, bias_out, acc, bias_acc, rows) = refs[:4], refs[4:]
+    seq, away, half = pl.program_id(0), pl.program_id(1), pl.program_id(3)
+    last = (seq == 1) & (away == 1) & (pl.program_id(2) == 1) & (half == pl.num_programs(3) - 1)
+    for n in range(4):
+        @pl.when(seq * 2 + away == n)
+        def _(n=n):
+            load_rows(rows, x_refs[n], spans, info[1])
+    dq_t = jnp.where(half == info[3], jnp.concatenate([dq_ref[0, 0, :, :512], dq_ref[0, 0, :, 512:]], axis=0).astype(f32), 0.0)
     d_t = jnp.concatenate([
-        own_ref[0, 0, 0], jnp.where(half == core_ref[0], dqs_ref[0, 0].astype(f32), 0.0).astype(bf16),
-        own_ref[0, 0, 1], dks_ref[0, 0, 0], own_ref[0, 0, 2], dks_ref[1, 0, 0]], axis=0)
-
-    @pl.when(first)
+        own_ref[0, 0, 0], dq_t.astype(bf16), own_ref[0, 0, 1], dkv_ref[0, 0, 0], own_ref[0, 0, 2], dkv_ref[1, 0, 0]], axis=0)
+
+    @pl.when((seq == 0) & (away == 0) & (pl.program_id(2) == 0) & (half == 0))
     def _():
         acc[...] = jnp.zeros_like(acc)
         bias_acc[...] = jnp.zeros_like(bias_acc)
-    acc[...] += dg(d_t, rows, 1, 0)
+    acc[...] += dg(d_t, rows[...], 1, 0)
     bias_acc[...] += dg(jnp.ones((8, d_t.shape[1]), bf16), d_t, 1, 1)
 
     @pl.when(last)
@@ -510,37 +545,49 @@
         bias_out[...] = bias_acc[...] * scale
 
 
-def head_grads(scale, gathered, dqkv_own, dq_sh, dkv_sh, core):
-    _, owners, zs, seqs, stretch, width = gathered.shape
+def head_grads(scale, sources, dqkv_own, dq_sh, dkv_sh, info):
+    _, _, zs, stretch, width = sources[0].shape
     local = 2 * zs * stretch
     spans = 512 // (2 * stretch)
+    halves = local // 512
+
+    def source_spec(n):
+        def index(s, a, o, h, i):
+            now = 2 * s + a
+            across = jnp.where(now == n, o, jnp.where(now < n, 0, 1))
+            return (across, 0, jnp.where(now == n, h, jnp.where(now < n, 0, halves - 1)), 0, 0)
+        return pl.BlockSpec((1, 2, spans, stretch, width), index)
     return pl.pallas_call(
         functools.partial(head_grad_kernel, scale, spans),
         grid_spec=pltpu.PrefetchScalarGridSpec(
-            num_scalar_prefetch=1, grid=(seqs, owners, local // 512),
-            in_specs=[
-                pl.BlockSpec((2, 1, spans, 1, stretch, width), lambda s, o, h, c: (0, o, h, s, 0, 0)),
-                pl.BlockSpec((1, 1, 3, HD, 512), lambda s, o, h, c: (s, o, 0, 0, h)),
-                pl.BlockSpec((1, 1, HD, 512), lambda s, o, h, c: (s, o, 0, 0)),
-                pl.BlockSpec((2, 1, 1, HD, 512), lambda s, o, h, c: (0, s, o, 0, h))],
-            out_specs=[pl.BlockSpec((width, 384), lambda s, o, h, c: (0, 0)), pl.BlockSpec((8, 384), lambda s, o, h, c: (0, 0))],
-            scratch_shapes=[pltpu.VMEM((384, width), f32), pltpu.VMEM((8, 384), f32)]),
+            num_scalar_prefetch=1, grid=(2, 2, 2, halves),
+            in_specs=[source_spec(n) for n in range(4)] + [
+                pl.BlockSpec((1, 1, 3, HD, 512), lambda s, a, o, h, i: (s, owner_of(a, o, i), 0, 0, h)),
+                pl.BlockSpec((1, 1, 32, local), lambda s, a, o, h, i: (s, owner_of(a, o, i), 0, 0)),
+                pl.BlockSpec((2, 1, 1, HD, 512), lambda s, a, o, h, i: (0, s, owner_of(a, o, i), 0, h))],
+            out_specs=[pl.BlockSpec((width, 384), lambda s, a, o, h, i: (0, 0)), pl.BlockSpec((8, 384), lambda s, a, o, h, i: (0, 0))],
+            scratch_shapes=[pltpu.VMEM((384, width), f32), pltpu.VMEM((8, 384), f32), pltpu.VMEM((512, width), bf16)]),
         out_shape=[jax.ShapeDtypeStruct((width, 384), bf16), jax.ShapeDtypeStruct((8, 384), f32)],
         compiler_params=pltpu.CompilerParams(vmem_limit_bytes=40 << 20), name="head_grads",
-        cost_estimate=cost(seqs * owners * local * 768 * width, gathered.size * 2),
-    )(core, gathered, dqkv_own, dq_sh, dkv_sh)
-
-
-def token_grad_kernel(own_ref, dqs_ref, dks_ref, w_ref, resid_ref, out_ref):
+        cost_estimate=cost(8 * local * 768 * width, 8 * local * width * 2),
+    )(info, *sources, dqkv_own, dq_sh, dkv_sh)
+
+
+def token_grad_kernel(own_ref, low_ref, high_ref, dkv_ref, w_ref, resid_ref, out_ref):
     total = resid_ref[...]
     for kind in range(3):
-        made = jnp.concatenate([part for p in range(4) for part in (
-            own_ref[p, 0, kind], dqs_ref[p, 0] if kind == 0 else dks_ref[p, kind - 1], own_ref[p, 1, kind])], axis=0)
-        total = total + dg(made, weight_part(w_ref, 96 * kind, 96), 0, 1)
+        made = []
+        for p in range(4):
+            if kind == 0:
+                middle = jnp.concatenate([low_ref[p, 0], high_ref[p, 0]], axis=0)
+            else:
+                middle = jnp.concatenate([dkv_ref[p, kind - 1, n] for n in range(2)], axis=0)
+            made += [own_ref[p, 0, kind], middle, own_ref[p, 1, kind]]
+        total = total + dg(jnp.concatenate(made, axis=0), weight_part(w_ref, 96 * kind, 96), 0, 1)
     out_ref[...] = total.astype(bf16)
 
 
-def token_grad(own, dq_sh, dkv_sh, weights, resid):
+def token_grad(own, shared, weights, resid):
     local, width = resid.shape
     steps = local // RB
     half_steps = steps // 2
@@ -549,15 +596,17 @@
         token_grad_kernel, grid=(steps,),
         in_specs=[
             pl.BlockSpec((4, 2, 3, HD, RB), lambda r: (0, 0, 0, 0, r)),
-            pl.BlockSpec((4, 1, HD, RB), lambda r: (0, r // half_steps, 0, r % half_steps)),
-            pl.BlockSpec((4, 2, HD, RB), lambda r: (0, 0, 0, r)),
+            pl.BlockSpec((4, 1, None, 32, RB), lambda r: (0, r // half_steps, 0, 0, r % half_steps)),
+            pl.BlockSpec((4, 1, None, 32, RB), lambda r: (0, r // half_steps, 0, 0, half_steps + r % half_steps)),
+            pl.BlockSpec((4, 2, 2, 32, RB), lambda r: (0, 0, 0, 0, r)),
             pl.BlockSpec(weights.shape, lambda r: (0, 0, 0)), rows],
         out_specs=rows, out_shape=jax.ShapeDtypeStruct((local, width), bf16),
         compiler_params=pltpu.CompilerParams(vmem_limit_bytes=40 << 20), name="token_grad",
         cost_estimate=cost(local * width * width * 6, local * width * 12),
-    )(own, dq_sh, dkv_sh, weights, resid)
-
-
+    )(own, shared[:, :, :1], shared[:, :, :1], shared[:, :, 1:], weights, resid)
+
+
+SWAP = [(0, 1), (1, 0)]
 PAIR = ("x", "y", "c")
 ALL = ("z", "x", "y", "c")
 SHARD = ("z", "x")
@@ -609,10 +658,28 @@
     seq_count, _, stretch, width = tokens.shape
     per = w_query.shape[0]
     x, y, c = lax.axis_index("x"), lax.axis_index("y"), lax.axis_index("c")
-    core = c.astype(jnp.int32)[None]
-
-    ordered = jnp.take(tokens[:, 0], deal_order, axis=0).reshape(zs, 2, stretch, width)
-    spread = lax.all_to_all(ordered, "z", split_axis=0, concat_axis=0, tiled=True)
+    def deal(seq):
+        ordered = jnp.take(tokens[:, 0], deal_order[seq::2], axis=0)
+        return lax.all_to_all(ordered, "z", split_axis=0, concat_axis=0, tiled=True)
+
+    half = zs // 2
+
+    def corner(across, along):
+        return [lax.ppermute(across[:half], "y", SWAP), lax.ppermute(along[half:], "x", SWAP)]
+
+    def this_core(own, across, along, corner):
+        return jnp.concatenate([own, across, along] + corner, axis=0).reshape(2, 2, zs, stretch, width)
+
+    first_own = deal(0)
+    first_own, held_tokens = lax.optimization_barrier((first_own, tokens))
+    tokens = held_tokens
+    across_a, along_a = lax.ppermute(first_own, "x", SWAP), lax.ppermute(first_own, "y", SWAP)
+    second_own = deal(1)
+    across_a, along_a, second_own = lax.optimization_barrier((across_a, along_a, second_own))
+    near_a = this_core(first_own, across_a, along_a, corner(across_a, along_a))
+    far_a = lax.ppermute(near_a, "c", SWAP)
+    near_a, second_own = lax.optimization_barrier((near_a, second_own))
+    across_b, along_b = lax.ppermute(second_own, "x", SWAP), lax.ppermute(second_own, "y", SWAP)
 
     def head_columns(matrix):
         heads = matrix.reshape(per, 2, 2, 3, HD)
@@ -634,7 +701,7 @@
         return [lax.dynamic_index_in_dim(mine, 2 * c, axis=0, keepdims=False), mine[1]]
     bias_row = jnp.concatenate(head_bias(0) + [jnp.zeros((2 * HD,), bf16)] + head_bias(1)).astype(f32)[None]
 
-    gathered = lax.all_gather(spread, PAIR, axis=0, tiled=False).reshape(2, 4, zs, 2, stretch, width)
+    mine_rows = jnp.where(x == 0, jnp.stack([first_own, across_a]), jnp.stack([second_own, across_b]))[None]
 
     panels = w_inner.reshape(per, 4, 768)
     vectors = (b_output, ln1_gain, ln1_shift, b_outer, ln2_gain, ln2_shift)
@@ -655,7 +722,7 @@
     matches = slots[:, None] == jnp.arange(seq_count, dtype=jnp.int32)[None, :]
     lens = jnp.sum(jnp.where(matches, lengths[None, :], 0), axis=1).astype(jnp.int32)
 
-    q, k, v, sizes = project(gathered, head_weight, bias_row, lens)
+    infos = [jnp.stack([lens[n], x, y, c]).astype(jnp.int32) for n in range(2)]
 
     def swap(array):
         flat = array.reshape((8,) + array.shape[2:])
@@ -667,15 +734,23 @@
     def to_heads(array):
         return swap(array).reshape((2, 4) + array.shape[2:])
 
-    own, lse_own = attend_forward(False, q, k, v, sizes, lens, core)
+    heads_a = project(near_a, far_a, head_weight, bias_row, infos[0])
+    heads_a, across_b, along_b = lax.optimization_barrier((heads_a, across_b, along_b))
+    near_b = this_core(second_own, across_b, along_b, corner(across_b, along_b))
+    own_first, lse_own_a = attend_forward(False, 0, *heads_a, infos[0], None)
+    own_first, near_b = lax.optimization_barrier((own_first, near_b))
+    far_b = lax.ppermute(near_b, "c", SWAP)
+    sh_first, lse_sh_a = attend_forward(True, 0, *heads_a, infos[0], None)
+    sh_first, far_b = lax.optimization_barrier((sh_first, far_b))
+    heads_b = project(near_b, far_b, head_weight, bias_row, infos[1])
+    own, lse_own_b = attend_forward(False, 1, *heads_b, infos[1], own_first)
     own_t = to_tokens(own)
-    own, later_core = lax.optimization_barrier((own, core))
-    sh, lse_sh = attend_forward(True, q, k, v, sizes, lens, later_core)
+    own, info_later = lax.optimization_barrier((own, infos[1]))
+    sh, lse_sh_b = attend_forward(True, 1, *heads_b, info_later, sh_first)
     sh_sent, own_t = lax.optimization_barrier((sh, own_t))
     sh_t = to_tokens(sh_sent)
-    at = jnp.stack([x, y * 2 + c]).astype(jnp.int32)
     (act, resid, g_own, g_sh, active, d_inner, normed, d_outer, d_branch, vec_sums, bin_sums) = feed_forward(
-        gathered, own_t, sh_t, cotangent.reshape(-1, width), layer_weights, inner_bias, vector_rows, at)
+        mine_rows, own_t, sh_t, cotangent.reshape(-1, width), layer_weights, inner_bias, vector_rows, infos[0])
     g_own_h, g_sh_h = to_heads(g_own), to_heads(g_sh)
     active, back_all = lax.optimization_barrier((active, back_all))
     packed = weight_grads(scale, active, d_outer, normed, d_inner, own_t, sh_t, d_branch)
@@ -688,29 +763,41 @@
     back_weights = canonical_heads(back_all, shards)
     layer_part = lax.psum_scatter(ready.reshape(-1, width), ALL, scatter_dimension=0, tiled=True)
 
-    dqkv_own, = attend_backward(False, q, k, v, lse_own, own, g_own_h, lens, core)
+    qkv_a, qkv_b = heads_a[:3], heads_b[:3]
+    first = attend_backward(False, 0, *qkv_a, lse_own_a, own, g_own_h, infos[0], None)
+    dqkv_own, = attend_backward(False, 1, *qkv_b, lse_own_b, own, g_own_h, infos[1], first)
     back_own = to_tokens(dqkv_own)
-    dqkv_own, later_core = lax.optimization_barrier((dqkv_own, core))
-    dq_sh, dkv_sh = attend_backward(True, q, k, v, lse_sh, sh, g_sh_h, lens, later_core)
-    dq_sent, back_own = lax.optimization_barrier((dq_sh, back_own))
-    back_q = to_tokens(dq_sent)
+    dqkv_own, info_a, info_b = lax.optimization_barrier((dqkv_own, *infos))
+    first = attend_backward(True, 0, *qkv_a, lse_sh_a, sh, g_sh_h, info_a, None)
+    dq_sh, dkv_sh = attend_backward(True, 1, *qkv_b, lse_sh_b, sh, g_sh_h, info_b, first)
     kept = lax.dynamic_index_in_dim(dkv_sh, c, axis=0, keepdims=False)
     given = lax.dynamic_index_in_dim(dkv_sh, 1 - c, axis=0, keepdims=False)
-    taken = lax.ppermute(given, "c", [(0, 1), (1, 0)])
-    back_kv = to_tokens((kept.astype(f32) + taken.astype(f32)).astype(bf16))
-    d_heads, d_bias = head_grads(scale, gathered, dqkv_own, dq_sh, dkv_sh, core)
+    taken = lax.ppermute(given, "c", SWAP)
+    shared_out = jnp.concatenate([dq_sh, (kept.astype(f32) + taken.astype(f32)).astype(bf16)], axis=2)
+    shared_out, back_own, dqkv_own = lax.optimization_barrier((shared_out, back_own, dqkv_own))
+    back_shared = to_tokens(shared_out.reshape(2, 4, 3, 32, -1))
+    d_heads, d_bias = head_grads(scale, (near_a, far_a, near_b, far_b), dqkv_own, dq_sh, dkv_sh, infos[0])
     chunk = width // zs
     head_ready = jnp.concatenate([
         d_heads.reshape(zs, chunk, 384),
         jnp.broadcast_to(d_bias[:1].astype(bf16)[None], (zs, 16, 384))], axis=1)
-    head_ready, layer_part = lax.optimization_barrier((head_ready, layer_part))
+    head_ready, layer_part, back_shared = lax.optimization_barrier((head_ready, layer_part, back_shared))
     head_part = lax.psum_scatter(head_ready.reshape(-1, 384), "z", scatter_dimension=0, tiled=True)
     head_grads_all = lax.all_gather(head_part, PAIR, axis=0, tiled=False).reshape(4, 2, chunk + 16, 6, HD).astype(f32)
 
     layer_grads = lax.all_gather(layer_part, ("y", "c"), axis=0, tiled=True)
-    d_rows = token_grad(back_own, back_q, back_kv, back_weights, resid)
+    d_rows = token_grad(back_own, back_shared, back_weights, resid)
     returned = lax.all_to_all(
         d_rows.reshape(shards, stretch, width), SHARD, split_axis=0, concat_axis=0, tiled=True)
+    place = lax.axis_index("z") * 2 + x
+    own_slice = lambda row, n: lax.dynamic_slice_in_dim(row, place * n, n)
+    layer_grads = layer_grads.astype(f32)
+    d_wouter = layer_grads[:4 * per]
+    d_winner = layer_grads[4 * per:8 * per].reshape(4, per, width).transpose(1, 0, 2).reshape(per, 4 * width)
+    d_woutput = layer_grads[8 * per:9 * per]
+    d_binner = own_slice(layer_grads[9 * per:9 * per + 4].reshape(-1), 4 * per)
+    d_bo, d_g1, d_s1, d_bout, d_g2, d_s2 = (own_slice(layer_grads[9 * per + 4 + n], per) for n in range(6))
+    returned, d_wouter, d_winner, d_woutput = lax.optimization_barrier((returned, d_wouter, d_winner, d_woutput))
     d_tokens = jnp.zeros_like(returned).at[deal_order].set(returned)[:, None]
 
     mine = lax.dynamic_slice_in_dim(head_grads_all, x * per, per, axis=2)
@@ -722,17 +809,9 @@
         return joined.transpose(2, 0, 1, 3).reshape(part.shape[2], width)
     d_wq, d_wk, d_wv = (full(mine, kind) for kind in range(3))
     bias_part = head_grads_all[:, :, chunk:chunk + 1]
-    place = lax.axis_index("z") * 2 + x
-    own_slice = lambda row, n: lax.dynamic_slice_in_dim(row, place * n, n)
     d_bq = own_slice(full(bias_part, 0)[0], per)
     d_bv = own_slice(full(bias_part, 2)[0], per)
 
-    layer_grads = layer_grads.astype(f32)
-    d_wouter = layer_grads[:4 * per]
-    d_winner = layer_grads[4 * per:8 * per].reshape(4, per, width).transpose(1, 0, 2).reshape(per, 4 * width)
-    d_woutput = layer_grads[8 * per:9 * per]
-    d_binner = own_slice(layer_grads[9 * per:9 * per + 4].reshape(-1), 4 * per)
-    d_bo, d_g1, d_s1, d_bout, d_g2, d_s2 = (own_slice(layer_grads[9 * per + 4 + n], per) for n in range(6))
     return (act.reshape(1, shards, stretch, width), d_tokens, d_wq, d_wk, d_wv, d_woutput, d_bq, d_bv, d_bo,
             d_g1, d_s1, d_winner, d_binner, d_wouter, d_bout, d_g2, d_s2)
 

time: 680 us -> 691 us (1.016)
  blocking collectives: 59.8 us -> 0 us
  local copies, waits for them, and re-layouts: 75.1 us -> 102 us
  Pallas kernels: 295 us -> 321 us
  starting transfers between devices: 33.3 us -> 48.5 us
    all_to_all x1 -> x0, blocking collectives: 59.8 us -> none  [body(): lax.all_to_all(ordered, 'z', split_axis=0, concat_axis=0, tiled=True)]
    all_gather x1 -> x0, waiting for transfers between devices: 57.7 us -> none  [body(): lax.all_gather(spread, PAIR, axis=0, tiled=False)]
    ppermute x1 -> x11, waiting for transfers between devices: 0.01 us -> 44 us  [the longest x1 16.7 us: body(): lax.ppermute(first_own, 'x', SWAP)]
    all_to_all x1, waiting for transfers between devices: 35.7 us -> 0.01 us  [body(): lax.all_to_all(d_rows.reshape(shards, stretch, width), SHARD, split_axis=...]
    all_to_all x0 -> x2, waiting for transfers between devices: none -> 35.1 us  [deal(): return lax.all_to_all(ordered, 'z', split_axis=0, concat_axis=0, tiled=True)]
    all_gather x1, waiting for transfers between devices: 0.02 us -> 24.7 us  [body(): layer_grads = lax.all_gather(layer_part, ('y', 'c'), axis=0, tiled=True)]
    reduce_scatter x1, waiting for transfers between devices: 79.8 us -> 55.5 us  [body(): lax.psum_scatter(ready.reshape(-1, width), ALL, scatter_dimension=0, tile...]
    pallas_call x4 -> x8, Pallas kernels: 198 us -> 220 us  [the longest x4 122 us: attend_forward(): pl.pallas_call(kernel, grid_spec=pltpu.PrefetchScalarGridSpec(num_scalar_...]
  transfers between devices with their start and end apart: 17 -> 27, of which waited for: 5 -> 16; matrix products, arithmetic and copies ran while one was open for 6% -> 10% of each run, Pallas kernels for 43% -> 46%
where the time goes in v3:
time: 691 us; the launch traced here: 693 us
  Pallas kernels  321 us (46%)
  waiting for transfers between devices  188 us (27%)
  local copies, waits for them, and re-layouts  102 us (15%)
  starting transfers between devices  48.5 us (7%)
  other arithmetic  17.5 us (3%)
  between operations  15.6 us (2%)
    pallas_call x4, Pallas kernels, attend_forward(): pl.pallas_call(kernel, grid_spec=pltpu.PrefetchScalarGridSpec(num_scalar_...  122 us
    pallas_call x4, Pallas kernels, attend_backward(): pl.pallas_call(functools.partial(bwd_kernel, shared, first), grid_spec=pl...  98 us
    reduce_scatter x1, waiting for transfers between devices, body(): lax.psum_scatter(ready.reshape(-1, width), ALL, scatter_dimension=0, tile...  55.5 us
    pallas_call x1, Pallas kernels, feed_forward(): pl.pallas_call(functools.partial(ffn_kernel, spans), grid_spec=pltpu.Pref...  41 us
    all_to_all x2, waiting for transfers between devices, deal(): return lax.all_to_all(ordered, 'z', split_axis=0, concat_axis=0, tiled=True)  35.1 us
    unnamed x150, local copies, waits for them, and re-layouts  34.6 us
    all_gather x1, waiting for transfers between devices, body(): layer_grads = lax.all_gather(layer_part, ('y', 'c'), axis=0, tiled=True)  24.7 us
    all_to_all x6, starting transfers between devices, swap(): return lax.all_to_all(flat, PAIR, split_axis=0, concat_axis=0, tiled=True)  23.9 us
  transfers between devices with their start and end apart: 27, of which 16 were waited for; matrix products, arithmetic and copies ran while one was open for 10% of the time, Pallas kernels for 46%

profile of v3, /device:TPU:0, one launch (start us, length us, event | category | flops | bytes accessed | tf_op | source)
XLA Modules:
  0.0 693.4 jit_solution(1283075670375540827)
XLA Ops:
  16.0 5.6 concatenate.79
  27.8 6.3 all-to-all-start
  34.2 30.8 %all-to-all-done = bf16[4,128,768]{2,1,0:T(8,128)(2,1)S(1)} async-done(((bf16[4,128,768]{2,1,0:T(8,128)(2,1)}), bf16[4,128,768]{2,1,0:T(8,128)(2,1)S(1)}, u32[]{:S(2)}, u32[]{:S(2)}) %all-to-all-start) | async-done | bytes 786464 | tf_op jit(solution)/shard_map/all_to_all | solution.py:663
  66.7 3.5 all-to-all-start.1
  73.3 16.7 %collective-permute-done = bf16[4,128,768]{2,1,0:T(8,128)(2,1)S(1)} collective-permute-done((bf16[4,128,768]{2,1,0:T(8,128)(2,1)S(1)}, bf16[4,128,768]{2,1,0:T(8,128)(2,1)S(1)}, u32[]{:S(2)}, u32[]{:S(2)}) %collective-permute-start) | collective-permute-done | bytes 786464 | tf_op jit(solution)/shard_map/ppermute | solution.py:676
  91.4 4.3 all-to-all-done.1
  101.3 7.8 %collective-permute-done.2 = bf16[2,128,768]{2,1,0:T(8,128)(2,1)S(1)} collective-permute-done((bf16[2,128,768]{2,1,0:T(8,128)(2,1)S(1)}, bf16[2,128,768]{2,1,0:T(8,128)(2,1)S(1)}, u32[]{:S(2)}, u32[]{:S(2)}) %collective-permute-start.2) | collective-permute-done | bytes 393248 | tf_op jit(solution)/shard_map/ppermute | solution.py:668
  109.1 4.7 collective-permute-done.3
  114.8 2.5 slice.318
  118.4 2.5 collective-permute-start.4
  121.0 3.6 reshape.371
  124.6 2.6 constant_dynamic-slice_fusion.11
  130.2 9.5 %qkv.2 = (bf16[2,4,64,1024]{3,2,1,0:T(8,128)(2,1)S(1)}, bf16[2,8,512,128]{3,2,1,0:T(8,128)(2,1)S(1)}, bf16[2,8,128,512]{3,2,1,0:T(8,128)(2,1)S(1)}, f32[4,2,1,128]{3,2,1,0:T(1,128)S(1)}) custom-call(s32[4]{0:T(128)S(1)} %add_add_fusion.info, bf16[2,2,4,128,768]{4,3,2,1,0:T(8,128)(2,1)S(1)} %bitcast.142, ...), custom_call_target="tpu_custom_call" | custom-call | flops 2415919104 | bytes 12582912 | tf_op jit(solution)/shard_map/qkv/pallas_call | solution.py:95
  141.1 8.2 %collective-permute-done.4 = bf16[4,128,768]{2,1,0:T(8,128)(2,1)} collective-permute-done((bf16[4,128,768]{2,1,0:T(8,128)(2,1)}, bf16[4,128,768]{2,1,0:T(8,128)(2,1)}, u32[]{:S(2)}, u32[]{:S(2)}) %collective-permute-start.4) | collective-permute-done | bytes 786464 | tf_op jit(solution)/shard_map/ppermute | solution.py:682
  149.3 2.5 collective-permute-done.6
  154.0 55.6 %attend_forward_own.2 = (bf16[2,4,64,1024]{3,2,1,0:T(8,128)(2,1)}, f32[4,1,1024]{2,1,0:T(1,128)S(1)}) custom-call(s32[4]{0:T(128)S(1)} %add_add_fusion.info, bf16[2,4,64,1024]{3,2,1,0:T(8,128)(2,1)S(1)} %get-tuple-element.112.q.q_ref, bf16[2,8,512,128]{3,2,1,0:T(8,128)(2,1)S(1)} %get-tuple-element.113.k.k_ref, bf16[2,8,128,512]{3,2,1,0:T(8,128)(2,1)} %copy-done.4, ...), custom_call_target="tpu_custom_call" | custom-call | flops 10307921920 | bytes 2097152 | tf_op jit(solution)/shard_map/attend_forward_own/pallas_call | solution.py:224
  217.9 40.7 %attend_forward_shared.2 = (bf16[2,4,64,512]{3,2,1,0:T(8,128)(2,1)}, f32[2,1,1024]{2,1,0:T(1,128)S(1)}) custom-call(s32[4]{0:T(128)S(1)} %add_add_fusion.info, bf16[2,4,64,1024]{3,2,1,0:T(8,128)(2,1)S(1)} %get-tuple-element.112.q.q_ref, bf16[2,8,512,128]{3,2,1,0:T(8,128)(2,1)S(1)} %get-tuple-element.113.k.k_ref, bf16[2,8,128,512]{3,2,1,0:T(8,128)(2,1)S(1)} %copy-done.5, ...), custom_call_target="tpu_custom_call" | custom-call | flops 5153960960 | bytes 2097152 | tf_op jit(solution)/shard_map/attend_forward_shared/pallas_call | solution.py:224
  259.2 9.9 %qkv.3 = (bf16[2,4,64,1024]{3,2,1,0:T(8,128)(2,1)S(1)}, bf16[2,8,512,128]{3,2,1,0:T(8,128)(2,1)S(1)}, bf16[2,8,128,512]{3,2,1,0:T(8,128)(2,1)S(1)}, f32[4,2,1,128]{3,2,1,0:T(1,128)S(1)}) custom-call(s32[4]{0:T(128)S(1)} %get-tuple-element.147.info, bf16[2,2,4,128,768]{4,3,2,1,0:T(8,128)(2,1)} %bitcast.28.near_ref.refs_2_, ...), custom_call_target="tpu_custom_call" | custom-call | flops 2415919104 | bytes 12582912 | tf_op jit(solution)/shard_map/qkv/pallas_call | solution.py:95
  270.5 17.5 %attend_forward_own.3 = (bf16[2,4,64,1024]{3,2,1,0:T(8,128)(2,1)}, f32[4,1,1024]{2,1,0:T(1,128)S(1)}) custom-call(s32[4]{0:T(128)S(1)} %get-tuple-element.147.info, bf16[2,4,64,1024]{3,2,1,0:T(8,128)(2,1)S(1)} %get-tuple-element.122.q_ref, bf16[2,8,512,128]{3,2,1,0:T(8,128)(2,1)S(1)} %get-tuple-element.123.k_ref, ...), custom_call_target="tpu_custom_call", output_to_operand_aliasing={{0}: (5, {})} | custom-call | flops 10307921920 | bytes 2097152 | tf_op jit(solution)/shard_map/attend_forward_own/pallas_call | solution.py:224
  288.5 3.6 all-to-all-start.2
  294.9 8.7 %attend_forward_shared.3 = (bf16[2,4,64,512]{3,2,1,0:T(8,128)(2,1)}, f32[2,1,1024]{2,1,0:T(1,128)S(1)}) custom-call(s32[4]{0:T(128)S(1)} %get-tuple-element.147.info, bf16[2,4,64,1024]{3,2,1,0:T(8,128)(2,1)S(1)} %copy-done.19, bf16[2,8,512,128]{3,2,1,0:T(8,128)(2,1)S(1)} %get-tuple-element.123.k_ref, ...), custom_call_target="tpu_custom_call", output_to_operand_aliasing={{0}: (5, {})} | custom-call | flops 5153960960 | bytes 2097152 | tf_op jit(solution)/shard_map/attend_forward_shared/pallas_call | solution.py:224
  306.5 3.5 all-to-all-start.3
  310.1 3.3 maximum_select_fusion.x_ref
  319.5 41.0 %feed_forward.1 = (bf16[1024,768]{1,0:T(8,128)(2,1)}, f32[1024,768]{1,0:T(8,128)}, bf16[4,2,64,1024]{3,2,1,0:T(8,128)(2,1)}, bf16[4,2,64,512]{3,2,1,0:T(8,128)(2...) custom-call(s32[4]{0:T(128)} %copy-done.33, ...), custom_call_target="tpu_custom_call" | custom-call | flops 21743271936 | bytes 62914560 | tf_op jit(solution)/shard_map/feed_forward/pallas_call | solution.py:453
  362.6 3.6 all-to-all-start.4
  366.2 2.8 copy-done.9
  369.0 7.2 %outer_grad.1.packed_ref = bf16[8,896,768]{2,1,0:T(8,128)(2,1)} custom-call(bf16[1024,3072]{1,0:T(8,128)(2,1)S(1)} %copy-done.9, bf16[1024,768]{1,0:T(8,128)(2,1)S(1)} %copy-done.26), custom_call_target="tpu_custom_call" | custom-call | flops 4831838208 | bytes 11010048 | tf_op jit(solution)/shard_map/outer_grad/pallas_call | solution.py:502
  376.4 8.8 %inner_grad.1 = bf16[8,896,768]{2,1,0:T(8,128)(2,1)} custom-call(bf16[8,896,768]{2,1,0:T(8,128)(2,1)} %outer_grad.1.packed_ref, bf16[1024,768]{1,0:T(8,128)(2,1)S(1)} %copy-done.24, bf16[1024,3072]{1,0:T(8,128)(2,1)S(1)} %copy-done.10, bf16[4,2,64,1024]{3,2,1,0:T(8,128)(2,1)S(1)} %bitcast.145, ...), custom_call_target="tpu_custom_call", output_to_operand_aliasing={{}: (0, {})} | custom-call | flops 6039797760 | bytes 13762560 | tf_op jit(solution)/shard_map/inner_grad/pallas_call | solution.py:511
  387.0 4.5 all-to-all-start.5
  391.5 46.5 %attend_backward_own.2.rest_0_ = bf16[2,4,3,64,1024]{4,3,2,1,0:T(8,128)(2,1)} custom-call(s32[4]{0:T(128)} %copy-done.33, bf16[2,4,64,1024]{3,2,1,0:T(8,128)(2,1)} %copy-done.17, bf16[2,8,512,128]{3,2,1,0:T(8,128)(2,1)} %copy-done.3, bf16[2,8,128,512]{3,2,1,0:T(8,128)(2,1)} %copy-done.4, f32[4,1,1024]{2,1,0:T(1,128)} %copy-done.29, ...), custom_call_target="tpu_custom_call" | custom-call | flops 1006632960 | bytes 8388608 | tf_op jit(solution)/shard_map/attend_backward_own/pallas_call | solution.py:331
  438.0 16.0 %attend_backward_own.3.refs_4_ = bf16[2,4,3,64,1024]{4,3,2,1,0:T(8,128)(2,1)} custom-call(s32[4]{0:T(128)} %copy-done.35, bf16[2,4,64,1024]{3,2,1,0:T(8,128)(2,1)} %copy-done.18, bf16[2,8,512,128]{3,2,1,0:T(8,128)(2,1)} %copy-done.6, bf16[2,8,128,512]{3,2,1,0:T(8,128)(2,1)} %copy-done.7, f32[4,1,1024]{2,1,0:T(1,128)} %copy-done.30, ...), custom_call_target="tpu_custom_call", output_to_operand_aliasing={{}: (7, {})} | custom-call | flops 1006632960 | bytes 8388608 | tf_op jit(solution)/shard_map/attend_backward_own/pallas_call | solution.py:331
  454.9 4.5 all-to-all-start.6
  459.3 25.3 %attend_backward_shared.2 = (bf16[2,4,32,1024]{3,2,1,0:T(8,128)(2,1)}, bf16[2,2,4,64,1024]{4,3,2,1,0:T(8,128)(2,1)}) custom-call(s32[4]{0:T(128)} %copy-done.33, bf16[2,4,64,1024]{3,2,1,0:T(8,128)(2,1)} %copy-done.17, bf16[2,8,512,128]{3,2,1,0:T(8,128)(2,1)} %copy-done.3, bf16[2,8,128,512]{3,2,1,0:T(8,128)(2,1)} %copy-done.4, f32[2,1,1024]{2,1,0:T(1,128)} %copy-done.31, ...), custom_call_target="tpu_custom_call" | custom-call | flops 503316480 | bytes 8388608 | tf_op jit(solution)/shard_map/attend_backward_shared/pallas_call | solution.py:331
  484.6 10.1 %attend_backward_shared.3 = (bf16[2,4,32,1024]{3,2,1,0:T(8,128)(2,1)}, bf16[2,2,4,64,1024]{4,3,2,1,0:T(8,128)(2,1)}) custom-call(s32[4]{0:T(128)} %copy-done.35, bf16[2,4,64,1024]{3,2,1,0:T(8,128)(2,1)} %copy-done.18, bf16[2,8,512,128]{3,2,1,0:T(8,128)(2,1)} %copy-done.6, ...), custom_call_target="tpu_custom_call", output_to_operand_aliasing={{0}: (7, {}), {1}: (8, {})} | custom-call | flops 503316480 | bytes 8388608 | tf_op jit(solution)/shard_map/attend_backward_shared/pallas_call | solution.py:331
  494.8 2.4 dynamic-slice_bitcast_fusion
  497.7 2.6 collective-permute-done.10
  504.0 4.3 all-to-all-start.7
  510.5 17.6 %head_grads.1 = (bf16[768,384]{1,0:T(8,128)(2,1)S(1)}, f32[8,384]{1,0:T(8,128)S(1)}) custom-call(s32[4]{0:T(128)S(1)} %copy-done.34, bf16[2,2,4,128,768]{4,3,2,1,0:T(8,128)(2,1)S(1)} %bitcast.143, bf16[2,2,4,128,768]{4,3,2,1,0:T(8,128)(2,1)} %collective-permute-done.5.far_ref.refs_1_, bf16[2,2,4,128,768]{4,3,2,1,0:T(8,128)(2,1)} %bitcast.28.near_ref.refs_2_, ...), custom_call_target="tpu_custom_call" | custom-call | flops 4831838208 | bytes 12582912 | tf_op jit(solution)/shard_map/head_grads/pallas_call | solution.py:560
  529.1 55.5 %reduce-scatter.3.cloned.1.call-done = bf16[224,768]{1,0:T(8,128)(2,1)} async-done(((bf16[7168,768]{1,0:T(8,128)(2,1)}), bf16[224,768]{1,0:T(8,128)(2,1)}) %reduce-scatter.3.cloned.1.call-update) | async-done | bytes 344080 | tf_op jit(solution)/shard_map/reduce_scatter | solution.py:764
  589.7 6.7 token_grad.1
  596.4 4.5 all-to-all-start.8
  600.9 9.8 %reduce-scatter.5.cloned.1.call-done = bf16[208,384]{1,0:T(8,128)(2,1)} async-done(((bf16[832,384]{1,0:T(8,128)(2,1)}), bf16[208,384]{1,0:T(8,128)(2,1)}) %reduce-scatter.5.cloned.1.call-update) | async-done | bytes 159760 | tf_op jit(solution)/shard_map/reduce_scatter | solution.py:785
  610.7 24.7 %all-gather.12.cloned.1.call-done = bf16[896,768]{1,0:T(8,128)(2,1)} async-done(((bf16[224,768]{1,0:T(8,128)(2,1)}), bf16[896,768]{1,0:T(8,128)(2,1)}) %all-gather.12.cloned.1.call-update) | async-done | bytes 1376272 | tf_op jit(solution)/shard_map/all_gather | solution.py:788
  635.4 2.4 fusion.20
  647.6 14.2 %all-gather.16.cloned.1.call-done = bf16[1664,384]{1,0:T(8,128)(2,1)} async-done(((bf16[208,384]{1,0:T(8,128)(2,1)}), bf16[1664,384]{1,0:T(8,128)(2,1)}) %all-gather.16.cloned.1.call-update) | async-done | bytes 1277968 | tf_op jit(solution)/shard_map/all_gather | solution.py:786
  661.8 2.9 copy.110
  664.7 6.8 reshape.401
  678.3 2.5 dynamic-slice_bitcast_fusion.1
  (322 shorter events, 96.7 us)
Async XLA Ops:
  7.2 18.9 %copy-start = (bf16[8,1,128,768]{3,2,1,0:T(8,128)(2,1)S(1)}, bf16[8,1,128,768]{3,2,1,0:T(8,128)(2,1)}, u32[]{:S(2)}) copy-start(bf16[8,1,128,768]{3,2,1,0:T(8,128)(2,1)} %param.23) | copy-start | bytes 4718596
  7.3 107.5 %all-gather.14.cloned.1.call-start = ((), (), s32[]{:S(2)}) async-start(), calls=%async_computation.16 | async-start | bytes 1548288 | tf_op jit(solution)/shard_map/all_gather | solution.py:694
  12.0 301.3 %all-gather.8.cloned.1.call-start = ((), (), s32[]{:S(2)}) async-start(), calls=%async_computation.11 | async-start | bytes 11354112 | tf_op jit(solution)/shard_map/all_gather | solution.py:711
  26.1 266.0 %copy-start.35 = (s32[4]{0:T(128)}, s32[4]{0:T(128)S(1)}, u32[]{:S(2)}) copy-start(s32[4]{0:T(128)S(1)} %get-tuple-element.147.info) | copy-start | bytes 52
  26.1 8.0 %copy-start.63 = (s32[8]{0:T(128)S(1)}, s32[8]{0:T(128)}, u32[]{:S(2)}) copy-start(s32[8]{0:T(128)} %param.25) | copy-start | bytes 100
  27.8 37.3 %all-to-all-start = ((bf16[4,128,768]{2,1,0:T(8,128)(2,1)}), bf16[4,128,768]{2,1,0:T(8,128)(2,1)S(1)}, u32[]{:S(2)}, u32[]{:S(2)}) async-start(bf16[4,128,768]{2,1,0:T(8,128)(2,1)} %broadcast_select_fusion.1), calls=%async_computation | async-start | bytes 1572864 | tf_op jit(solution)/shard_map/all_to_all | solution.py:663
  65.0 32.7 %copy-start.37 = (bf16[4,128,768]{2,1,0:T(8,128)(2,1)}, bf16[4,128,768]{2,1,0:T(8,128)(2,1)S(1)}, u32[]{:S(2)}) copy-start(bf16[4,128,768]{2,1,0:T(8,128)(2,1)S(1)} %all-to-all-done) | copy-start | bytes 2359300
  66.7 29.1 %all-to-all-start.1 = ((bf16[4,128,768]{2,1,0:T(8,128)(2,1)}), bf16[4,128,768]{2,1,0:T(8,128)(2,1)S(1)}, u32[]{:S(2)}, u32[]{:S(2)}) async-start(bf16[4,128,768]{2,1,0:T(8,128)(2,1)} %broadcast_select_fusion), calls=%async_computation.1 | async-start | bytes 1572864 | tf_op jit(solution)/shard_map/all_to_all | solution.py:663
  70.2 292.4 %all-gather.10.cloned.1.call-start = ((), (), s32[]{:S(2)}) async-start(), calls=%async_computation.12 | async-start | bytes 4055040 | tf_op jit(solution)/shard_map/all_gather | solution.py:718
  70.2 19.8 %collective-permute-start = (bf16[4,128,768]{2,1,0:T(8,128)(2,1)S(1)}, bf16[4,128,768]{2,1,0:T(8,128)(2,1)S(1)}, u32[]{:S(2)}, u32[]{:S(2)}) collective-permute-start(bf16[4,128,768]{2,1,0:T(8,128)(2,1)S(1)} %all-to-all-done), channel_id=1, source_target_pairs={{0,4},{4,0},{1,5},{5,1},{2,6},{6,2},{3,7},{7,3},{8,12},{12,8},{9,1... | collective-permute-start | bytes 2359304 | tf_op jit(solution)/shard_map/ppermute | solution.py:676
  71.8 19.7 %collective-permute-start.1 = (bf16[4,128,768]{2,1,0:T(8,128)(2,1)S(1)}, bf16[4,128,768]{2,1,0:T(8,128)(2,1)S(1)}, u32[]{:S(2)}, u32[]{:S(2)}) collective-permute-start(bf16[4,128,768]{2,1,0:T(8,128)(2,1)S(1)} %all-to-all-done), channel_id=1, source_target_pairs={{0,2},{2,0},{1,3},{3,1},{4,6},{6,4},{5,7},{7,5},{8,10},{10,8},{9,1... | collective-permute-start | bytes 2359304 | tf_op jit(solution)/shard_map/ppermute | solution.py:676
  90.0 7.8 %copy-start.41 = (bf16[4,128,768]{2,1,0:T(8,128)(2,1)}, bf16[4,128,768]{2,1,0:T(8,128)(2,1)S(1)}, u32[]{:S(2)}) copy-start(bf16[4,128,768]{2,1,0:T(8,128)(2,1)S(1)} %collective-permute-done) | copy-start | bytes 2359300
  95.8 13.3 %collective-permute-start.2 = (bf16[2,128,768]{2,1,0:T(8,128)(2,1)S(1)}, bf16[2,128,768]{2,1,0:T(8,128)(2,1)S(1)}, u32[]{:S(2)}, u32[]{:S(2)}) collective-permute-start(bf16[2,128,768]{2,1,0:T(8,128)(2,1)S(1)} %slice.244), channel_id=1, source_target_pairs={{0,2},{2,0},{1,3},{3,1},{4,6},{6,4},{5,7},{7,5},{8,10},{10,8},{9,1... | collective-permute-start | bytes 1179656 | tf_op jit(solution)/shard_map/ppermute | solution.py:668
  97.8 16.0 %collective-permute-start.3 = (bf16[2,128,768]{2,1,0:T(8,128)(2,1)S(1)}, bf16[2,128,768]{2,1,0:T(8,128)(2,1)S(1)}, u32[]{:S(2)}, u32[]{:S(2)}) collective-permute-start(bf16[2,128,768]{2,1,0:T(8,128)(2,1)S(1)} %slice.245), channel_id=1, source_target_pairs={{0,4},{4,0},{1,5},{5,1},{2,6},{6,2},{3,7},{7,3},{8,12},{12,8},{9,1... | collective-permute-start | bytes 1179656 | tf_op jit(solution)/shard_map/ppermute | solution.py:668
  113.8 10.8 %copy-start.11 = (bf16[16,128,768]{2,1,0:T(8,128)(2,1)}, bf16[16,128,768]{2,1,0:T(8,128)(2,1)S(1)}, u32[]{:S(2)}) copy-start(bf16[16,128,768]{2,1,0:T(8,128)(2,1)S(1)} %constant_dynamic-update-slice_fusion) | copy-start | bytes 9437188
  113.9 14.4 %collective-permute-start.5 = (bf16[2,2,4,128,768]{4,3,2,1,0:T(8,128)(2,1)S(1)}, bf16[2,2,4,128,768]{4,3,2,1,0:T(8,128)(2,1)}, u32[]{:S(2)}, u32[]{:S(2)}) collective-permute-start(bf16[2,2,4,128,768]{4,3,2,1,0:T(8,128)(2,1)S(1)} %bitcast.141), channel_id=1, source_target_pairs={{0,1},{1,0},{2,3},{3,2},{4,5},{5,4},{6,7},{7,6},{8,9},{9,8},{10,11... | collective-permute-start | bytes 9437192 | tf_op jit(solution)/shard_map/ppermute | solution.py:680
  114.7 101.6 %copy-start.33 = (s32[4]{0:T(128)}, s32[4]{0:T(128)S(1)}, u32[]{:S(2)}) copy-start(s32[4]{0:T(128)S(1)} %add_add_fusion.info) | copy-start | bytes 52
  118.4 30.9 %collective-permute-start.4 = (bf16[4,128,768]{2,1,0:T(8,128)(2,1)}, bf16[4,128,768]{2,1,0:T(8,128)(2,1)}, u32[]{:S(2)}, u32[]{:S(2)}) collective-permute-start(bf16[4,128,768]{2,1,0:T(8,128)(2,1)} %copy-done.38), channel_id=1, source_target_pairs={{0,4},{4,0},{1,5},{5,1},{2,6},{6,2},{3,7},{7,3},{8,12},{12,8},{9,1... | collective-permute-start | bytes 2359304 | tf_op jit(solution)/shard_map/ppermute | solution.py:682
  120.9 30.9 %collective-permute-start.6 = (bf16[4,128,768]{2,1,0:T(8,128)(2,1)}, bf16[4,128,768]{2,1,0:T(8,128)(2,1)}, u32[]{:S(2)}, u32[]{:S(2)}) collective-permute-start(bf16[4,128,768]{2,1,0:T(8,128)(2,1)} %copy-done.38), channel_id=1, source_target_pairs={{0,2},{2,0},{1,3},{3,1},{4,6},{6,4},{5,7},{7,5},{8,10},{10,8},{9,1... | collective-permute-start | bytes 2359304 | tf_op jit(solution)/shard_map/ppermute | solution.py:682
  127.3 12.5 %copy-start.27 = (bf16[768,1,384]{2,0,1:T(8,128)(2,1)}, bf16[768,1,384]{2,0,1:T(8,128)(2,1)S(1)}, u32[]{:S(2)}) copy-start(bf16[768,1,384]{2,0,1:T(8,128)(2,1)S(1)} %copy.134) | copy-start | bytes 1769476
  141.1 75.2 %copy-start.3 = (bf16[2,8,512,128]{3,2,1,0:T(8,128)(2,1)}, bf16[2,8,512,128]{3,2,1,0:T(8,128)(2,1)S(1)}, u32[]{:S(2)}) copy-start(bf16[2,8,512,128]{3,2,1,0:T(8,128)(2,1)S(1)} %get-tuple-element.113.k.k_ref) | copy-start | bytes 6291460
  141.1 75.2 %copy-start.17 = (bf16[2,4,64,1024]{3,2,1,0:T(8,128)(2,1)}, bf16[2,4,64,1024]{3,2,1,0:T(8,128)(2,1)S(1)}, u32[]{:S(2)}) copy-start(bf16[2,4,64,1024]{3,2,1,0:T(8,128)(2,1)S(1)} %get-tuple-element.112.q.q_ref) | copy-start | bytes 3145732
  152.8 61.0 %collective-permute-start.7 = (bf16[2,128,768]{2,1,0:T(8,128)(2,1)S(1)}, bf16[2,128,768]{2,1,0:T(8,128)(2,1)S(1)}, u32[]{:S(2)}, u32[]{:S(2)}) collective-permute-start(bf16[2,128,768]{2,1,0:T(8,128)(2,1)S(1)} %slice.255), channel_id=1, source_target_pairs={{0,2},{2,0},{1,3},{3,1},{4,6},{6,4},{5,7},{7,5},{8,10},{10,8},{9,1... | collective-permute-start | bytes 1179656 | tf_op jit(solution)/shard_map/ppermute | solution.py:668
  153.9 60.7 %collective-permute-start.8 = (bf16[2,128,768]{2,1,0:T(8,128)(2,1)S(1)}, bf16[2,128,768]{2,1,0:T(8,128)(2,1)S(1)}, u32[]{:S(2)}, u32[]{:S(2)}) collective-permute-start(bf16[2,128,768]{2,1,0:T(8,128)(2,1)S(1)} %slice.256), channel_id=1, source_target_pairs={{0,4},{4,0},{1,5},{5,1},{2,6},{6,2},{3,7},{7,3},{8,12},{12,8},{9,1... | collective-permute-start | bytes 1179656 | tf_op jit(solution)/shard_map/ppermute | solution.py:668
  215.4 43.8 %collective-permute-start.9 = (bf16[2,2,4,128,768]{4,3,2,1,0:T(8,128)(2,1)}, bf16[2,2,4,128,768]{4,3,2,1,0:T(8,128)(2,1)}, u32[]{:S(2)}, u32[]{:S(2)}) collective-permute-start(bf16[2,2,4,128,768]{4,3,2,1,0:T(8,128)(2,1)} %bitcast.28.near_ref.refs_2_), channel_id=1, source_target_pairs={{0,1},{1,0},{2,3},{3,2},{4,5},{5,4},{6,7},{7,6},{8,9},{9,8},{10,11... | collective-permute-start | bytes 9437192 | tf_op jit(solution)/shard_map/ppermute | solution.py:742
  217.9 41.3 %copy-start.28 = (bf16[768,1,384]{2,0,1:T(8,128)(2,1)S(1)}, bf16[768,1,384]{2,0,1:T(8,128)(2,1)}, u32[]{:S(2)}) copy-start(bf16[768,1,384]{2,0,1:T(8,128)(2,1)} %copy-done.27) | copy-start | bytes 1769476
  270.5 17.5 %copy-start.18 = (bf16[2,4,64,1024]{3,2,1,0:T(8,128)(2,1)}, bf16[2,4,64,1024]{3,2,1,0:T(8,128)(2,1)S(1)}, u32[]{:S(2)}) copy-start(bf16[2,4,64,1024]{3,2,1,0:T(8,128)(2,1)S(1)} %get-tuple-element.122.q_ref) | copy-start | bytes 3145732
  270.5 21.7 %copy-start.6 = (bf16[2,8,512,128]{3,2,1,0:T(8,128)(2,1)}, bf16[2,8,512,128]{3,2,1,0:T(8,128)(2,1)S(1)}, u32[]{:S(2)}) copy-start(bf16[2,8,512,128]{3,2,1,0:T(8,128)(2,1)S(1)} %get-tuple-element.123.k_ref) | copy-start | bytes 6291460
  288.5 17.9 %all-to-all-start.2 = ((bf16[8,64,1024]{2,1,0:T(8,128)(2,1)}), bf16[8,64,1024]{2,1,0:T(8,128)(2,1)S(1)}, u32[]{:S(2)}, u32[]{:S(2)}) async-start(bf16[8,64,1024]{2,1,0:T(8,128)(2,1)} %bitcast.29), calls=%async_computation.2 | async-start | bytes 2097152 | tf_op jit(solution)/shard_map/all_to_all | solution.py:729
  306.5 12.3 %all-to-all-start.3 = ((bf16[8,64,512]{2,1,0:T(8,128)(2,1)}), bf16[8,64,512]{2,1,0:T(8,128)(2,1)S(1)}, u32[]{:S(2)}, u32[]{:S(2)}) async-start(bf16[8,64,512]{2,1,0:T(8,128)(2,1)} %bitcast.31), calls=%async_computation.3 | async-start | bytes 1048576 | tf_op jit(solution)/shard_map/all_to_all | solution.py:729
  362.6 23.4 %all-to-all-start.4 = ((bf16[8,64,1024]{2,1,0:T(8,128)(2,1)}), bf16[8,64,1024]{2,1,0:T(8,128)(2,1)S(1)}, u32[]{:S(2)}, u32[]{:S(2)}) async-start(bf16[8,64,1024]{2,1,0:T(8,128)(2,1)} %bitcast.169), calls=%async_computation.4 | async-start | bytes 2097152 | tf_op jit(solution)/shard_map/all_to_all | solution.py:729
  366.1 218.4 %reduce-scatter.3.cloned.1.call-start = ((), (), s32[]{:S(2)}) async-start(), calls=%async_computation.13 | async-start | bytes 11354112 | tf_op jit(solution)/shard_map/reduce_scatter | solution.py:764
  369.0 7.3 %copy-start.53 = (f32[8,768]{1,0:T(8,128)S(1)}, f32[8,768]{1,0:T(8,128)}, u32[]{:S(2)}) copy-start(f32[8,768]{1,0:T(8,128)} %get-tuple-element.143) | copy-start | bytes 73732
  369.0 7.4 %copy-start.10 = (bf16[1024,3072]{1,0:T(8,128)(2,1)S(1)}, bf16[1024,3072]{1,0:T(8,128)(2,1)}, u32[]{:S(2)}) copy-start(bf16[1024,3072]{1,0:T(8,128)(2,1)} %get-tuple-element.140.dinner_ref) | copy-start | bytes 18874372
  369.0 7.4 %copy-start.16 = (bf16[8,64,1024]{2,1,0:T(8,128)(2,1)S(1)}, bf16[8,64,1024]{2,1,0:T(8,128)(2,1)}, u32[]{:S(2)}) copy-start(bf16[8,64,1024]{2,1,0:T(8,128)(2,1)} %copy-done.15) | copy-start | bytes 3145732
  369.0 7.4 %copy-start.23 = (bf16[8,64,512]{2,1,0:T(8,128)(2,1)S(1)}, bf16[8,64,512]{2,1,0:T(8,128)(2,1)}, u32[]{:S(2)}) copy-start(bf16[8,64,512]{2,1,0:T(8,128)(2,1)} %copy-done.22) | copy-start | bytes 1572868
  369.0 7.4 %copy-start.24 = (bf16[1024,768]{1,0:T(8,128)(2,1)S(1)}, bf16[1024,768]{1,0:T(8,128)(2,1)}, u32[]{:S(2)}) copy-start(bf16[1024,768]{1,0:T(8,128)(2,1)} %get-tuple-element.139.normed_ref) | copy-start | bytes 4718596
  369.0 7.4 %copy-start.25 = (bf16[1024,768]{1,0:T(8,128)(2,1)S(1)}, bf16[1024,768]{1,0:T(8,128)(2,1)}, u32[]{:S(2)}) copy-start(bf16[1024,768]{1,0:T(8,128)(2,1)} %get-tuple-element.141.dbranch_ref) | copy-start | bytes 4718596
  387.0 67.1 %all-to-all-start.5 = ((bf16[8,64,512]{2,1,0:T(8,128)(2,1)}), bf16[8,64,512]{2,1,0:T(8,128)(2,1)S(1)}, u32[]{:S(2)}, u32[]{:S(2)}) async-start(bf16[8,64,512]{2,1,0:T(8,128)(2,1)} %bitcast.40), calls=%async_computation.5 | async-start | bytes 1048576 | tf_op jit(solution)/shard_map/all_to_all | solution.py:729
  454.9 49.1 %all-to-all-start.6 = ((bf16[8,3,64,1024]{3,2,1,0:T(8,128)(2,1)}), bf16[8,3,64,1024]{3,2,1,0:T(8,128)(2,1)}, u32[]{:S(2)}, u32[]{:S(2)}) async-start(bf16[8,3,64,1024]{3,2,1,0:T(8,128)(2,1)} %bitcast.153), calls=%async_computation.6 | async-start | bytes 6291456 | tf_op jit(solution)/shard_map/all_to_all | solution.py:729
  497.2 3.2 collective-permute-start.10
  504.0 25.1 %all-to-all-start.7 = ((bf16[8,3,32,1024]{3,2,1,0:T(8,128)(2,1)}), bf16[8,3,32,1024]{3,2,1,0:T(8,128)(2,1)}, u32[]{:S(2)}, u32[]{:S(2)}) async-start(bf16[8,3,32,1024]{3,2,1,0:T(8,128)(2,1)} %bitcast.158), calls=%async_computation.8 | async-start | bytes 3145728 | tf_op jit(solution)/shard_map/all_to_all | solution.py:729
  508.3 102.4 %reduce-scatter.5.cloned.1.call-start = ((), (), s32[]{:S(2)}) async-start(), calls=%async_computation.15 | async-start | bytes 798720 | tf_op jit(solution)/shard_map/reduce_scatter | solution.py:785
  529.0 58.5 %copy-start.21 = (f32[1024,768]{1,0:T(8,128)S(1)}, f32[1024,768]{1,0:T(8,128)}, u32[]{:S(2)}) copy-start(f32[1024,768]{1,0:T(8,128)} %get-tuple-element.165.resid_ref) | copy-start | bytes 9437188
  584.6 50.8 %all-gather.12.cloned.1.call-start = ((), (), s32[]{:S(2)}) async-start(), calls=%async_computation.14 | async-start | bytes 1720320 | tf_op jit(solution)/shard_map/all_gather | solution.py:788
  596.4 50.0 %all-to-all-start.8 = ((bf16[8,128,768]{2,1,0:T(8,128)(2,1)}), bf16[8,128,768]{2,1,0:T(8,128)(2,1)S(1)}, u32[]{:S(2)}, u32[]{:S(2)}) async-start(bf16[8,128,768]{2,1,0:T(8,128)(2,1)} %bitcast.50), calls=%async_computation.9 | async-start | bytes 3145728 | tf_op jit(solution)/shard_map/all_to_all | solution.py:790
  600.9 60.9 %all-gather.16.cloned.1.call-start = ((), (), s32[]{:S(2)}) async-start(), calls=%async_computation.17 | async-start | bytes 1437696 | tf_op jit(solution)/shard_map/all_gather | solution.py:786
  647.6 14.2 %copy-start.40 = (bf16[8,128,768]{2,1,0:T(8,128)(2,1)}, bf16[8,128,768]{2,1,0:T(8,128)(2,1)S(1)}, u32[]{:S(2)}) copy-start(bf16[8,128,768]{2,1,0:T(8,128)(2,1)S(1)} %scatter_fusion) | copy-start | bytes 4718596
  (43 other events, 148.1 us)
Sparse Core Ops, SparseCore 0:
  12.1 52.7 all-gather.13
  67.8 109.5 all-gather.7
  216.4 57.4 all-gather.9
  386.1 198.3 reduce-scatter.2
  587.3 23.3 reduce-scatter.4
  612.1 23.2 all-gather.11
  637.3 24.4 all-gather.15
